TPU v7x, 32 devices: a whole 2x2x4 slice. The times are simulated.
32 devices in a mesh: expert: 16 (over z, y, core), tensor: 2 (over x).
Axes of the slice: x: 2, y: 2, z: 4, core: 2. Of those that a mesh axis runs over, the one named last changes fastest.
Arguments:
- tokens: bfloat16 [512, 7168], P('expert'), may hold values from -6 to 6
- cotangent: bfloat16 [512, 7168], P('expert'), may hold values from -1.5 to 1.5
- gate_weights: bfloat16 [512, 8], P('expert'), may hold values from 0.019897461 to 0.5
- route_slots: int32 [512, 8], P('expert'), may hold values from 0 to 15, all different within a row; in each aligned block of 32 rows (0 to 31, 32 to 63, ...) at most 24 rows name the same one
- replica_owner: int32 [2], replicated, may hold values from 0 to 13, as said below
- w_gate: bfloat16 [16, 7168, 1024], P('expert', None, 'tensor'), as said below
- w_up: bfloat16 [16, 7168, 1024], P('expert', None, 'tensor'), as said below
- w_down: bfloat16 [16, 7168, 1024], P('expert', None, 'tensor'), as said below
Outputs:
- input_grads: bfloat16 [512, 7168], P('expert', 'tensor')
- gate_grads: bfloat16 [512, 8], P('expert')
- expert_grads: bfloat16 [14, 7168, 3, 1024], P(None, 'expert', None, 'tensor')
Inputs may be any that keep to these rules, and one draw needn't show every extreme that they name: `route_slots`: in each block of 32 tokens no slot is named by more than 24 entries, a bound that some block reaches; a token names 8 different slots. `replica_owner`: numbers of experts; one expert may own several replicas, and a replica slot's weights equal its expert's. `w_gate`: slot 14 + r holds the same matrix as slot replica_owner[r]. `w_up`: slot 14 + r holds the same matrix as slot replica_owner[r]. `w_down`: slot 14 + r holds the same matrix as slot replica_owner[r].
All inputs are finite; a program needn't handle non-finite values.
Results may differ from a plain program's by a relative error of at most 0.012.
Values may be sent and summed in bfloat16 or wider, within the bound.
No kernel may reach another device: no remote copies, remote signals or barrier semaphores. Data moves between devices by JAX's collectives and lax.ppermute only.
A program may use at most 128 MiB of HBM per device.

v0:
```python
import jax
import jax.numpy as jnp
from jax import lax
from jax.sharding import PartitionSpec as P


def dispatch_targets(route_block, slot_total, capacity):
    flat_ids = route_block.reshape(-1)
    one_hot = (flat_ids[:, None] == jnp.arange(slot_total, dtype=jnp.int32)[None, :]).astype(
        jnp.int32
    )
    earlier = jnp.cumsum(one_hot, axis=0) - 1
    position = jnp.sum(one_hot * earlier, axis=1)
    return (flat_ids * capacity + position).reshape(route_block.shape)


def per_device(tokens, cotangent, gate_weights, route_slots, replica_owner, w_gate, w_up, w_down):
    slot_total = lax.axis_size("expert")
    tensor_total = lax.axis_size("tensor")
    tok_count, width = tokens.shape
    top_count = route_slots.shape[1]
    row_total = tok_count * top_count * 3 // 2
    capacity = row_total // slot_total
    width_part = width // tensor_total
    targets = dispatch_targets(route_slots, slot_total, capacity)
    matches = targets[None, :, :] == lax.iota(jnp.int32, row_total)[:, None, None]
    select = jnp.any(matches, axis=2).astype(jnp.bfloat16)
    gate_send = jnp.sum(
        jnp.where(matches, gate_weights.astype(jnp.float32)[None, :, :], 0.0), axis=(1, 2)
    )
    gate_send = gate_send.astype(jnp.bfloat16).reshape(slot_total, capacity)
    offset = lax.axis_index("tensor") * width_part
    x_part = lax.dynamic_slice_in_dim(tokens, offset, width_part, 1)
    dy_part = lax.dynamic_slice_in_dim(cotangent, offset, width_part, 1)
    x_send = jnp.dot(select, x_part, preferred_element_type=jnp.float32).astype(jnp.bfloat16)
    dy_send = jnp.dot(select, dy_part, preferred_element_type=jnp.float32).astype(jnp.bfloat16)
    x_recv, dy_recv, gate_rows = (
        lax.all_to_all(
            x_send.reshape(slot_total, capacity, width_part),
            "expert",
            split_axis=0,
            concat_axis=0,
            tiled=True,
        ),
        lax.all_to_all(
            dy_send.reshape(slot_total, capacity, width_part),
            "expert",
            split_axis=0,
            concat_axis=0,
            tiled=True,
        ),
        lax.all_to_all(gate_send, "expert", split_axis=0, concat_axis=0, tiled=True),
    )
    x_rows, dy_rows = (
        lax.all_gather(x_recv.reshape(row_total, width_part), "tensor", axis=1, tiled=True),
        lax.all_gather(dy_recv.reshape(row_total, width_part), "tensor", axis=1, tiled=True),
    )
    gate_rows = gate_rows.reshape(row_total)
    gate_mat = w_gate[0]
    up_mat = w_up[0]
    down_mat = w_down[0]
    gate_proj = jnp.dot(x_rows, gate_mat, preferred_element_type=jnp.float32)
    up_proj = jnp.dot(x_rows, up_mat, preferred_element_type=jnp.float32)
    sigmoid_gate = jax.nn.sigmoid(gate_proj)
    activated = gate_proj * sigmoid_gate
    hidden = (activated * up_proj).astype(jnp.bfloat16)
    out_part = lax.dot_general(
        hidden, down_mat, (((1,), (1,)), ((), ())), preferred_element_type=jnp.float32
    )
    row_score = lax.psum(jnp.sum(dy_rows.astype(jnp.float32) * out_part, axis=1), "tensor")
    row_score = row_score.astype(jnp.bfloat16)
    scaled = (gate_rows.astype(jnp.float32)[:, None] * dy_rows.astype(jnp.float32)).astype(
        jnp.bfloat16
    )
    hidden_grad = jnp.dot(scaled, down_mat, preferred_element_type=jnp.float32)
    up_grad = (hidden_grad * activated).astype(jnp.bfloat16)
    pre_grad = (
        hidden_grad * up_proj * sigmoid_gate * (1.0 + gate_proj * (1.0 - sigmoid_gate))
    ).astype(jnp.bfloat16)
    contract_rows = (((0,), (0,)), ((), ()))
    grad_gate = lax.dot_general(x_rows, pre_grad, contract_rows, preferred_element_type=jnp.float32)
    grad_up = lax.dot_general(x_rows, up_grad, contract_rows, preferred_element_type=jnp.float32)
    grad_down = lax.dot_general(scaled, hidden, contract_rows, preferred_element_type=jnp.float32)
    contract_hidden = (((1,), (1,)), ((), ()))
    input_part = lax.dot_general(
        pre_grad, gate_mat, contract_hidden, preferred_element_type=jnp.float32
    )
    input_part = input_part + lax.dot_general(
        up_grad, up_mat, contract_hidden, preferred_element_type=jnp.float32
    )
    row_input = lax.psum_scatter(
        input_part.astype(jnp.bfloat16), "tensor", scatter_dimension=1, tiled=True
    )
    back_rows, back_score = (
        lax.all_to_all(
            row_input.reshape(slot_total, capacity, width_part),
            "expert",
            split_axis=0,
            concat_axis=0,
            tiled=True,
        ),
        lax.all_to_all(
            row_score.reshape(slot_total, capacity),
            "expert",
            split_axis=0,
            concat_axis=0,
            tiled=True,
        ),
    )
    input_grads = lax.dot_general(
        select,
        back_rows.reshape(row_total, width_part),
        contract_rows,
        preferred_element_type=jnp.float32,
    ).astype(jnp.bfloat16)
    gate_grads = jnp.sum(
        jnp.where(matches, back_score.reshape(row_total).astype(jnp.float32)[:, None, None], 0.0),
        axis=0,
    ).astype(jnp.bfloat16)
    slot_grads = jnp.stack([grad_gate, grad_up, grad_down], axis=1).astype(jnp.bfloat16)
    hidden_part = slot_grads.shape[2]
    slot_grads = slot_grads.reshape(slot_total, width // slot_total, 3, hidden_part)
    expert_count = slot_total - replica_owner.shape[0]
    slot_table = jnp.concatenate([jnp.arange(expert_count, dtype=jnp.int32), replica_owner])
    combine_map = (
        slot_table[None, :] == jnp.arange(expert_count, dtype=jnp.int32)[:, None]
    ).astype(jnp.bfloat16)
    expert_grads = jnp.einsum(
        "es,skaf->ekaf",
        combine_map,
        lax.all_to_all(slot_grads, "expert", split_axis=0, concat_axis=0, tiled=True),
        preferred_element_type=jnp.float32,
    ).astype(jnp.bfloat16)
    return (input_grads, gate_grads, expert_grads)


def solution(mesh):
    in_specs = (
        P("expert", None),
        P("expert", None),
        P("expert", None),
        P("expert", None),
        P(),
        P("expert", None, "tensor"),
        P("expert", None, "tensor"),
        P("expert", None, "tensor"),
    )
    out_specs = (P("expert", "tensor"), P("expert", None), P(None, "expert", None, "tensor"))
    return jax.shard_map(
        per_device, mesh=mesh, in_specs=in_specs, out_specs=out_specs, check_vma=False
    )
```

profile of v0, /device:TPU:16, one launch (start us, length us, event | category | flops | bytes accessed | tf_op | source)
XLA Modules:
  0.0 952.2 jit_solution(17396092247295939263)
XLA Ops:
  10.4 67.7 %all_to_all.36 = bf16[16,24,3584]{2,1,0:T(8,128)(2,1)} all-to-all(bf16[16,24,3584]{2,1,0:T(8,128)(2,1)S(1)} %bitcast.72), channel_id=1, replica_groups=mesh['expert'=16,'tensor'=2] {'expert'}, dimensions={0} | all-to-all | bytes 5505024 | tf_op jit(solution)/shard_map/all_to_all | solution.py:38
  79.1 66.5 %all_to_all.37 = bf16[16,24,3584]{2,1,0:T(8,128)(2,1)} all-to-all(bf16[16,24,3584]{2,1,0:T(8,128)(2,1)S(1)} %bitcast.71), channel_id=1, replica_groups=mesh['expert'=16,'tensor'=2] {'expert'}, dimensions={0} | all-to-all | bytes 5505024 | tf_op jit(solution)/shard_map/all_to_all | solution.py:45
  145.7 4.0 all-gather.5.cloned.1.call-done
  149.7 7.8 fusion.9
  157.5 6.4 multiply_convert_fusion
  163.9 58.8 %all-gather.3.cloned.1.call-done = bf16[384,7168]{1,0:T(8,128)(2,1)} async-done(((bf16[384,3584]{1,0:T(8,128)(2,1)}), bf16[384,7168]{1,0:T(8,128)(2,1)}) %all-gather.3.cloned.1.call-update) | async-done | bytes 5505040 | tf_op jit(solution)/shard_map/all_gather | solution.py:56
  222.7 7.9 fusion.6
  230.6 4.9 psum.7
  236.3 6.0 all-to-all-start.4
  246.8 9.0 all_to_all.38
  255.9 8.0 multiply_convert_fusion.1
  263.9 10.8 %fusion.7 = f32[384,7168]{1,0:T(8,128)} fusion(bf16[384,512]{1,0:T(8,128)(2,1)S(1)} %get-tuple-element.21, bf16[1,7168,512]{2,1,0:T(8,128)(2,1)} %param.13), kind=kOutput, calls=%fused_computation.12 | convolution fusion | flops 2818572288 | bytes 18743296 | tf_op jit(solution)/shard_map/dot_general | solution.py:85
  274.7 11.3 %add_convert_fusion = bf16[384,7168]{1,0:T(8,128)(2,1)} fusion(f32[384,7168]{1,0:T(8,128)} %fusion.7, bf16[384,512]{1,0:T(8,128)(2,1)S(1)} %get-tuple-element.20, bf16[1,7168,512]{2,1,0:T(8,128)(2,1)} %param.14), kind=kOutput, calls=%fused_computation.8 | convolution fusion | flops 2824077312 | bytes 24248320 | tf_op jit(solution)/shard_map/dot_general | solution.py:88
  286.1 67.0 %reduce-scatter.2.cloned.1.call-done = bf16[384,3584]{1,0:T(8,128)(2,1)} async-done(((bf16[384,7168]{1,0:T(8,128)(2,1)}), bf16[384,3584]{1,0:T(8,128)(2,1)}) %reduce-scatter.2.cloned.1.call-update) | async-done | bytes 2752528 | tf_op jit(solution)/shard_map/reduce_scatter | solution.py:91
  353.1 6.0 all-to-all-start.3
  359.1 6.9 convolution_convert_fusion.1
  366.0 6.9 convolution_convert_fusion.2
  372.9 8.9 convolution_convert_fusion
  381.8 10.1 %pad_maximum_fusion = bf16[16,448,3,512]{3,1,2,0:T(8,128)(2,1)} fusion(bf16[16,448,1,512]{3,1,2,0:T(8,128)(2,1)} %bitcast.75, bf16[16,448,1,512]{3,1,2,0:T(8,128)(2,1)S(1)} %bitcast.73, bf16[16,448,1,512]{3,1,2,0:T(8,128)(2,1)S(1)} %bitcast.74), kind=kLoop, calls=%fused_computation | loop fusion | flops 22020096 | bytes 44040192 | tf_op jit(solution)/shard_map/stack | solution.py:120
  392.0 28.8 %all-to-all-done.3 = bf16[16,24,3584]{2,1,0:T(8,128)(2,1)S(1)} async-done(((bf16[16,24,3584]{2,1,0:T(8,128)(2,1)}), bf16[16,24,3584]{2,1,0:T(8,128)(2,1)S(1)}, u32[]{:S(2)}, u32[]{:S(2)}) %all-to-all-start.3) | async-done | bytes 2752544 | tf_op jit(solution)/shard_map/all_to_all | solution.py:95
  420.7 5.5 all-to-all-start.5
  428.3 472.3 %all-to-all-done.5 = bf16[16,448,3,512]{3,1,2,0:T(8,128)(2,1)} async-done(((bf16[16,448,3,512]{3,1,2,0:T(8,128)(2,1)}), bf16[16,448,3,512]{3,1,2,0:T(8,128)(2,1)}, u32[]{:S(2)}, u32[]{:S(2)}) %all-to-all-start.5) | async-done | bytes 22020128 | tf_op jit(solution)/shard_map/all_to_all | solution.py:131
  900.6 23.5 %fusion.2 = bf16[14,448,3,512]{3,0,2,1:T(8,128)(2,1)} fusion(bf16[16,448,3,512]{3,1,2,0:T(8,128)(2,1)} %all-to-all-done.5, s32[16]{0:T(128)S(1)} %pad_add_fusion), kind=kOutput, calls=%fused_computation.3 | convolution fusion | flops 317915360 | bytes 41287744 | tf_op jit(solution)/shard_map/es,skaf->ekaf/dot_general | solution.py:128
  924.1 21.6 %copy.62 = bf16[14,448,3,512]{3,1,2,0:T(8,128)(2,1)} copy(bf16[14,448,3,512]{3,0,2,1:T(8,128)(2,1)} %fusion.2) | data formatting | bytes 38535168
  (53 shorter events, 11.5 us)
Async XLA Ops:
  7.2 2.3 copy-start
  7.2 71.0 %copy-start.4 = (bf16[32,7168]{1,0:T(8,128)(2,1)S(1)}, bf16[32,7168]{1,0:T(8,128)(2,1)}, u32[]{:S(2)}) copy-start(bf16[32,7168]{1,0:T(8,128)(2,1)} %param.9) | copy-start | bytes 1376260
  7.2 142.5 %all-gather.5.cloned.1.call-start = ((), (), s32[]{:S(2)}) async-start(), calls=%async_computation.8 | async-start | bytes 8257536 | tf_op jit(solution)/shard_map/all_gather | solution.py:55
  78.1 144.6 %all-gather.3.cloned.1.call-start = ((), (), s32[]{:S(2)}) async-start(), calls=%async_computation.7 | async-start | bytes 8257536 | tf_op jit(solution)/shard_map/all_gather | solution.py:56
  149.7 7.8 copy-start.6
  163.9 66.7 %copy-start.8 = (bf16[384,512]{1,0:T(8,128)(2,1)}, bf16[384,512]{1,0:T(8,128)(2,1)S(1)}, u32[]{:S(2)}) copy-start(bf16[384,512]{1,0:T(8,128)(2,1)S(1)} %get-tuple-element.22) | copy-start | bytes 1179652
  222.7 19.6 %copy-start.5 = (bf16[32,8]{0,1:T(8,128)(2,1)S(1)}, bf16[32,8]{0,1:T(8,128)(2,1)}, u32[]{:S(2)}) copy-start(bf16[32,8]{0,1:T(8,128)(2,1)} %param.10) | copy-start | bytes 1540
  236.3 10.1 %all-to-all-start.4 = ((bf16[16,1,24]{2,1,0:T(2,128)(2,1)}), bf16[16,1,24]{2,1,0:T(2,128)(2,1)S(1)}, u32[]{:S(2)}, u32[]{:S(2)}) async-start(bf16[16,1,24]{2,1,0:T(2,128)(2,1)} %all_to_all.29), calls=%async_computation.5 | async-start | bytes 16384 | tf_op jit(solution)/shard_map/all_to_all | solution.py:102
  242.3 110.7 %reduce-scatter.2.cloned.1.call-start = ((), (), s32[]{:S(2)}) async-start(), calls=%async_computation.9 | async-start | bytes 8257536 | tf_op jit(solution)/shard_map/reduce_scatter | solution.py:91
  263.9 10.9 %copy-start.2 = (bf16[384,512]{1,0:T(8,128)(2,1)}, bf16[384,512]{1,0:T(8,128)(2,1)S(1)}, u32[]{:S(2)}) copy-start(bf16[384,512]{1,0:T(8,128)(2,1)S(1)} %get-tuple-element.21) | copy-start | bytes 1179652
  353.1 67.7 %all-to-all-start.3 = ((bf16[16,24,3584]{2,1,0:T(8,128)(2,1)}), bf16[16,24,3584]{2,1,0:T(8,128)(2,1)S(1)}, u32[]{:S(2)}, u32[]{:S(2)}) async-start(bf16[16,24,3584]{2,1,0:T(8,128)(2,1)} %bitcast.76), calls=%async_computation.4 | async-start | bytes 5505024 | tf_op jit(solution)/shard_map/all_to_all | solution.py:95
  359.1 6.9 copy-start.3
  366.0 6.9 copy-start.9
  392.0 34.3 %copy-start.7 = (s32[2]{0:T(128)S(1)}, s32[2]{0:T(128)}, u32[]{:S(2)}) copy-start(s32[2]{0:T(128)} %param.12) | copy-start | bytes 28
  420.7 479.8 %all-to-all-start.5 = ((bf16[16,448,3,512]{3,1,2,0:T(8,128)(2,1)}), bf16[16,448,3,512]{3,1,2,0:T(8,128)(2,1)}, u32[]{:S(2)}, u32[]{:S(2)}) async-start(bf16[16,448,3,512]{3,1,2,0:T(8,128)(2,1)} %pad_maximum_fusion), calls=%async_computation.6 | async-start | bytes 44040192 | tf_op jit(solution)/shard_map/all_to_all | solution.py:131
  924.1 21.6 %copy-start.1 = (bf16[32,7168]{1,0:T(8,128)(2,1)S(1)}, bf16[32,7168]{1,0:T(8,128)(2,1)}, u32[]{:S(2)}) copy-start(bf16[32,7168]{1,0:T(8,128)(2,1)} %param.8) | copy-start | bytes 1376260
Sparse Core Ops, SparseCore 0:
  78.3 71.3 all-gather.4
  151.2 71.4 all-gather.2
  286.2 66.8 reduce-scatter.1
where the time goes:
time: 953 us; the launch traced here: 952 us
  waiting for transfers between devices  635 us (67%)
  blocking collectives  148 us (16%)
  matrix products  102 us (11%)
  local copies, waits for them, and re-layouts  24.6 us (3%)
  starting transfers between devices  17.7 us (2%)
  between operations  14 us (1%)
  other arithmetic  11.4 us (1%)
    all_to_all x1, waiting for transfers between devices, per_device(): lax.all_to_all(slot_grads, 'expert', split_axis=0, concat_axis=0, tiled=T...  472 us
    all_to_all x1, blocking collectives, per_device(): lax.all_to_all(x_send.reshape(slot_total, capacity, width_part), 'expert'...  67.7 us
    reduce_scatter x1, waiting for transfers between devices, per_device(): lax.psum_scatter(input_part.astype(jnp.bfloat16), 'tensor', scatter_dimen...  67 us
    all_to_all x1, blocking collectives, per_device(): lax.all_to_all(dy_send.reshape(slot_total, capacity, width_part), 'expert...  66.5 us
    all_gather x1, waiting for transfers between devices, per_device(): lax.all_gather(dy_recv.reshape(row_total, width_part), 'tensor', axis=1,...  58.8 us
    all_to_all x1, waiting for transfers between devices, per_device(): lax.all_to_all(row_input.reshape(slot_total, capacity, width_part), 'expe...  28.8 us
    dot_general x1, matrix products, per_device(): jnp.einsum('es,skaf->ekaf', combine_map, lax.all_to_all(slot_grads, 'expe...  23.5 us
    unnamed x23, local copies, waits for them, and re-layouts  23.1 us
  transfers between devices with their start and end apart: 6, of which 6 were waited for; matrix products, arithmetic and copies ran while one was open for 5% of the time, Pallas kernels for 0%

commit v1 on v0

v1 whole, which is shorter than its diff:
```python
import jax
import jax.numpy as jnp
from jax import lax
from jax.experimental import pallas as pl
from jax.experimental.pallas import tpu as pltpu
from jax.sharding import PartitionSpec as P


BF = jnp.bfloat16
F32 = jnp.float32
LANES = 128
ANY = pl.BlockSpec(memory_space=pl.ANY)


def split_axis(total):
    cores = 2
    chips = total // cores
    b = 1
    while b * b * 4 <= chips:
        b *= 2
    return chips // b, b, cores


def block_of(size, most):
    return max(n for n in range(LANES, most + 1, LANES) if size % n == 0)


class Grid:
    def __init__(self):
        self.total = lax.axis_size("expert")
        self.sizes = split_axis(self.total)
        self.me = lax.axis_index("expert")
        _, nb, nc = self.sizes
        self.pos = (self.me // (nb * nc), (self.me // nc) % nb, self.me % nc)
        self.parts = lax.axis_size("tensor")
        self.part = lax.axis_index("tensor")

    def flat(self, a, b, c):
        _, nb, nc = self.sizes
        return (a * nb + b) * nc + c

    def shift(self, value, axis, step):
        pairs = []
        for a in range(self.sizes[0]):
            for b in range(self.sizes[1]):
                for c in range(self.sizes[2]):
                    src = [a, b, c]
                    src[axis] = (src[axis] + step) % self.sizes[axis]
                    pairs.append((self.flat(*src), self.flat(a, b, c)))
        return lax.ppermute(value, "expert", pairs)

    def tensor_shift(self, value, step):
        n = self.parts
        return lax.ppermute(value, "tensor", [((i + step) % n, i) for i in range(n)])

    def ids(self):
        na, nb, nc = self.sizes
        a, b, c = self.pos
        places = [(da, db, dc) for dc in range(nc) for db in range(nb) for da in range(na)]
        return jnp.stack(
            [self.flat((a + da) % na, (b + db) % nb, (c + dc) % nc) for da, db, dc in places]
        ).astype(jnp.int32)

    def gather_small(self, own):
        out = own[None]
        for axis in range(3):
            parts = [out] + [self.shift(out, axis, k) for k in range(1, self.sizes[axis])]
            out = jnp.concatenate(parts)
        return out

    def gather(self, own):
        na, nb, nc = self.sizes
        line = [own]
        for k in range(1, na):
            line.append(self.shift(own, 0, k))
        plane = list(line)
        for j in range(1, nb):
            for k in range(na):
                plane.append(self.shift(line[k], 1, j))
        out = list(plane)
        for d in range(1, nc):
            for piece in plane:
                out.append(self.shift(piece, 2, d))
        return out

    def gather_rows(self, own):
        na, nb, nc = self.sizes
        part = own.shape[1] // self.parts
        mine = lax.dynamic_slice_in_dim(own, self.part * part, part, 1)
        plane = [(0, None, own)]
        line = []
        for k in range(1, na):
            line.append(self.shift(mine, 0, k))
        for j in range(1, nb):
            plane.append((j * na, None, self.shift(own, 1, j)))
        groups = [(1, jnp.concatenate(line))]
        for j in range(1, nb):
            groups.append((j * na + 1, self.shift(groups[0][1], 1, j)))
        for block, piece in groups:
            plane.append((block, 0, piece))
            for h in range(1, self.parts):
                plane.append((block, h, self.tensor_shift(piece, h)))
        out = list(plane)
        for d in range(1, nc):
            for block, h, piece in plane:
                out.append((d * na * nb + block, h, self.shift(piece, 2, d)))
        return out


def load_rows(where, at_ref, piece_refs, whole, sem, parts, tok):
    part = whole.shape[1] // parts
    copies = []
    for n, ((block, h), ref) in enumerate(zip(where, piece_refs)):
        rows = pl.ds(block * tok, ref.shape[0])
        if h is None:
            to = whole.at[rows, :]
        else:
            start = pl.multiple_of(((at_ref[0] + h) % parts) * part, LANES)
            to = whole.at[rows, pl.ds(start, part)]
        copies.append(pltpu.make_async_copy(ref, to, sem.at[n]))
    for copy in copies:
        copy.start()
    for copy in copies:
        copy.wait()


def pick_matrix(place, rows):
    ids = lax.broadcasted_iota(jnp.int32, (rows, place.shape[1]), 0)
    return jnp.where(ids == place, 1.0, 0.0).astype(BF)


def window_of(width, depth):
    return min(width, -(-(depth + LANES - 1) // LANES) * LANES)


def gate_kernel(where, parts, tok, at_ref, wg_ref, wu_ref, gate_ref, place_ref, *refs):
    count = len(where)
    pieces = refs[:count]
    proj_ref, up_ref, down_ref, window_ref, whole, acc, sem, wsem = refs[count:]
    j = pl.program_id(0)
    block = wg_ref.shape[0]
    window = window_ref.shape[1]

    @pl.when(j == 0)
    def _():
        load_rows(where, at_ref, pieces, whole, sem, parts, tok)

    cols = pl.ds(pl.multiple_of(j * block, LANES), block)
    x = whole[:, cols]
    g = jnp.dot(x, wg_ref[...], preferred_element_type=F32)
    u = jnp.dot(x, wu_ref[...], preferred_element_type=F32)

    @pl.when(j == 0)
    def _():
        acc[0] = g
        acc[1] = u

    @pl.when(j > 0)
    def _():
        acc[0] += g
        acc[1] += u

    @pl.when(j == pl.num_programs(0) - 1)
    def _():
        start = pl.multiple_of(at_ref[1], LANES)
        copy = pltpu.make_async_copy(whole.at[:, pl.ds(start, window)], window_ref, wsem)
        copy.start()
        proj, up = acc[0], acc[1]
        proj_ref[...] = proj
        up_ref[...] = up
        hidden = proj * jax.nn.sigmoid(proj) * up
        weighted = (gate_ref[...] * hidden).astype(BF)
        pick = pick_matrix(place_ref[...], down_ref.shape[0])
        down_ref[...] = jnp.dot(pick, weighted, preferred_element_type=F32).astype(BF)
        copy.wait()


def down_kernel(where, parts, tok, at_ref, wd_ref, gate_ref, place_ref, proj_ref, up_ref, *refs):
    count = len(where)
    pieces = refs[:count]
    pre_ref, upg_ref, send_ref, score_ref, window_ref, whole, acc, sem, wsem = refs[count:]
    j = pl.program_id(0)
    block = wd_ref.shape[0]
    window = window_ref.shape[1]

    @pl.when(j == 0)
    def _():
        load_rows(where, at_ref, pieces, whole, sem, parts, tok)

    cols = pl.ds(pl.multiple_of(j * block, LANES), block)
    d = jnp.dot(whole[:, cols], wd_ref[...], preferred_element_type=F32)

    @pl.when(j == 0)
    def _():
        acc[...] = d

    @pl.when(j > 0)
    def _():
        acc[...] += d

    @pl.when(j == pl.num_programs(0) - 1)
    def _():
        start = pl.multiple_of(at_ref[1], LANES)
        copy = pltpu.make_async_copy(whole.at[:, pl.ds(start, window)], window_ref, wsem)
        copy.start()
        proj, up, dy_down = proj_ref[...], up_ref[...], acc[...]
        sigma = jax.nn.sigmoid(proj)
        activated = proj * sigma
        score = jnp.sum(activated * up * dy_down, axis=1, keepdims=True)
        lane = lax.broadcasted_iota(jnp.int32, score_ref.shape, 1)
        score_ref[...] = jnp.where(lane == at_ref[2], score, 0.0).astype(BF)
        grad = gate_ref[...] * dy_down
        upg = (grad * activated).astype(BF)
        pre = (grad * up * sigma * (1.0 + proj * (1.0 - sigma))).astype(BF)
        pre_ref[...] = pre
        upg_ref[...] = upg
        rows, hidden = send_ref.shape[0], pre.shape[1]
        pick = pick_matrix(place_ref[...], rows)
        send_ref[:, :hidden] = jnp.dot(pick, pre, preferred_element_type=F32).astype(BF)
        send_ref[:, hidden:] = jnp.dot(pick, upg, preferred_element_type=F32).astype(BF)
        copy.wait()


def full(shape):
    return pl.BlockSpec(shape, lambda *_: (0,) * len(shape))


def forward_call(kernel, at, weights, small, pieces, outs, accs, width, rows_all, depth, parts, tok):
    where = [(block, h) for block, h, _ in pieces]
    values = [piece for _, _, piece in pieces]
    hidden = weights[0].shape[1]
    block = block_of(width, 1024)
    window = window_of(width, depth)
    body = lambda *refs: kernel(where, parts, tok, *refs)
    return pl.pallas_call(
        body,
        grid_spec=pltpu.PrefetchScalarGridSpec(
            num_scalar_prefetch=1,
            grid=(width // block,),
            in_specs=[pl.BlockSpec((block, hidden), lambda j, at: (j, 0)) for _ in weights]
            + [full(value.shape) for value in small]
            + [ANY for _ in values],
            out_specs=[full(out.shape) for out in outs] + [ANY],
            scratch_shapes=[
                pltpu.VMEM((rows_all, width), BF),
                pltpu.VMEM(accs, F32),
                pltpu.SemaphoreType.DMA((len(values),)),
                pltpu.SemaphoreType.DMA,
            ],
        ),
        out_shape=list(outs) + [jax.ShapeDtypeStruct((rows_all, window), BF)],
    )(at, *weights, *small, *values)


def input_kernel(index_ref, pre_ref, up_ref, score_ref, wg_ref, wu_ref, out_ref):
    dims = (((1,), (1,)), ((), ()))
    acc = lax.dot_general(pre_ref[...], wg_ref[...], dims, preferred_element_type=F32)
    acc = acc + lax.dot_general(up_ref[...], wu_ref[...], dims, preferred_element_type=F32)
    rows = out_ref.shape[2]
    block = wg_ref.shape[0]
    j = pl.program_id(1)
    part = out_ref.shape[3] - score_ref.shape[1]
    cols = pl.ds(pl.multiple_of(j * block, LANES), block)
    for c in range(out_ref.shape[0]):
        out_ref[c, 0, :, cols] = acc[c * rows : (c + 1) * rows].astype(BF)

    @pl.when(j == 0)
    def _():
        for c in range(out_ref.shape[0]):
            out_ref[c, 0, :, part:] = score_ref[c * rows : (c + 1) * rows, :]


def input_parts(grid, pre, up, score, w_gate, w_up):
    tokens, hidden = pre.shape
    width = w_gate.shape[0]
    parts, cores = grid.parts, grid.sizes[2]
    part = width // parts
    block = block_of(part, 512)
    steps = part // block
    index = grid.part.astype(jnp.int32).reshape(1)

    def weight_map(h, j, idx):
        return (((idx[0] + h) % parts) * steps + j, 0)

    return pl.pallas_call(
        input_kernel,
        grid_spec=pltpu.PrefetchScalarGridSpec(
            num_scalar_prefetch=1,
            grid=(parts, steps),
            in_specs=[
                full((tokens, hidden)),
                full((tokens, hidden)),
                full(score.shape),
                pl.BlockSpec((block, hidden), weight_map),
                pl.BlockSpec((block, hidden), weight_map),
            ],
            out_specs=pl.BlockSpec(
                (cores, 1, tokens // cores, part + LANES), lambda h, j, idx: (0, h, 0, 0)
            ),
        ),
        out_shape=jax.ShapeDtypeStruct((cores, parts, tokens // cores, part + LANES), BF),
    )(index, pre, up, score, w_gate, w_up)


def pick_kernel(place_ref, x_ref, dy_ref, xo_ref, dyo_ref):
    pick = pick_matrix(place_ref[0], xo_ref.shape[2])
    dims = (((1,), (1,)), ((), ()))
    xo_ref[0] = lax.dot_general(x_ref[...], pick, dims, preferred_element_type=F32).astype(BF)
    dyo_ref[0] = lax.dot_general(dy_ref[...], pick, dims, preferred_element_type=F32).astype(BF)


def picked(place, x_t, dy_t, rows):
    slots, tokens = place.shape
    depth = x_t.shape[0]
    out = jax.ShapeDtypeStruct((slots, depth, rows), BF)
    return pl.pallas_call(
        pick_kernel,
        grid=(slots,),
        in_specs=[
            pl.BlockSpec((1, 1, tokens), lambda s: (s, 0, 0)),
            full(x_t.shape),
            full(dy_t.shape),
        ],
        out_specs=[pl.BlockSpec((1, depth, rows), lambda s: (s, 0, 0))] * 2,
        out_shape=[out, out],
    )(place.reshape(slots, 1, tokens), x_t, dy_t)


def expert_kernel(slots, replicas, table_ref, rows_ref, *refs):
    pieces = refs[:slots]
    out_ref, left, right, acc, sem_l, sem_r = refs[-6:]
    e = pl.program_id(0)
    experts = slots - replicas
    count = out_ref.shape[1]
    hidden = out_ref.shape[3]

    def left_copy(i):
        return pltpu.make_async_copy(rows_ref.at[i], left.at[i], sem_l.at[i])

    def right_copy(i, at):
        return pltpu.make_async_copy(pieces[i], right.at[at], sem_r.at[at])

    @pl.when(e == 0)
    def _():
        for i in range(slots):
            left_copy(i).start()
            right_copy(i, i).start()
        for r in range(replicas):
            i = table_ref[experts + r]
            left_copy(i).wait()
            right_copy(0, i).wait()

    at = table_ref[e]
    left_copy(at).wait()
    right_copy(0, at).wait()
    rows = left[at]
    for j in range(count):
        acc[j] = jnp.dot(
            rows, right[at, :, j * hidden : (j + 1) * hidden], preferred_element_type=F32
        )
    for r in range(replicas):

        @pl.when(table_ref[slots + r] == e)
        def _(r=r):
            i = table_ref[experts + r]
            for j in range(count):
                acc[j] += jnp.dot(
                    left[i], right[i, :, j * hidden : (j + 1) * hidden], preferred_element_type=F32
                )

    for j in range(count):
        out_ref[0, j] = acc[j].astype(BF)


def expert_sums(table, rows, pieces, first, count, total, previous, replicas):
    slots, depth, n = rows.shape
    experts = slots - replicas
    hidden = pieces[0].shape[1] // count
    operands = [rows] + list(pieces)
    aliases = {}
    if previous is not None:
        operands.append(previous)
        aliases = {len(operands): 0}
    return pl.pallas_call(
        lambda *refs: expert_kernel(slots, replicas, *refs),
        grid_spec=pltpu.PrefetchScalarGridSpec(
            num_scalar_prefetch=1,
            grid=(experts,),
            in_specs=[ANY for _ in operands],
            out_specs=pl.BlockSpec(
                (1, count, depth, hidden), lambda e, t: (e, first // count, 0, 0)
            ),
            scratch_shapes=[
                pltpu.VMEM((slots, depth, n), BF),
                pltpu.VMEM((slots, n, count * hidden), BF),
                pltpu.VMEM((count, depth, hidden), F32),
                pltpu.SemaphoreType.DMA((slots,)),
                pltpu.SemaphoreType.DMA((slots,)),
            ],
        ),
        out_shape=jax.ShapeDtypeStruct((experts, total, depth, hidden), BF),
        input_output_aliases=aliases,
    )(table, *operands)


def after(value, *others):
    return lax.optimization_barrier((value, *others))[0]


def per_device(tokens, cotangent, gate_weights, route_slots, replica_owner, w_gate, w_up, w_down):
    grid = Grid()
    slots = grid.total
    na, nb, nc = grid.sizes
    tok, width = tokens.shape
    top = route_slots.shape[1]
    rows = tok * top * 3 // 2
    replicas = replica_owner.shape[0]
    wg, wu, wd = w_gate[0], w_up[0], w_down[0]
    hidden = wg.shape[1]
    all_tok = tok * slots
    depth = width // slots
    part = width // grid.parts

    meta = jnp.concatenate(
        [route_slots.astype(BF), gate_weights, jnp.zeros((tok, LANES - 2 * top), BF)], axis=1
    )
    meta_all = grid.gather_small(meta).reshape(all_tok, LANES)
    x_pieces = grid.gather_rows(tokens)
    dy_pieces = grid.gather_rows(cotangent)

    ids = grid.ids()
    routes = meta_all[:, :top].astype(jnp.int32)
    gates = meta_all[:, top : 2 * top].astype(F32)
    token_ids = (ids[:, None] * tok + jnp.arange(tok, dtype=jnp.int32)[None, :]).reshape(-1)
    named = jnp.any(routes[None, :, :] == ids[:, None, None], axis=2)
    before = (token_ids[:, None] < token_ids[None, :]).astype(BF)
    place = jnp.dot(named.astype(BF), before, preferred_element_type=F32).astype(jnp.int32)
    place = jnp.where(named, place, -1)
    gate = jnp.sum(jnp.where(routes == ids[0], gates, 0.0), axis=1)[:, None]

    first = grid.me * depth
    window = window_of(width, depth)
    start = jnp.minimum(first // LANES * LANES, width - window)
    at = jnp.stack([grid.part, start, grid.me]).astype(jnp.int32)
    square = jax.ShapeDtypeStruct((all_tok, hidden), F32)
    square_b = jax.ShapeDtypeStruct((all_tok, hidden), BF)
    proj, up_proj, down, x_window = forward_call(
        gate_kernel,
        at,
        [wg, wu],
        [gate, place[:1]],
        x_pieces,
        [square, square, jax.ShapeDtypeStruct((rows, hidden), BF)],
        (2, all_tok, hidden),
        width,
        all_tok,
        depth,
        grid.parts,
        tok,
    )
    down_all = grid.gather(down)
    pre, upg, send, score, dy_window = forward_call(
        down_kernel,
        at,
        [wd],
        [gate, place[:1], proj, up_proj],
        dy_pieces,
        [
            square_b,
            square_b,
            jax.ShapeDtypeStruct((rows, 2 * hidden), BF),
            jax.ShapeDtypeStruct((all_tok, LANES), BF),
        ],
        (all_tok, hidden),
        width,
        all_tok,
        depth,
        grid.parts,
        tok,
    )
    send_all = grid.gather(send)

    parts = input_parts(grid, pre, upg, score, wg, wu)
    kept = parts[0].astype(F32)
    for k in range(1, nc):
        kept = kept + grid.shift(parts[k], 2, -k).astype(F32)
    kept = kept.astype(BF)
    terms = [kept[0]] + [grid.tensor_shift(kept[k], -k) for k in range(1, grid.parts)]
    if grid.parts > 2:
        terms = list(jnp.roll(jnp.stack(terms)[::-1], grid.part + 1, axis=0))
    total = terms[0].astype(F32)
    for term in terms[1:]:
        total = total + term.astype(F32)
    total = total.astype(BF).reshape(nb, na, tok, part + LANES)
    line = total[0].astype(F32)
    for k in range(1, nb):
        line = line + grid.shift(total[k], 1, -k).astype(F32)
    line = line.astype(BF)
    last = line[0].astype(F32)
    for k in range(1, na):
        last = last + grid.shift(line[k], 0, -k).astype(F32)
    input_grads = last[:, :part].astype(BF)
    lane = jnp.arange(LANES, dtype=jnp.int32)
    own_routes = route_slots[:, :, None] == lane[None, None, :]
    gate_grads = jnp.sum(jnp.where(own_routes, last[:, None, part:], 0.0), axis=2).astype(BF)

    x_window, dy_window = after(x_window, parts), after(dy_window, parts)
    x_t = lax.dynamic_slice_in_dim(x_window, first - start, depth, 1).T
    dy_t = lax.dynamic_slice_in_dim(dy_window, first - start, depth, 1).T
    x_pick, dy_pick = picked(place, x_t, dy_t, rows)
    spot = jnp.sum(
        jnp.where(
            ids[None, :] == jnp.arange(slots, dtype=jnp.int32)[:, None],
            jnp.arange(slots, dtype=jnp.int32)[None, :],
            0,
        ),
        axis=1,
    )
    table = jnp.concatenate([spot, replica_owner]).astype(jnp.int32)
    out = expert_sums(table, dy_pick, down_all, 2, 1, 3, None, replicas)
    out = expert_sums(table, x_pick, send_all, 0, 2, 3, out, replicas)
    return input_grads, gate_grads, jnp.transpose(out, (0, 2, 1, 3))


def solution(mesh):
    in_specs = (
        P("expert", None),
        P("expert", None),
        P("expert", None),
        P("expert", None),
        P(),
        P("expert", None, "tensor"),
        P("expert", None, "tensor"),
        P("expert", None, "tensor"),
    )
    out_specs = (P("expert", "tensor"), P("expert", None), P(None, "expert", None, "tensor"))

    return jax.shard_map(
        per_device, mesh=mesh, in_specs=in_specs, out_specs=out_specs, check_vma=False
    )
```

time: 953 us -> 425 us (0.45)
  waiting for transfers between devices: 635 us -> 227 us
  blocking collectives: 148 us -> 0 us
  matrix products: 102 us -> 0.34 us
  Pallas kernels: 0 us -> 99.9 us
  starting transfers between devices: 17.7 us -> 66.9 us
  between operations: 14 us -> 1.37 us
    all_to_all x3 -> x0, waiting for transfers between devices: 505 us -> none  [the longest x1 472 us: per_device(): lax.all_to_all(slot_grads, 'expert', split_axis=0, concat_axis=0, tiled=T...]
    ppermute x0 -> x67, waiting for transfers between devices: none -> 227 us  [the longest x62 206 us: shift(): return lax.ppermute(value, 'expert', pairs)]
    all_to_all x3 -> x0, blocking collectives: 143 us -> none  [the longest x1 67.7 us: per_device(): lax.all_to_all(x_send.reshape(slot_total, capacity, width_part), 'expert'...]
    dot_general x13 -> x1, matrix products: 102 us -> 0.34 us  [per_device(): jnp.dot(named.astype(BF), before, preferred_element_type=F32)]
    pallas_call x0 -> x6, Pallas kernels: none -> 99.9 us  [the longest x2 34.8 us: expert_sums(): pl.pallas_call(lambda *refs: expert_kernel(slots, replicas, *refs), grid_...]
    reduce_scatter x1 -> x0, waiting for transfers between devices: 67 us -> none  [per_device(): lax.psum_scatter(input_part.astype(jnp.bfloat16), 'tensor', scatter_dimen...]
    ppermute x0 -> x67, starting transfers between devices: none -> 66.9 us  [the longest x62 59.3 us: shift(): return lax.ppermute(value, 'expert', pairs)]
    all_gather x2 -> x0, waiting for transfers between devices: 62.8 us -> none  [the longest x1 58.8 us: per_device(): lax.all_gather(dy_recv.reshape(row_total, width_part), 'tensor', axis=1,...]
  transfers between devices with their start and end apart: 6 -> 67, of which waited for: 6 -> 24; matrix products, arithmetic and copies ran while one was open for 5% -> 4% of each run, Pallas kernels for 0% -> 16%
where the time goes in v1:
time: 425 us; the launch traced here: 420 us
  waiting for transfers between devices  227 us (53%)
  Pallas kernels  99.9 us (24%)
  starting transfers between devices  66.9 us (16%)
  local copies, waits for them, and re-layouts  19.5 us (5%)
  other arithmetic  5.25 us (1%)
    ppermute x62, waiting for transfers between devices, shift(): return lax.ppermute(value, 'expert', pairs)  206 us
    ppermute x62, starting transfers between devices, shift(): return lax.ppermute(value, 'expert', pairs)  59.3 us
    pallas_call x2, Pallas kernels, expert_sums(): pl.pallas_call(lambda *refs: expert_kernel(slots, replicas, *refs), grid_...  34.8 us
    pallas_call x2, Pallas kernels, forward_call(): pl.pallas_call(body, grid_spec=pltpu.PrefetchScalarGridSpec(num_scalar_pr...  33.8 us
    ppermute x5, waiting for transfers between devices, tensor_shift(): lax.ppermute(value, 'tensor', [((i + step) % n, i) for i in range(n)])  20.6 us
    pallas_call x1, Pallas kernels, input_parts(): pl.pallas_call(input_kernel, grid_spec=pltpu.PrefetchScalarGridSpec(num_s...  18.1 us
    pallas_call x1, Pallas kernels, picked(): pl.pallas_call(pick_kernel, grid=(slots,), in_specs=[pl.BlockSpec((1, 1,...  13.2 us
  transfers between devices with their start and end apart: 67, of which 24 were waited for; matrix products, arithmetic and copies ran while one was open for 4% of the time, Pallas kernels for 16%

profile of v1, /device:TPU:16, one launch (start us, length us, event | category | flops | bytes accessed | tf_op | source)
XLA Modules:
  0.0 420.0 jit_solution(7341932750303535308)
XLA Ops:
  19.2 19.2 %collective-permute-done.6 = bf16[32,3584]{1,0:T(8,128)(2,1)S(1)} collective-permute-done((bf16[32,3584]{1,0:T(8,128)(2,1)S(1)}, bf16[32,3584]{1,0:T(8,128)(2,1)S(1)}, u32[]{:S(2)}, u32[]{:S(2)}) %collective-permute-start.6) | collective-permute-done | bytes 229408 | tf_op jit(solution)/shard_map/ppermute | solution.py:50
  40.0 8.1 %collective-permute-done.7 = bf16[32,3584]{1,0:T(8,128)(2,1)S(1)} collective-permute-done((bf16[32,3584]{1,0:T(8,128)(2,1)S(1)}, bf16[32,3584]{1,0:T(8,128)(2,1)S(1)}, u32[]{:S(2)}, u32[]{:S(2)}) %collective-permute-start.7) | collective-permute-done | bytes 229408 | tf_op jit(solution)/shard_map/ppermute | solution.py:50
  55.5 8.3 %collective-permute-done.18.refs_7_ = bf16[32,7168]{1,0:T(8,128)(2,1)S(1)} collective-permute-done((bf16[32,7168]{1,0:T(8,128)(2,1)}, bf16[32,7168]{1,0:T(8,128)(2,1)S(1)}, u32[]{:S(2)}, u32[]{:S(2)}) %collective-permute-start.18) | collective-permute-done | bytes 458784 | tf_op jit(solution)/shard_map/ppermute | solution.py:50
  65.3 13.3 %collective-permute-done.10.refs_9_ = bf16[96,3584]{1,0:T(8,128)(2,1)S(1)} collective-permute-done((bf16[96,3584]{1,0:T(8,128)(2,1)S(1)}, bf16[96,3584]{1,0:T(8,128)(2,1)S(1)}, u32[]{:S(2)}, u32[]{:S(2)}) %collective-permute-start.10) | collective-permute-done | bytes 688160 | tf_op jit(solution)/shard_map/ppermute | solution.py:50
  82.0 10.6 %collective-permute-done.23.refs_10_ = bf16[96,3584]{1,0:T(8,128)(2,1)} collective-permute-done((bf16[96,3584]{1,0:T(8,128)(2,1)S(1)}, bf16[96,3584]{1,0:T(8,128)(2,1)}, u32[]{:S(2)}, u32[]{:S(2)}) %collective-permute-start.23) | collective-permute-done | bytes 688160 | tf_op jit(solution)/shard_map/ppermute | solution.py:50
  94.6 7.2 %collective-permute-done.11.refs_10_ = bf16[96,3584]{1,0:T(8,128)(2,1)S(1)} collective-permute-done((bf16[96,3584]{1,0:T(8,128)(2,1)S(1)}, bf16[96,3584]{1,0:T(8,128)(2,1)S(1)}, u32[]{:S(2)}, u32[]{:S(2)}) %collective-permute-start.11) | collective-permute-done | bytes 688160 | tf_op jit(solution)/shard_map/ppermute | solution.py:54
  104.0 11.9 %collective-permute-done.24.refs_11_ = bf16[96,3584]{1,0:T(8,128)(2,1)} collective-permute-done((bf16[96,3584]{1,0:T(8,128)(2,1)}, bf16[96,3584]{1,0:T(8,128)(2,1)}, u32[]{:S(2)}, u32[]{:S(2)}) %collective-permute-start.24) | collective-permute-done | bytes 688160 | tf_op jit(solution)/shard_map/ppermute | solution.py:54
  122.7 18.5 %shard_map.103 = (f32[512,512]{1,0:T(8,128)}, f32[512,512]{1,0:T(8,128)}, bf16[384,512]{1,0:T(8,128)(2,1)}, bf16[512,640]{1,0:T(8,128)(2,1)}) custom-call(s32[3]{0:T(128)} %pad_add_fusion.refs_0_, bf16[7168,512]{1,0:T(8,128)(2,1)} %bitcast.62, bf16[7168,512]{1,0:T(8,128)(2,1)} %bitcast.64, f32[512,1]{1,0:T(8,128)} %copy.48.refs_3_.refs_2_, ...), custom_call_target="tpu_custom_call" | custom-call | tf_op jit(solution)/shard_map/pallas_call | solution.py:235
  141.2 15.3 %shard_map.104 = (bf16[512,512]{1,0:T(8,128)(2,1)}, bf16[512,512]{1,0:T(8,128)(2,1)}, bf16[384,1024]{1,0:T(8,128)(2,1)}, bf16[512,128]{1,0:T(8,128)(2,1)}, bf16[512,640]{1,0:T(8,128)(2,1)}) custom-call(s32[3]{0:T(128)} %pad_add_fusion.refs_0_, bf16[7168,512]{1,0:T(8,128)(2,1)} %bitcast.66, f32[512,1]{1,0:T(8,128)} %copy.48.refs_3_.refs_2_, ...), custom_call_target="tpu_custom_call" | custom-call | tf_op jit(solution)/shard_map/pallas_call | solution.py:235
  156.6 18.1 %shard_map.105 = bf16[2,2,256,3712]{3,2,1,0:T(8,128)(2,1)} custom-call(s32[1]{0:T(128)} %bitcast.index_ref, bf16[512,512]{1,0:T(8,128)(2,1)} %get-tuple-element.18.pre_ref, bf16[512,512]{1,0:T(8,128)(2,1)} %get-tuple-element.19.up_ref, bf16[512,128]{1,0:T(8,128)(2,1)} %get-tuple-element.20.score_ref, bf16[7168,512]{1,0:T(8,128)(2,1)} %bitcast.63, ...), custom_call_target="tpu_custom_call" | custom-call | tf_op jit(solution)/shard_map/pallas_call | solution.py:285
  177.3 6.5 %collective-permute-done.31 = bf16[2,256,3712]{2,1,0:T(8,128)(2,1)S(1)} collective-permute-done((bf16[2,256,3712]{2,1,0:T(8,128)(2,1)S(1)}, bf16[2,256,3712]{2,1,0:T(8,128)(2,1)S(1)}, u32[]{:S(2)}, u32[]{:S(2)}) %collective-permute-start.31) | collective-permute-done | bytes 3801120 | tf_op jit(solution)/shard_map/ppermute | solution.py:50
  201.3 15.6 %collective-permute-done.53.refs_4_ = bf16[384,512]{1,0:T(8,128)(2,1)S(1)} collective-permute-done((bf16[384,512]{1,0:T(8,128)(2,1)S(1)}, bf16[384,512]{1,0:T(8,128)(2,1)S(1)}, u32[]{:S(2)}, u32[]{:S(2)}) %collective-permute-start.53) | collective-permute-done | bytes 393248 | tf_op jit(solution)/shard_map/ppermute | solution.py:50
  218.5 6.8 %collective-permute-done.52.refs_3_ = bf16[384,512]{1,0:T(8,128)(2,1)S(1)} collective-permute-done((bf16[384,512]{1,0:T(8,128)(2,1)S(1)}, bf16[384,512]{1,0:T(8,128)(2,1)S(1)}, u32[]{:S(2)}, u32[]{:S(2)}) %collective-permute-start.52) | collective-permute-done | bytes 393248 | tf_op jit(solution)/shard_map/ppermute | solution.py:50
  230.0 9.2 %collective-permute-start.39 = (bf16[384,1024]{1,0:T(8,128)(2,1)}, bf16[384,1024]{1,0:T(8,128)(2,1)}, u32[]{:S(2)}, u32[]{:S(2)}) collective-permute-start(bf16[384,1024]{1,0:T(8,128)(2,1)} %get-tuple-element.26.refs_2_), channel_id=1, source_target_pairs={{24,0},{26,2},{28,4},{30,6},{0,8},{2,10},{4,12},{6,14},{8,16},{10,... | collective-permute-start | bytes 2359304 | tf_op jit(solution)/shard_map/ppermute | solution.py:50
  242.6 19.7 %collective-permute-done.56.refs_7_ = bf16[384,512]{1,0:T(8,128)(2,1)} collective-permute-done((bf16[384,512]{1,0:T(8,128)(2,1)S(1)}, bf16[384,512]{1,0:T(8,128)(2,1)}, u32[]{:S(2)}, u32[]{:S(2)}) %collective-permute-start.56) | collective-permute-done | bytes 393248 | tf_op jit(solution)/shard_map/ppermute | solution.py:50
  263.8 6.1 %collective-permute-start.37 = (bf16[384,1024]{1,0:T(8,128)(2,1)}, bf16[384,1024]{1,0:T(8,128)(2,1)}, u32[]{:S(2)}, u32[]{:S(2)}) collective-permute-start(bf16[384,1024]{1,0:T(8,128)(2,1)} %get-tuple-element.26.refs_2_), channel_id=1, source_target_pairs={{8,0},{10,2},{12,4},{14,6},{16,8},{18,10},{20,12},{22,14},{24,16},... | collective-permute-start | bytes 2359304 | tf_op jit(solution)/shard_map/ppermute | solution.py:50
  272.9 14.3 %collective-permute-done.38.refs_4_ = bf16[384,1024]{1,0:T(8,128)(2,1)} collective-permute-done((bf16[384,1024]{1,0:T(8,128)(2,1)}, bf16[384,1024]{1,0:T(8,128)(2,1)}, u32[]{:S(2)}, u32[]{:S(2)}) %collective-permute-start.38) | collective-permute-done | bytes 786464 | tf_op jit(solution)/shard_map/ppermute | solution.py:50
  287.3 16.6 %collective-permute-done.37.refs_3_ = bf16[384,1024]{1,0:T(8,128)(2,1)} collective-permute-done((bf16[384,1024]{1,0:T(8,128)(2,1)}, bf16[384,1024]{1,0:T(8,128)(2,1)}, u32[]{:S(2)}, u32[]{:S(2)}) %collective-permute-start.37) | collective-permute-done | bytes 786464 | tf_op jit(solution)/shard_map/ppermute | solution.py:50
  308.0 16.5 %collective-permute-done.43.refs_9_ = bf16[384,1024]{1,0:T(8,128)(2,1)S(1)} collective-permute-done((bf16[384,1024]{1,0:T(8,128)(2,1)}, bf16[384,1024]{1,0:T(8,128)(2,1)S(1)}, u32[]{:S(2)}, u32[]{:S(2)}) %collective-permute-start.43) | collective-permute-done | bytes 786464 | tf_op jit(solution)/shard_map/ppermute | solution.py:50
  324.6 17.0 %collective-permute-done.42.refs_8_ = bf16[384,1024]{1,0:T(8,128)(2,1)} collective-permute-done((bf16[384,1024]{1,0:T(8,128)(2,1)}, bf16[384,1024]{1,0:T(8,128)(2,1)}, u32[]{:S(2)}, u32[]{:S(2)}) %collective-permute-start.42) | collective-permute-done | bytes 786464 | tf_op jit(solution)/shard_map/ppermute | solution.py:50
  341.5 16.4 %collective-permute-done.41.refs_7_ = bf16[384,1024]{1,0:T(8,128)(2,1)} collective-permute-done((bf16[384,1024]{1,0:T(8,128)(2,1)}, bf16[384,1024]{1,0:T(8,128)(2,1)}, u32[]{:S(2)}, u32[]{:S(2)}) %collective-permute-start.41) | collective-permute-done | bytes 786464 | tf_op jit(solution)/shard_map/ppermute | solution.py:50
  369.2 13.2 %shard_map.106 = (bf16[16,448,384]{2,1,0:T(8,128)(2,1)}, bf16[16,448,384]{2,1,0:T(8,128)(2,1)}) custom-call(s32[16,1,512]{2,1,0:T(1,128)} %reshape.192.place_ref, bf16[448,512]{1,0:T(8,128)(2,1)} %get-tuple-element.56.x_ref, bf16[448,512]{1,0:T(8,128)(2,1)} %get-tuple-element.55.dy_ref), custom_call_target="tpu_custom_call" | custom-call | tf_op jit(solution)/shard_map/pallas_call | solution.py:316
  382.5 14.7 %shard_map.107.refs_18_ = bf16[14,3,448,512]{3,2,1,0:T(8,128)(2,1)} custom-call(s32[18]{0:T(128)} %pad_add_fusion.1.refs_0_, bf16[16,448,384]{2,1,0:T(8,128)(2,1)} %get-tuple-element.27.refs_1_, bf16[384,512]{1,0:T(8,128)(2,1)} %get-tuple-element.28.refs_2_, bf16[384,512]{1,0:T(8,128)(2,1)} %copy-done.23, bf16[384,512]{1,0:T(8,128)(2,1)} %copy-done.22, ...), custom_call_target="tpu_custom_call" | custom-call | tf_op jit(solution)/shard_map/pallas_call | solution.py:384
  397.1 20.1 %shard_map.108 = bf16[14,3,448,512]{3,2,1,0:T(8,128)(2,1)} custom-call(s32[18]{0:T(128)} %pad_add_fusion.1.refs_0_, bf16[16,448,384]{2,1,0:T(8,128)(2,1)} %get-tuple-element.25.refs_1_, bf16[384,1024]{1,0:T(8,128)(2,1)} %get-tuple-element.26.refs_2_, bf16[384,1024]{1,0:T(8,128)(2,1)} %collective-permute-done.37.refs_3_, ...), custom_call_target="tpu_custom_call", output_to_operand_aliasing={{}: (18, {})} | custom-call | tf_op jit(solution)/shard_map/pallas_call | solution.py:384
  (232 shorter events, 95.5 us)
Async XLA Ops:
  6.4 45.9 %collective-permute-start.21 = (bf16[32,3584]{1,0:T(8,128)(2,1)S(1)}, bf16[32,3584]{1,0:T(8,128)(2,1)S(1)}, u32[]{:S(2)}, u32[]{:S(2)}) collective-permute-start(bf16[32,3584]{1,0:T(8,128)(2,1)S(1)} %constant_dynamic-slice_fusion), channel_id=1, source_target_pairs={{24,0},{26,2},{28,4},{30,6},{0,8},{2,10},{4,12},{6,14},{8,16},{10,... | collective-permute-start | bytes 688136 | tf_op jit(solution)/shard_map/ppermute | solution.py:50
  7.3 44.5 %collective-permute-start.20 = (bf16[32,3584]{1,0:T(8,128)(2,1)S(1)}, bf16[32,3584]{1,0:T(8,128)(2,1)S(1)}, u32[]{:S(2)}, u32[]{:S(2)}) collective-permute-start(bf16[32,3584]{1,0:T(8,128)(2,1)S(1)} %constant_dynamic-slice_fusion), channel_id=1, source_target_pairs={{16,0},{18,2},{20,4},{22,6},{24,8},{26,10},{28,12},{30,14},{0,16},... | collective-permute-start | bytes 688136 | tf_op jit(solution)/shard_map/ppermute | solution.py:50
  52.4 40.2 %collective-permute-start.23 = (bf16[96,3584]{1,0:T(8,128)(2,1)S(1)}, bf16[96,3584]{1,0:T(8,128)(2,1)}, u32[]{:S(2)}, u32[]{:S(2)}) collective-permute-start(bf16[96,3584]{1,0:T(8,128)(2,1)S(1)} %constant_dynamic-update-slice_fusion.14.refs_8_), channel_id=1, source_target_pairs={{4,0},{6,2},{0,4},{2,6},{12,8},{14,10},{8,12},{10,14},{20,16},{22,... | collective-permute-start | bytes 2064392 | tf_op jit(solution)/shard_map/ppermute | solution.py:50
  54.0 40.1 %collective-permute-start.22 = (bf16[96,3584]{1,0:T(8,128)(2,1)S(1)}, bf16[96,3584]{1,0:T(8,128)(2,1)}, u32[]{:S(2)}, u32[]{:S(2)}) collective-permute-start(bf16[96,3584]{1,0:T(8,128)(2,1)S(1)} %constant_dynamic-update-slice_fusion.14.refs_8_), channel_id=1, source_target_pairs={{1,0},{0,1},{3,2},{2,3},{5,4},{4,5},{7,6},{6,7},{9,8},{8,9},{11,10... | collective-permute-start | bytes 2064392 | tf_op jit(solution)/shard_map/ppermute | solution.py:54
  103.7 37.5 %collective-permute-start.27 = (bf16[96,3584]{1,0:T(8,128)(2,1)S(1)}, bf16[96,3584]{1,0:T(8,128)(2,1)}, u32[]{:S(2)}, u32[]{:S(2)}) collective-permute-start(bf16[96,3584]{1,0:T(8,128)(2,1)S(1)} %constant_dynamic-update-slice_fusion.14.refs_8_), channel_id=1, source_target_pairs={{2,0},{0,2},{6,4},{4,6},{10,8},{8,10},{14,12},{12,14},{18,16},{16,... | collective-permute-start | bytes 2064392 | tf_op jit(solution)/shard_map/ppermute | solution.py:50
  184.9 43.5 %collective-permute-start.32 = (bf16[256,3712]{1,0:T(8,128)(2,1)S(1)}, bf16[256,3712]{1,0:T(8,128)(2,1)S(1)}, u32[]{:S(2)}, u32[]{:S(2)}) collective-permute-start(bf16[256,3712]{1,0:T(8,128)(2,1)S(1)} %slice_bitcast_fusion.2), channel_id=1, source_target_pairs={{1,0},{0,1},{3,2},{2,3},{5,4},{4,5},{7,6},{6,7},{9,8},{8,9},{11,10... | collective-permute-start | bytes 5701640 | tf_op jit(solution)/shard_map/ppermute | solution.py:54
  191.3 34.0 %collective-permute-start.52 = (bf16[384,512]{1,0:T(8,128)(2,1)S(1)}, bf16[384,512]{1,0:T(8,128)(2,1)S(1)}, u32[]{:S(2)}, u32[]{:S(2)}) collective-permute-start(bf16[384,512]{1,0:T(8,128)(2,1)S(1)} %copy-done.18), channel_id=1, source_target_pairs={{8,0},{10,2},{12,4},{14,6},{16,8},{18,10},{20,12},{22,14},{24,16},... | collective-permute-start | bytes 1179656 | tf_op jit(solution)/shard_map/ppermute | solution.py:50
  228.9 34.8 %collective-permute-start.44 = (bf16[384,1024]{1,0:T(8,128)(2,1)}, bf16[384,1024]{1,0:T(8,128)(2,1)}, u32[]{:S(2)}, u32[]{:S(2)}) collective-permute-start(bf16[384,1024]{1,0:T(8,128)(2,1)} %get-tuple-element.26.refs_2_), channel_id=1, source_target_pairs={{2,0},{0,2},{6,4},{4,6},{10,8},{8,10},{14,12},{12,14},{18,16},{16,... | collective-permute-start | bytes 2359304 | tf_op jit(solution)/shard_map/ppermute | solution.py:50
  229.5 40.3 %collective-permute-start.40 = (bf16[384,1024]{1,0:T(8,128)(2,1)}, bf16[384,1024]{1,0:T(8,128)(2,1)}, u32[]{:S(2)}, u32[]{:S(2)}) collective-permute-start(bf16[384,1024]{1,0:T(8,128)(2,1)} %get-tuple-element.26.refs_2_), channel_id=1, source_target_pairs={{4,0},{6,2},{0,4},{2,6},{12,8},{14,10},{8,12},{10,14},{20,16},{22,... | collective-permute-start | bytes 2359304 | tf_op jit(solution)/shard_map/ppermute | solution.py:50
  230.0 42.8 %collective-permute-start.39 = (bf16[384,1024]{1,0:T(8,128)(2,1)}, bf16[384,1024]{1,0:T(8,128)(2,1)}, u32[]{:S(2)}, u32[]{:S(2)}) collective-permute-start(bf16[384,1024]{1,0:T(8,128)(2,1)} %get-tuple-element.26.refs_2_), channel_id=1, source_target_pairs={{24,0},{26,2},{28,4},{30,6},{0,8},{2,10},{4,12},{6,14},{8,16},{10,... | collective-permute-start | bytes 2359304 | tf_op jit(solution)/shard_map/ppermute | solution.py:50
  239.2 47.9 %collective-permute-start.38 = (bf16[384,1024]{1,0:T(8,128)(2,1)}, bf16[384,1024]{1,0:T(8,128)(2,1)}, u32[]{:S(2)}, u32[]{:S(2)}) collective-permute-start(bf16[384,1024]{1,0:T(8,128)(2,1)} %get-tuple-element.26.refs_2_), channel_id=1, source_target_pairs={{16,0},{18,2},{20,4},{22,6},{24,8},{26,10},{28,12},{30,14},{0,16},... | collective-permute-start | bytes 2359304 | tf_op jit(solution)/shard_map/ppermute | solution.py:50
  262.2 43.9 %collective-permute-start.33 = (bf16[4,32,3712]{2,1,0:T(8,128)(2,1)S(1)}, bf16[4,32,3712]{2,1,0:T(8,128)(2,1)S(1)}, u32[]{:S(2)}, u32[]{:S(2)}) collective-permute-start(bf16[4,32,3712]{2,1,0:T(8,128)(2,1)S(1)} %bitcast.68), channel_id=1, source_target_pairs={{4,0},{6,2},{0,4},{2,6},{12,8},{14,10},{8,12},{10,14},{20,16},{22,... | collective-permute-start | bytes 2850824 | tf_op jit(solution)/shard_map/ppermute | solution.py:50
  263.8 40.1 %collective-permute-start.37 = (bf16[384,1024]{1,0:T(8,128)(2,1)}, bf16[384,1024]{1,0:T(8,128)(2,1)}, u32[]{:S(2)}, u32[]{:S(2)}) collective-permute-start(bf16[384,1024]{1,0:T(8,128)(2,1)} %get-tuple-element.26.refs_2_), channel_id=1, source_target_pairs={{8,0},{10,2},{12,4},{14,6},{16,8},{18,10},{20,12},{22,14},{24,16},... | collective-permute-start | bytes 2359304 | tf_op jit(solution)/shard_map/ppermute | solution.py:50
  269.9 34.1 %collective-permute-start.66 = (bf16[384,512]{1,0:T(8,128)(2,1)}, bf16[384,512]{1,0:T(8,128)(2,1)}, u32[]{:S(2)}, u32[]{:S(2)}) collective-permute-start(bf16[384,512]{1,0:T(8,128)(2,1)} %collective-permute-done.58.refs_9_), channel_id=1, source_target_pairs={{2,0},{0,2},{6,4},{4,6},{10,8},{8,10},{14,12},{12,14},{18,16},{16,... | collective-permute-start | bytes 1179656 | tf_op jit(solution)/shard_map/ppermute | solution.py:50
  304.7 36.8 %collective-permute-start.42 = (bf16[384,1024]{1,0:T(8,128)(2,1)}, bf16[384,1024]{1,0:T(8,128)(2,1)}, u32[]{:S(2)}, u32[]{:S(2)}) collective-permute-start(bf16[384,1024]{1,0:T(8,128)(2,1)} %collective-permute-done.38.refs_4_), channel_id=1, source_target_pairs={{4,0},{6,2},{0,4},{2,6},{12,8},{14,10},{8,12},{10,14},{20,16},{22,... | collective-permute-start | bytes 2359304 | tf_op jit(solution)/shard_map/ppermute | solution.py:50
  306.2 51.7 %collective-permute-start.41 = (bf16[384,1024]{1,0:T(8,128)(2,1)}, bf16[384,1024]{1,0:T(8,128)(2,1)}, u32[]{:S(2)}, u32[]{:S(2)}) collective-permute-start(bf16[384,1024]{1,0:T(8,128)(2,1)} %collective-permute-done.37.refs_3_), channel_id=1, source_target_pairs={{4,0},{6,2},{0,4},{2,6},{12,8},{14,10},{8,12},{10,14},{20,16},{22,... | collective-permute-start | bytes 2359304 | tf_op jit(solution)/shard_map/ppermute | solution.py:50
  307.5 51.3 %collective-permute-start.46 = (bf16[384,1024]{1,0:T(8,128)(2,1)}, bf16[384,1024]{1,0:T(8,128)(2,1)S(1)}, u32[]{:S(2)}, u32[]{:S(2)}) collective-permute-start(bf16[384,1024]{1,0:T(8,128)(2,1)} %collective-permute-done.38.refs_4_), channel_id=1, source_target_pairs={{2,0},{0,2},{6,4},{4,6},{10,8},{8,10},{14,12},{12,14},{18,16},{16,... | collective-permute-start | bytes 2359304 | tf_op jit(solution)/shard_map/ppermute | solution.py:50
  307.7 52.1 %collective-permute-start.45 = (bf16[384,1024]{1,0:T(8,128)(2,1)}, bf16[384,1024]{1,0:T(8,128)(2,1)S(1)}, u32[]{:S(2)}, u32[]{:S(2)}) collective-permute-start(bf16[384,1024]{1,0:T(8,128)(2,1)} %collective-permute-done.37.refs_3_), channel_id=1, source_target_pairs={{2,0},{0,2},{6,4},{4,6},{10,8},{8,10},{14,12},{12,14},{18,16},{16,... | collective-permute-start | bytes 2359304 | tf_op jit(solution)/shard_map/ppermute | solution.py:50
  324.6 36.9 %collective-permute-start.51 = (bf16[384,1024]{1,0:T(8,128)(2,1)S(1)}, bf16[384,1024]{1,0:T(8,128)(2,1)S(1)}, u32[]{:S(2)}, u32[]{:S(2)}) collective-permute-start(bf16[384,1024]{1,0:T(8,128)(2,1)S(1)} %collective-permute-done.43.refs_9_), channel_id=1, source_target_pairs={{2,0},{0,2},{6,4},{4,6},{10,8},{8,10},{14,12},{12,14},{18,16},{16,... | collective-permute-start | bytes 2359304 | tf_op jit(solution)/shard_map/ppermute | solution.py:50
  341.5 55.6 %collective-permute-start.50 = (bf16[384,1024]{1,0:T(8,128)(2,1)}, bf16[384,1024]{1,0:T(8,128)(2,1)}, u32[]{:S(2)}, u32[]{:S(2)}) collective-permute-start(bf16[384,1024]{1,0:T(8,128)(2,1)} %collective-permute-done.42.refs_8_), channel_id=1, source_target_pairs={{2,0},{0,2},{6,4},{4,6},{10,8},{8,10},{14,12},{12,14},{18,16},{16,... | collective-permute-start | bytes 2359304 | tf_op jit(solution)/shard_map/ppermute | solution.py:50
  357.9 39.3 %collective-permute-start.49 = (bf16[384,1024]{1,0:T(8,128)(2,1)}, bf16[384,1024]{1,0:T(8,128)(2,1)}, u32[]{:S(2)}, u32[]{:S(2)}) collective-permute-start(bf16[384,1024]{1,0:T(8,128)(2,1)} %collective-permute-done.41.refs_7_), channel_id=1, source_target_pairs={{2,0},{0,2},{6,4},{4,6},{10,8},{8,10},{14,12},{12,14},{18,16},{16,... | collective-permute-start | bytes 2359304 | tf_op jit(solution)/shard_map/ppermute | solution.py:50
  358.8 58.5 %collective-permute-start.34 = (bf16[32,3712]{1,0:T(8,128)(2,1)}, bf16[32,3712]{1,0:T(8,128)(2,1)S(1)}, u32[]{:S(2)}, u32[]{:S(2)}) collective-permute-start(bf16[32,3712]{1,0:T(8,128)(2,1)} %get-tuple-element.42), channel_id=1, source_target_pairs={{24,0},{26,2},{28,4},{30,6},{0,8},{2,10},{4,12},{6,14},{8,16},{10,... | collective-permute-start | bytes 712712 | tf_op jit(solution)/shard_map/ppermute | solution.py:50
  359.8 57.6 %collective-permute-start.36 = (bf16[32,3712]{1,0:T(8,128)(2,1)}, bf16[32,3712]{1,0:T(8,128)(2,1)S(1)}, u32[]{:S(2)}, u32[]{:S(2)}) collective-permute-start(bf16[32,3712]{1,0:T(8,128)(2,1)} %get-tuple-element.43), channel_id=1, source_target_pairs={{8,0},{10,2},{12,4},{14,6},{16,8},{18,10},{20,12},{22,14},{24,16},... | collective-permute-start | bytes 712712 | tf_op jit(solution)/shard_map/ppermute | solution.py:50
  361.4 55.9 %collective-permute-start.35 = (bf16[32,3712]{1,0:T(8,128)(2,1)}, bf16[32,3712]{1,0:T(8,128)(2,1)}, u32[]{:S(2)}, u32[]{:S(2)}) collective-permute-start(bf16[32,3712]{1,0:T(8,128)(2,1)} %get-tuple-element.44), channel_id=1, source_target_pairs={{16,0},{18,2},{20,4},{22,6},{24,8},{26,10},{28,12},{30,14},{0,16},... | collective-permute-start | bytes 712712 | tf_op jit(solution)/shard_map/ppermute | solution.py:50
  (74 other events, 2054.8 us)

commit v2 on v1

--- a/solution.py
+++ b/solution.py
@@ -23,6 +23,10 @@
 
 def block_of(size, most):
     return max(n for n in range(LANES, most + 1, LANES) if size % n == 0)
+
+
+def nearest_steps(size):
+    return sorted(range(1, size), key=lambda k: (min(k, size - k), k))
 
 
 class Grid:
@@ -64,16 +68,21 @@
     def gather_small(self, own):
         out = own[None]
         for axis in range(3):
-            parts = [out] + [self.shift(out, axis, k) for k in range(1, self.sizes[axis])]
+            parts = [out]
+            for k in range(1, self.sizes[axis]):
+                parts.append(self.shift(out, axis, k))
             out = jnp.concatenate(parts)
         return out
 
+    def nearest(self):
+        return nearest_steps(self.sizes[0])
+
     def gather(self, own):
         na, nb, nc = self.sizes
-        line = [own]
-        for k in range(1, na):
-            line.append(self.shift(own, 0, k))
-        plane = list(line)
+        line = {0: own}
+        for k in self.nearest():
+            line[k] = self.shift(own, 0, k)
+        plane = [line[k] for k in range(na)]
         for j in range(1, nb):
             for k in range(na):
                 plane.append(self.shift(line[k], 1, j))
@@ -83,40 +92,58 @@
                 out.append(self.shift(piece, 2, d))
         return out
 
-    def gather_rows(self, own):
+    def gather_rows(self, own, lent):
         na, nb, nc = self.sizes
-        part = own.shape[1] // self.parts
-        mine = lax.dynamic_slice_in_dim(own, self.part * part, part, 1)
+        width = own.shape[1]
+        keep = width - (self.parts - 1) * lent
+        mine = lax.dynamic_slice_in_dim(own, self.part * lent, keep, 1)
+        lend = self.part * ((width - lent) // (self.parts - 1) - lent)
         plane = [(0, None, own)]
-        line = []
-        for k in range(1, na):
-            line.append(self.shift(mine, 0, k))
+        swaps = [(0, None, own)]
+        line = {}
+        for k in self.nearest():
+            line[k] = self.shift(mine, 0, k)
         for j in range(1, nb):
-            plane.append((j * na, None, self.shift(own, 1, j)))
-        groups = [(1, jnp.concatenate(line))]
-        for j in range(1, nb):
-            groups.append((j * na + 1, self.shift(groups[0][1], 1, j)))
-        for block, piece in groups:
-            plane.append((block, 0, piece))
+            piece = self.shift(own, 1, j)
+            plane.append((j * na, None, piece))
+            swaps.append((j * na, None, piece))
+        for j in range(nb):
+            row = dict(line)
+            if j > 0:
+                for k in self.nearest():
+                    row[k] = self.shift(line[k], 1, j)
+            kinds = [row]
             for h in range(1, self.parts):
-                plane.append((block, h, self.tensor_shift(piece, h)))
+                lent_row = {}
+                for k in self.nearest():
+                    piece = row[k]
+                    if lent < keep:
+                        piece = lax.dynamic_slice_in_dim(piece, lend, lent, 1)
+                    lent_row[k] = self.tensor_shift(piece, h)
+                kinds.append(lent_row)
+            for h, pieces in enumerate(kinds):
+                plane += [(j * na + k, h, pieces[k]) for k in range(1, na)]
+                group = jnp.concatenate([pieces[k] for k in range(1, na)])
+                swaps.append((j * na + 1, h, group))
         out = list(plane)
         for d in range(1, nc):
-            for block, h, piece in plane:
+            for block, h, piece in swaps:
                 out.append((d * na * nb + block, h, self.shift(piece, 2, d)))
         return out
 
 
 def load_rows(where, at_ref, piece_refs, whole, sem, parts, tok):
-    part = whole.shape[1] // parts
+    width = whole.shape[1]
     copies = []
     for n, ((block, h), ref) in enumerate(zip(where, piece_refs)):
         rows = pl.ds(block * tok, ref.shape[0])
         if h is None:
             to = whole.at[rows, :]
         else:
-            start = pl.multiple_of(((at_ref[0] + h) % parts) * part, LANES)
-            to = whole.at[rows, pl.ds(start, part)]
+            cols = ref.shape[1]
+            step = (width - cols) // (parts - 1)
+            start = pl.multiple_of(((at_ref[0] + h) % parts) * step, LANES)
+            to = whole.at[rows, pl.ds(start, cols)]
         copies.append(pltpu.make_async_copy(ref, to, sem.at[n]))
     for copy in copies:
         copy.start()
@@ -178,7 +205,7 @@
 def down_kernel(where, parts, tok, at_ref, wd_ref, gate_ref, place_ref, proj_ref, up_ref, *refs):
     count = len(where)
     pieces = refs[:count]
-    pre_ref, upg_ref, send_ref, score_ref, window_ref, whole, acc, sem, wsem = refs[count:]
+    pre_ref, upg_ref, pre_rows_ref, upg_rows_ref, score_ref, window_ref, whole, acc, sem, wsem = refs[count:]
     j = pl.program_id(0)
     block = wd_ref.shape[0]
     window = window_ref.shape[1]
@@ -214,10 +241,9 @@
         pre = (grad * up * sigma * (1.0 + proj * (1.0 - sigma))).astype(BF)
         pre_ref[...] = pre
         upg_ref[...] = upg
-        rows, hidden = send_ref.shape[0], pre.shape[1]
-        pick = pick_matrix(place_ref[...], rows)
-        send_ref[:, :hidden] = jnp.dot(pick, pre, preferred_element_type=F32).astype(BF)
-        send_ref[:, hidden:] = jnp.dot(pick, upg, preferred_element_type=F32).astype(BF)
+        pick = pick_matrix(place_ref[...], pre_rows_ref.shape[0])
+        pre_rows_ref[...] = jnp.dot(pick, pre, preferred_element_type=F32).astype(BF)
+        upg_rows_ref[...] = jnp.dot(pick, upg, preferred_element_type=F32).astype(BF)
         copy.wait()
 
 
@@ -256,49 +282,45 @@
     dims = (((1,), (1,)), ((), ()))
     acc = lax.dot_general(pre_ref[...], wg_ref[...], dims, preferred_element_type=F32)
     acc = acc + lax.dot_general(up_ref[...], wu_ref[...], dims, preferred_element_type=F32)
-    rows = out_ref.shape[2]
+    rows = out_ref.shape[1]
     block = wg_ref.shape[0]
-    j = pl.program_id(1)
-    part = out_ref.shape[3] - score_ref.shape[1]
+    j = pl.program_id(0)
+    part = out_ref.shape[2] - score_ref.shape[1]
     cols = pl.ds(pl.multiple_of(j * block, LANES), block)
     for c in range(out_ref.shape[0]):
-        out_ref[c, 0, :, cols] = acc[c * rows : (c + 1) * rows].astype(BF)
+        out_ref[c, :, cols] = acc[c * rows : (c + 1) * rows].astype(BF)
 
     @pl.when(j == 0)
     def _():
         for c in range(out_ref.shape[0]):
-            out_ref[c, 0, :, part:] = score_ref[c * rows : (c + 1) * rows, :]
-
-
-def input_parts(grid, pre, up, score, w_gate, w_up):
+            out_ref[c, :, part:] = score_ref[c * rows : (c + 1) * rows, :]
+
+
+def input_part(grid, h, pre, up, score, w_gate, w_up):
     tokens, hidden = pre.shape
     width = w_gate.shape[0]
     parts, cores = grid.parts, grid.sizes[2]
     part = width // parts
     block = block_of(part, 512)
     steps = part // block
-    index = grid.part.astype(jnp.int32).reshape(1)
-
-    def weight_map(h, j, idx):
-        return (((idx[0] + h) % parts) * steps + j, 0)
-
+    index = ((grid.part + h) % parts).astype(jnp.int32).reshape(1)
+    weight = pl.BlockSpec((block, hidden), lambda j, idx: (idx[0] * steps + j, 0))
+    shape = (cores, tokens // cores, part + LANES)
     return pl.pallas_call(
         input_kernel,
         grid_spec=pltpu.PrefetchScalarGridSpec(
             num_scalar_prefetch=1,
-            grid=(parts, steps),
+            grid=(steps,),
             in_specs=[
                 full((tokens, hidden)),
                 full((tokens, hidden)),
                 full(score.shape),
-                pl.BlockSpec((block, hidden), weight_map),
-                pl.BlockSpec((block, hidden), weight_map),
+                weight,
+                weight,
             ],
-            out_specs=pl.BlockSpec(
-                (cores, 1, tokens // cores, part + LANES), lambda h, j, idx: (0, h, 0, 0)
-            ),
+            out_specs=full(shape),
         ),
-        out_shape=jax.ShapeDtypeStruct((cores, parts, tokens // cores, part + LANES), BF),
+        out_shape=jax.ShapeDtypeStruct(shape, BF),
     )(index, pre, up, score, w_gate, w_up)
 
 
@@ -342,9 +364,18 @@
 
     @pl.when(e == 0)
     def _():
-        for i in range(slots):
+        def issue(n, carry):
+            i = table_ref[jnp.where(n < replicas, experts + n, n - replicas)]
             left_copy(i).start()
-            right_copy(i, i).start()
+            for k in range(slots):
+
+                @pl.when(i == k)
+                def _(k=k):
+                    right_copy(k, k).start()
+
+            return carry
+
+        lax.fori_loop(0, slots, issue, 0)
         for r in range(replicas):
             i = table_ref[experts + r]
             left_copy(i).wait()
@@ -403,6 +434,12 @@
     )(table, *operands)
 
 
+def lent_columns(width, parts, sevenths):
+    if parts > 2:
+        return width // parts
+    return width * sevenths // 7 // LANES * LANES
+
+
 def after(value, *others):
     return lax.optimization_barrier((value, *others))[0]
 
@@ -425,8 +462,8 @@
         [route_slots.astype(BF), gate_weights, jnp.zeros((tok, LANES - 2 * top), BF)], axis=1
     )
     meta_all = grid.gather_small(meta).reshape(all_tok, LANES)
-    x_pieces = grid.gather_rows(tokens)
-    dy_pieces = grid.gather_rows(cotangent)
+    x_pieces = grid.gather_rows(tokens, width // grid.parts)
+    dy_pieces = grid.gather_rows(cotangent, lent_columns(width, grid.parts, 2))
 
     ids = grid.ids()
     routes = meta_all[:, :top].astype(jnp.int32)
@@ -459,7 +496,7 @@
         tok,
     )
     down_all = grid.gather(down)
-    pre, upg, send, score, dy_window = forward_call(
+    pre, upg, pre_rows, upg_rows, score, dy_window = forward_call(
         down_kernel,
         at,
         [wd],
@@ -468,7 +505,8 @@
         [
             square_b,
             square_b,
-            jax.ShapeDtypeStruct((rows, 2 * hidden), BF),
+            jax.ShapeDtypeStruct((rows, hidden), BF),
+            jax.ShapeDtypeStruct((rows, hidden), BF),
             jax.ShapeDtypeStruct((all_tok, LANES), BF),
         ],
         (all_tok, hidden),
@@ -478,14 +516,19 @@
         grid.parts,
         tok,
     )
-    send_all = grid.gather(send)
-
-    parts = input_parts(grid, pre, upg, score, wg, wu)
-    kept = parts[0].astype(F32)
-    for k in range(1, nc):
-        kept = kept + grid.shift(parts[k], 2, -k).astype(F32)
-    kept = kept.astype(BF)
-    terms = [kept[0]] + [grid.tensor_shift(kept[k], -k) for k in range(1, grid.parts)]
+    pre_all = grid.gather(pre_rows)
+    upg_all = grid.gather(upg_rows)
+
+    terms = {}
+    for h in [*range(1, grid.parts), 0]:
+        share = input_part(grid, h, pre, upg, score, wg, wu)
+        total = share[0].astype(F32)
+        for k in range(1, nc):
+            total = total + grid.shift(share[k], 2, -k).astype(F32)
+        terms[h] = total.astype(BF)
+        if h > 0:
+            terms[h] = grid.tensor_shift(terms[h], -h)
+    terms = [terms[h] for h in range(grid.parts)]
     if grid.parts > 2:
         terms = list(jnp.roll(jnp.stack(terms)[::-1], grid.part + 1, axis=0))
     total = terms[0].astype(F32)
@@ -504,7 +547,7 @@
     own_routes = route_slots[:, :, None] == lane[None, None, :]
     gate_grads = jnp.sum(jnp.where(own_routes, last[:, None, part:], 0.0), axis=2).astype(BF)
 
-    x_window, dy_window = after(x_window, parts), after(dy_window, parts)
+    x_window, dy_window = after(x_window, share), after(dy_window, share)
     x_t = lax.dynamic_slice_in_dim(x_window, first - start, depth, 1).T
     dy_t = lax.dynamic_slice_in_dim(dy_window, first - start, depth, 1).T
     x_pick, dy_pick = picked(place, x_t, dy_t, rows)
@@ -518,7 +561,8 @@
     )
     table = jnp.concatenate([spot, replica_owner]).astype(jnp.int32)
     out = expert_sums(table, dy_pick, down_all, 2, 1, 3, None, replicas)
-    out = expert_sums(table, x_pick, send_all, 0, 2, 3, out, replicas)
+    out = expert_sums(table, x_pick, pre_all, 0, 1, 3, out, replicas)
+    out = expert_sums(table, x_pick, upg_all, 1, 1, 3, out, replicas)
     return input_grads, gate_grads, jnp.transpose(out, (0, 2, 1, 3))
 
 

time: 425 us -> 466 us (1.096)
  waiting for transfers between devices: 227 us -> 247 us
  starting transfers between devices: 66.9 us -> 74.9 us
  other arithmetic: 5.25 us -> 12.7 us
    ppermute x62 -> x82, waiting for transfers between devices: 206 us -> 221 us  [shift(): return lax.ppermute(value, 'expert', pairs)]
    concatenate x0 -> x8, other arithmetic: none -> 7.52 us  [gather_rows(): group = jnp.concatenate([pieces[k] for k in range(1, na)])]
    ppermute x5 -> x13, waiting for transfers between devices: 20.6 us -> 26.1 us  [tensor_shift(): lax.ppermute(value, 'tensor', [((i + step) % n, i) for i in range(n)])]
    ppermute x5 -> x13, starting transfers between devices: 7.52 us -> 12.1 us  [tensor_shift(): lax.ppermute(value, 'tensor', [((i + step) % n, i) for i in range(n)])]
    ppermute x62 -> x82, starting transfers between devices: 59.3 us -> 62.8 us  [shift(): return lax.ppermute(value, 'expert', pairs)]
    pallas_call x1 -> x2, Pallas kernels: 18.1 us -> 20.2 us  [input_part(): pl.pallas_call(input_kernel, grid_spec=pltpu.PrefetchScalarGridSpec(num_s...]
    pallas_call x2 -> x3, Pallas kernels: 34.8 us -> 36.8 us  [expert_sums(): pl.pallas_call(lambda *refs: expert_kernel(slots, replicas, *refs), grid_...]
  transfers between devices with their start and end apart: 67 -> 95, of which waited for: 24 -> 44; matrix products, arithmetic and copies ran while one was open for 4% -> 5% of each run, Pallas kernels for 16% -> 17%
where the time goes in v2:
time: 466 us; the launch traced here: 462 us
  waiting for transfers between devices  247 us (53%)
  Pallas kernels  104 us (22%)
  starting transfers between devices  74.9 us (16%)
  local copies, waits for them, and re-layouts  20.6 us (4%)
  other arithmetic  12.7 us (3%)
    ppermute x82, waiting for transfers between devices, shift(): return lax.ppermute(value, 'expert', pairs)  221 us
    ppermute x82, starting transfers between devices, shift(): return lax.ppermute(value, 'expert', pairs)  62.8 us
    pallas_call x3, Pallas kernels, expert_sums(): pl.pallas_call(lambda *refs: expert_kernel(slots, replicas, *refs), grid_...  36.8 us
    pallas_call x2, Pallas kernels, forward_call(): pl.pallas_call(body, grid_spec=pltpu.PrefetchScalarGridSpec(num_scalar_pr...  34 us
    ppermute x13, waiting for transfers between devices, tensor_shift(): lax.ppermute(value, 'tensor', [((i + step) % n, i) for i in range(n)])  26.1 us
    pallas_call x2, Pallas kernels, input_part(): pl.pallas_call(input_kernel, grid_spec=pltpu.PrefetchScalarGridSpec(num_s...  20.2 us
    pallas_call x1, Pallas kernels, picked(): pl.pallas_call(pick_kernel, grid=(slots,), in_specs=[pl.BlockSpec((1, 1,...  13.2 us
    ppermute x13, starting transfers between devices, tensor_shift(): lax.ppermute(value, 'tensor', [((i + step) % n, i) for i in range(n)])  12.1 us
  transfers between devices with their start and end apart: 95, of which 44 were waited for; matrix products, arithmetic and copies ran while one was open for 5% of the time, Pallas kernels for 17%

profile of v2, /device:TPU:16, one launch (start us, length us, event | category | flops | bytes accessed | tf_op | source)
XLA Modules:
  0.0 461.8 jit_solution(3855374943721341980)
XLA Ops:
  14.7 9.9 %collective-permute-done.3 = bf16[4,32,128]{2,1,0:T(8,128)(2,1)S(1)} collective-permute-done((bf16[4,32,128]{2,1,0:T(8,128)(2,1)S(1)}, bf16[4,32,128]{2,1,0:T(8,128)(2,1)S(1)}, u32[]{:S(2)}, u32[]{:S(2)}) %collective-permute-start.3) | collective-permute-done | bytes 32800 | tf_op jit(solution)/shard_map/ppermute | solution.py:54
  31.7 18.2 %collective-permute-done.25.refs_8_ = bf16[32,5120]{1,0:T(8,128)(2,1)S(1)} collective-permute-done((bf16[32,5120]{1,0:T(8,128)(2,1)S(1)}, bf16[32,5120]{1,0:T(8,128)(2,1)S(1)}, u32[]{:S(2)}, u32[]{:S(2)}) %collective-permute-start.25) | collective-permute-done | bytes 327712 | tf_op jit(solution)/shard_map/ppermute | solution.py:54
  88.4 7.0 %collective-permute-done.33.refs_16_ = bf16[32,5120]{1,0:T(8,128)(2,1)S(1)} collective-permute-done((bf16[32,5120]{1,0:T(8,128)(2,1)S(1)}, bf16[32,5120]{1,0:T(8,128)(2,1)S(1)}, u32[]{:S(2)}, u32[]{:S(2)}) %collective-permute-start.33) | collective-permute-done | bytes 327712 | tf_op jit(solution)/shard_map/ppermute | solution.py:54
  134.4 18.7 %shard_map.103 = (f32[512,512]{1,0:T(8,128)}, f32[512,512]{1,0:T(8,128)}, bf16[384,512]{1,0:T(8,128)(2,1)}, bf16[512,640]{1,0:T(8,128)(2,1)}) custom-call(s32[3]{0:T(128)} %pad_add_fusion.refs_0_, bf16[7168,512]{1,0:T(8,128)(2,1)} %bitcast.64, bf16[7168,512]{1,0:T(8,128)(2,1)} %bitcast.67, f32[512,1]{1,0:T(8,128)} %copy.49.refs_3_.refs_2_, ...), custom_call_target="tpu_custom_call" | custom-call | tf_op jit(solution)/shard_map/pallas_call | solution.py:261
  154.4 15.3 %shard_map.104 = (bf16[512,512]{1,0:T(8,128)(2,1)}, bf16[512,512]{1,0:T(8,128)(2,1)}, bf16[384,512]{1,0:T(8,128)(2,1)}, bf16[384,512]{1,0:T(8,128)(2,1)}, bf16[5...) custom-call(s32[3]{0:T(128)} %pad_add_fusion.refs_0_, bf16[7168,512]{1,0:T(8,128)(2,1)} %bitcast.70, ...), custom_call_target="tpu_custom_call" | custom-call | tf_op jit(solution)/shard_map/pallas_call | solution.py:261
  169.7 10.1 %shard_map.106 = bf16[2,256,3712]{2,1,0:T(8,128)(2,1)} custom-call(s32[1]{0:T(128)} %bitcast.28.index_ref, bf16[512,512]{1,0:T(8,128)(2,1)} %get-tuple-element.19.pre_ref, bf16[512,512]{1,0:T(8,128)(2,1)} %get-tuple-element.20.up_ref, bf16[512,128]{1,0:T(8,128)(2,1)} %get-tuple-element.21.score_ref, bf16[7168,512]{1,0:T(8,128)(2,1)} %bitcast.65, ...), custom_call_target="tpu_custom_call" | custom-call | tf_op jit(solution)/shard_map/pallas_call | solution.py:309
  190.1 10.1 %shard_map.105 = bf16[2,256,3712]{2,1,0:T(8,128)(2,1)} custom-call(s32[1]{0:T(128)} %bitcast.index_ref, bf16[512,512]{1,0:T(8,128)(2,1)} %get-tuple-element.19.pre_ref, bf16[512,512]{1,0:T(8,128)(2,1)} %get-tuple-element.20.up_ref, bf16[512,128]{1,0:T(8,128)(2,1)} %get-tuple-element.21.score_ref, bf16[7168,512]{1,0:T(8,128)(2,1)} %bitcast.66, ...), custom_call_target="tpu_custom_call" | custom-call | tf_op jit(solution)/shard_map/pallas_call | solution.py:309
  203.4 13.9 %collective-permute-done.81.refs_4_ = bf16[384,512]{1,0:T(8,128)(2,1)S(1)} collective-permute-done((bf16[384,512]{1,0:T(8,128)(2,1)S(1)}, bf16[384,512]{1,0:T(8,128)(2,1)S(1)}, u32[]{:S(2)}, u32[]{:S(2)}) %collective-permute-start.81) | collective-permute-done | bytes 393248 | tf_op jit(solution)/shard_map/ppermute | solution.py:54
  223.6 9.7 %collective-permute-done.65.refs_3_ = bf16[384,512]{1,0:T(8,128)(2,1)S(1)} collective-permute-done((bf16[384,512]{1,0:T(8,128)(2,1)S(1)}, bf16[384,512]{1,0:T(8,128)(2,1)S(1)}, u32[]{:S(2)}, u32[]{:S(2)}) %collective-permute-start.65) | collective-permute-done | bytes 393248 | tf_op jit(solution)/shard_map/ppermute | solution.py:54
  234.8 20.6 %collective-permute-done.66.refs_4_ = bf16[384,512]{1,0:T(8,128)(2,1)S(1)} collective-permute-done((bf16[384,512]{1,0:T(8,128)(2,1)S(1)}, bf16[384,512]{1,0:T(8,128)(2,1)S(1)}, u32[]{:S(2)}, u32[]{:S(2)}) %collective-permute-start.66) | collective-permute-done | bytes 393248 | tf_op jit(solution)/shard_map/ppermute | solution.py:54
  260.9 6.7 %collective-permute-done.50.refs_3_ = bf16[384,512]{1,0:T(8,128)(2,1)} collective-permute-done((bf16[384,512]{1,0:T(8,128)(2,1)S(1)}, bf16[384,512]{1,0:T(8,128)(2,1)}, u32[]{:S(2)}, u32[]{:S(2)}) %collective-permute-start.50) | collective-permute-done | bytes 393248 | tf_op jit(solution)/shard_map/ppermute | solution.py:54
  269.1 21.0 %collective-permute-done.51.refs_4_ = bf16[384,512]{1,0:T(8,128)(2,1)} collective-permute-done((bf16[384,512]{1,0:T(8,128)(2,1)S(1)}, bf16[384,512]{1,0:T(8,128)(2,1)}, u32[]{:S(2)}, u32[]{:S(2)}) %collective-permute-start.51) | collective-permute-done | bytes 393248 | tf_op jit(solution)/shard_map/ppermute | solution.py:54
  296.1 9.9 %collective-permute-done.84.refs_7_ = bf16[384,512]{1,0:T(8,128)(2,1)S(1)} collective-permute-done((bf16[384,512]{1,0:T(8,128)(2,1)S(1)}, bf16[384,512]{1,0:T(8,128)(2,1)S(1)}, u32[]{:S(2)}, u32[]{:S(2)}) %collective-permute-start.84) | collective-permute-done | bytes 393248 | tf_op jit(solution)/shard_map/ppermute | solution.py:54
  306.0 7.5 %collective-permute-done.85.refs_8_ = bf16[384,512]{1,0:T(8,128)(2,1)S(1)} collective-permute-done((bf16[384,512]{1,0:T(8,128)(2,1)S(1)}, bf16[384,512]{1,0:T(8,128)(2,1)S(1)}, u32[]{:S(2)}, u32[]{:S(2)}) %collective-permute-start.85) | collective-permute-done | bytes 393248 | tf_op jit(solution)/shard_map/ppermute | solution.py:54
  316.5 7.4 %collective-permute-done.86.refs_9_ = bf16[384,512]{1,0:T(8,128)(2,1)S(1)} collective-permute-done((bf16[384,512]{1,0:T(8,128)(2,1)S(1)}, bf16[384,512]{1,0:T(8,128)(2,1)S(1)}, u32[]{:S(2)}, u32[]{:S(2)}) %collective-permute-start.86) | collective-permute-done | bytes 393248 | tf_op jit(solution)/shard_map/ppermute | solution.py:54
  327.9 7.9 %collective-permute-done.69.refs_7_ = bf16[384,512]{1,0:T(8,128)(2,1)S(1)} collective-permute-done((bf16[384,512]{1,0:T(8,128)(2,1)S(1)}, bf16[384,512]{1,0:T(8,128)(2,1)S(1)}, u32[]{:S(2)}, u32[]{:S(2)}) %collective-permute-start.69) | collective-permute-done | bytes 393248 | tf_op jit(solution)/shard_map/ppermute | solution.py:54
  338.1 6.1 %collective-permute-done.70.refs_8_ = bf16[384,512]{1,0:T(8,128)(2,1)S(1)} collective-permute-done((bf16[384,512]{1,0:T(8,128)(2,1)S(1)}, bf16[384,512]{1,0:T(8,128)(2,1)S(1)}, u32[]{:S(2)}, u32[]{:S(2)}) %collective-permute-start.70) | collective-permute-done | bytes 393248 | tf_op jit(solution)/shard_map/ppermute | solution.py:54
  344.2 8.4 %collective-permute-done.71.refs_9_ = bf16[384,512]{1,0:T(8,128)(2,1)S(1)} collective-permute-done((bf16[384,512]{1,0:T(8,128)(2,1)S(1)}, bf16[384,512]{1,0:T(8,128)(2,1)S(1)}, u32[]{:S(2)}, u32[]{:S(2)}) %collective-permute-start.71) | collective-permute-done | bytes 393248 | tf_op jit(solution)/shard_map/ppermute | solution.py:54
  356.4 25.0 %collective-permute-done.54.refs_7_ = bf16[384,512]{1,0:T(8,128)(2,1)S(1)} collective-permute-done((bf16[384,512]{1,0:T(8,128)(2,1)}, bf16[384,512]{1,0:T(8,128)(2,1)S(1)}, u32[]{:S(2)}, u32[]{:S(2)}) %collective-permute-start.54) | collective-permute-done | bytes 393248 | tf_op jit(solution)/shard_map/ppermute | solution.py:54
  381.5 8.5 %collective-permute-done.55.refs_8_ = bf16[384,512]{1,0:T(8,128)(2,1)} collective-permute-done((bf16[384,512]{1,0:T(8,128)(2,1)}, bf16[384,512]{1,0:T(8,128)(2,1)}, u32[]{:S(2)}, u32[]{:S(2)}) %collective-permute-start.55) | collective-permute-done | bytes 393248 | tf_op jit(solution)/shard_map/ppermute | solution.py:54
  408.8 13.2 %shard_map.107 = (bf16[16,448,384]{2,1,0:T(8,128)(2,1)}, bf16[16,448,384]{2,1,0:T(8,128)(2,1)}) custom-call(s32[16,1,512]{2,1,0:T(1,128)} %reshape.196.place_ref, bf16[448,512]{1,0:T(8,128)(2,1)} %get-tuple-element.58.x_ref, bf16[448,512]{1,0:T(8,128)(2,1)} %get-tuple-element.57.dy_ref), custom_call_target="tpu_custom_call" | custom-call | tf_op jit(solution)/shard_map/pallas_call | solution.py:338
  422.0 12.3 %shard_map.108.refs_18_ = bf16[14,3,448,512]{3,2,1,0:T(8,128)(2,1)} custom-call(s32[18]{0:T(128)} %pad_add_fusion.1.refs_0_, bf16[16,448,384]{2,1,0:T(8,128)(2,1)} %get-tuple-element.29.refs_1_, bf16[384,512]{1,0:T(8,128)(2,1)} %get-tuple-element.30.refs_2_, bf16[384,512]{1,0:T(8,128)(2,1)} %copy-done.39, bf16[384,512]{1,0:T(8,128)(2,1)} %copy-done.40, ...), custom_call_target="tpu_custom_call" | custom-call | tf_op jit(solution)/shard_map/pallas_call | solution.py:415
  434.3 12.3 %shard_map.109.refs_18_ = bf16[14,3,448,512]{3,2,1,0:T(8,128)(2,1)} custom-call(s32[18]{0:T(128)} %pad_add_fusion.1.refs_0_, bf16[16,448,384]{2,1,0:T(8,128)(2,1)} %get-tuple-element.26.refs_1_, bf16[384,512]{1,0:T(8,128)(2,1)} %get-tuple-element.28.refs_2_, bf16[384,512]{1,0:T(8,128)(2,1)} %copy-done.43, ...), custom_call_target="tpu_custom_call", output_to_operand_aliasing={{}: (18, {})} | custom-call | tf_op jit(solution)/shard_map/pallas_call | solution.py:415
  446.6 12.3 %shard_map.110 = bf16[14,3,448,512]{3,2,1,0:T(8,128)(2,1)} custom-call(s32[18]{0:T(128)} %pad_add_fusion.1.refs_0_, bf16[16,448,384]{2,1,0:T(8,128)(2,1)} %get-tuple-element.26.refs_1_, bf16[384,512]{1,0:T(8,128)(2,1)} %get-tuple-element.27.refs_2_, bf16[384,512]{1,0:T(8,128)(2,1)} %collective-permute-done.50.refs_3_, ...), custom_call_target="tpu_custom_call", output_to_operand_aliasing={{}: (18, {})} | custom-call | tf_op jit(solution)/shard_map/pallas_call | solution.py:415
  (398 shorter events, 168.0 us)
Async XLA Ops:
  12.5 83.7 %collective-permute-start.5 = (bf16[32,7168]{1,0:T(8,128)(2,1)}, bf16[32,7168]{1,0:T(8,128)(2,1)S(1)}, u32[]{:S(2)}, u32[]{:S(2)}) collective-permute-start(bf16[32,7168]{1,0:T(8,128)(2,1)} %refs_5_.1), channel_id=1, source_target_pairs={{4,0},{6,2},{0,4},{2,6},{12,8},{14,10},{8,12},{10,14},{20,16},{22,... | collective-permute-start | bytes 1376264 | tf_op jit(solution)/shard_map/ppermute | solution.py:54
  26.0 71.7 %collective-permute-start.18 = (bf16[32,7168]{1,0:T(8,128)(2,1)S(1)}, bf16[32,7168]{1,0:T(8,128)(2,1)}, u32[]{:S(2)}, u32[]{:S(2)}) collective-permute-start(bf16[32,7168]{1,0:T(8,128)(2,1)S(1)} %copy-done.9), channel_id=1, source_target_pairs={{2,0},{0,2},{6,4},{4,6},{10,8},{8,10},{14,12},{12,14},{18,16},{16,... | collective-permute-start | bytes 1376264 | tf_op jit(solution)/shard_map/ppermute | solution.py:54
  123.2 29.8 %collective-permute-start.39 = (bf16[96,5120]{1,0:T(8,128)(2,1)}, bf16[96,5120]{1,0:T(8,128)(2,1)S(1)}, u32[]{:S(2)}, u32[]{:S(2)}) collective-permute-start(bf16[96,5120]{1,0:T(8,128)(2,1)} %pad_maximum_fusion), channel_id=1, source_target_pairs={{2,0},{0,2},{6,4},{4,6},{10,8},{8,10},{14,12},{12,14},{18,16},{16,... | collective-permute-start | bytes 2949128 | tf_op jit(solution)/shard_map/ppermute | solution.py:54
  124.8 28.3 %collective-permute-start.41 = (bf16[96,5120]{1,0:T(8,128)(2,1)S(1)}, bf16[96,5120]{1,0:T(8,128)(2,1)S(1)}, u32[]{:S(2)}, u32[]{:S(2)}) collective-permute-start(bf16[96,5120]{1,0:T(8,128)(2,1)S(1)} %pad_maximum_fusion.1), channel_id=1, source_target_pairs={{2,0},{0,2},{6,4},{4,6},{10,8},{8,10},{14,12},{12,14},{18,16},{16,... | collective-permute-start | bytes 2949128 | tf_op jit(solution)/shard_map/ppermute | solution.py:54
  183.2 34.2 %collective-permute-start.81 = (bf16[384,512]{1,0:T(8,128)(2,1)S(1)}, bf16[384,512]{1,0:T(8,128)(2,1)S(1)}, u32[]{:S(2)}, u32[]{:S(2)}) collective-permute-start(bf16[384,512]{1,0:T(8,128)(2,1)S(1)} %copy-done.36), channel_id=1, source_target_pairs={{16,0},{18,2},{20,4},{22,6},{24,8},{26,10},{28,12},{30,14},{0,16},... | collective-permute-start | bytes 1179656 | tf_op jit(solution)/shard_map/ppermute | solution.py:54
  186.6 34.7 %collective-permute-start.82 = (bf16[384,512]{1,0:T(8,128)(2,1)S(1)}, bf16[384,512]{1,0:T(8,128)(2,1)S(1)}, u32[]{:S(2)}, u32[]{:S(2)}) collective-permute-start(bf16[384,512]{1,0:T(8,128)(2,1)S(1)} %copy-done.36), channel_id=1, source_target_pairs={{24,0},{26,2},{28,4},{30,6},{0,8},{2,10},{4,12},{6,14},{8,16},{10,... | collective-permute-start | bytes 1179656 | tf_op jit(solution)/shard_map/ppermute | solution.py:54
  188.6 32.7 %collective-permute-start.83 = (bf16[384,512]{1,0:T(8,128)(2,1)S(1)}, bf16[384,512]{1,0:T(8,128)(2,1)}, u32[]{:S(2)}, u32[]{:S(2)}) collective-permute-start(bf16[384,512]{1,0:T(8,128)(2,1)S(1)} %copy-done.36), channel_id=1, source_target_pairs={{4,0},{6,2},{0,4},{2,6},{12,8},{14,10},{8,12},{10,14},{20,16},{22,... | collective-permute-start | bytes 1179656 | tf_op jit(solution)/shard_map/ppermute | solution.py:54
  203.4 111.7 %collective-permute-start.43 = (bf16[256,3712]{1,0:T(8,128)(2,1)S(1)}, bf16[256,3712]{1,0:T(8,128)(2,1)S(1)}, u32[]{:S(2)}, u32[]{:S(2)}) collective-permute-start(bf16[256,3712]{1,0:T(8,128)(2,1)S(1)} %slice_bitcast_fusion.2), channel_id=1, source_target_pairs={{2,0},{0,2},{6,4},{4,6},{10,8},{8,10},{14,12},{12,14},{18,16},{16,... | collective-permute-start | bytes 5701640 | tf_op jit(solution)/shard_map/ppermute | solution.py:54
  217.4 97.7 %collective-permute-start.45 = (bf16[256,3712]{1,0:T(8,128)(2,1)S(1)}, bf16[256,3712]{1,0:T(8,128)(2,1)S(1)}, u32[]{:S(2)}, u32[]{:S(2)}) collective-permute-start(bf16[256,3712]{1,0:T(8,128)(2,1)S(1)} %fusion), channel_id=1, source_target_pairs={{1,0},{0,1},{3,2},{2,3},{5,4},{4,5},{7,6},{6,7},{9,8},{8,9},{11,10... | collective-permute-start | bytes 5701640 | tf_op jit(solution)/shard_map/ppermute | solution.py:58
  221.3 34.1 %collective-permute-start.66 = (bf16[384,512]{1,0:T(8,128)(2,1)S(1)}, bf16[384,512]{1,0:T(8,128)(2,1)S(1)}, u32[]{:S(2)}, u32[]{:S(2)}) collective-permute-start(bf16[384,512]{1,0:T(8,128)(2,1)S(1)} %copy-done.38), channel_id=1, source_target_pairs={{16,0},{18,2},{20,4},{22,6},{24,8},{26,10},{28,12},{30,14},{0,16},... | collective-permute-start | bytes 1179656 | tf_op jit(solution)/shard_map/ppermute | solution.py:54
  221.4 34.0 %collective-permute-start.67 = (bf16[384,512]{1,0:T(8,128)(2,1)S(1)}, bf16[384,512]{1,0:T(8,128)(2,1)S(1)}, u32[]{:S(2)}, u32[]{:S(2)}) collective-permute-start(bf16[384,512]{1,0:T(8,128)(2,1)S(1)} %copy-done.38), channel_id=1, source_target_pairs={{24,0},{26,2},{28,4},{30,6},{0,8},{2,10},{4,12},{6,14},{8,16},{10,... | collective-permute-start | bytes 1179656 | tf_op jit(solution)/shard_map/ppermute | solution.py:54
  255.5 34.6 %collective-permute-start.51 = (bf16[384,512]{1,0:T(8,128)(2,1)S(1)}, bf16[384,512]{1,0:T(8,128)(2,1)}, u32[]{:S(2)}, u32[]{:S(2)}) collective-permute-start(bf16[384,512]{1,0:T(8,128)(2,1)S(1)} %copy-done.37), channel_id=1, source_target_pairs={{16,0},{18,2},{20,4},{22,6},{24,8},{26,10},{28,12},{30,14},{0,16},... | collective-permute-start | bytes 1179656 | tf_op jit(solution)/shard_map/ppermute | solution.py:54
  259.0 35.1 %collective-permute-start.52 = (bf16[384,512]{1,0:T(8,128)(2,1)S(1)}, bf16[384,512]{1,0:T(8,128)(2,1)}, u32[]{:S(2)}, u32[]{:S(2)}) collective-permute-start(bf16[384,512]{1,0:T(8,128)(2,1)S(1)} %copy-done.37), channel_id=1, source_target_pairs={{24,0},{26,2},{28,4},{30,6},{0,8},{2,10},{4,12},{6,14},{8,16},{10,... | collective-permute-start | bytes 1179656 | tf_op jit(solution)/shard_map/ppermute | solution.py:54
  296.1 29.2 %collective-permute-start.88 = (bf16[384,512]{1,0:T(8,128)(2,1)S(1)}, bf16[384,512]{1,0:T(8,128)(2,1)S(1)}, u32[]{:S(2)}, u32[]{:S(2)}) collective-permute-start(bf16[384,512]{1,0:T(8,128)(2,1)S(1)} %collective-permute-done.80.refs_3_), channel_id=1, source_target_pairs={{2,0},{0,2},{6,4},{4,6},{10,8},{8,10},{14,12},{12,14},{18,16},{16,... | collective-permute-start | bytes 1179656 | tf_op jit(solution)/shard_map/ppermute | solution.py:54
  336.6 60.2 %collective-permute-start.46 = (bf16[4,32,3712]{2,1,0:T(8,128)(2,1)S(1)}, bf16[4,32,3712]{2,1,0:T(8,128)(2,1)S(1)}, u32[]{:S(2)}, u32[]{:S(2)}) collective-permute-start(bf16[4,32,3712]{2,1,0:T(8,128)(2,1)S(1)} %bitcast.72), channel_id=1, source_target_pairs={{4,0},{6,2},{0,4},{2,6},{12,8},{14,10},{8,12},{10,14},{20,16},{22,... | collective-permute-start | bytes 2850824 | tf_op jit(solution)/shard_map/ppermute | solution.py:54
  352.7 28.8 %collective-permute-start.54 = (bf16[384,512]{1,0:T(8,128)(2,1)}, bf16[384,512]{1,0:T(8,128)(2,1)S(1)}, u32[]{:S(2)}, u32[]{:S(2)}) collective-permute-start(bf16[384,512]{1,0:T(8,128)(2,1)} %collective-permute-done.50.refs_3_), channel_id=1, source_target_pairs={{4,0},{6,2},{0,4},{2,6},{12,8},{14,10},{8,12},{10,14},{20,16},{22,... | collective-permute-start | bytes 1179656 | tf_op jit(solution)/shard_map/ppermute | solution.py:54
  354.3 35.7 %collective-permute-start.55 = (bf16[384,512]{1,0:T(8,128)(2,1)}, bf16[384,512]{1,0:T(8,128)(2,1)}, u32[]{:S(2)}, u32[]{:S(2)}) collective-permute-start(bf16[384,512]{1,0:T(8,128)(2,1)} %collective-permute-done.51.refs_4_), channel_id=1, source_target_pairs={{4,0},{6,2},{0,4},{2,6},{12,8},{14,10},{8,12},{10,14},{20,16},{22,... | collective-permute-start | bytes 1179656 | tf_op jit(solution)/shard_map/ppermute | solution.py:54
  354.8 41.0 %collective-permute-start.56 = (bf16[384,512]{1,0:T(8,128)(2,1)}, bf16[384,512]{1,0:T(8,128)(2,1)}, u32[]{:S(2)}, u32[]{:S(2)}) collective-permute-start(bf16[384,512]{1,0:T(8,128)(2,1)} %collective-permute-done.52.refs_5_), channel_id=1, source_target_pairs={{4,0},{6,2},{0,4},{2,6},{12,8},{14,10},{8,12},{10,14},{20,16},{22,... | collective-permute-start | bytes 1179656 | tf_op jit(solution)/shard_map/ppermute | solution.py:54
  356.3 39.5 %collective-permute-start.58 = (bf16[384,512]{1,0:T(8,128)(2,1)}, bf16[384,512]{1,0:T(8,128)(2,1)S(1)}, u32[]{:S(2)}, u32[]{:S(2)}) collective-permute-start(bf16[384,512]{1,0:T(8,128)(2,1)} %collective-permute-done.50.refs_3_), channel_id=1, source_target_pairs={{2,0},{0,2},{6,4},{4,6},{10,8},{8,10},{14,12},{12,14},{18,16},{16,... | collective-permute-start | bytes 1179656 | tf_op jit(solution)/shard_map/ppermute | solution.py:54
  399.4 47.2 %collective-permute-start.63 = (bf16[384,512]{1,0:T(8,128)(2,1)}, bf16[384,512]{1,0:T(8,128)(2,1)}, u32[]{:S(2)}, u32[]{:S(2)}) collective-permute-start(bf16[384,512]{1,0:T(8,128)(2,1)} %collective-permute-done.55.refs_8_), channel_id=1, source_target_pairs={{2,0},{0,2},{6,4},{4,6},{10,8},{8,10},{14,12},{12,14},{18,16},{16,... | collective-permute-start | bytes 1179656 | tf_op jit(solution)/shard_map/ppermute | solution.py:54
  400.0 46.7 %collective-permute-start.64 = (bf16[384,512]{1,0:T(8,128)(2,1)}, bf16[384,512]{1,0:T(8,128)(2,1)}, u32[]{:S(2)}, u32[]{:S(2)}) collective-permute-start(bf16[384,512]{1,0:T(8,128)(2,1)} %collective-permute-done.56.refs_9_), channel_id=1, source_target_pairs={{2,0},{0,2},{6,4},{4,6},{10,8},{8,10},{14,12},{12,14},{18,16},{16,... | collective-permute-start | bytes 1179656 | tf_op jit(solution)/shard_map/ppermute | solution.py:54
  401.0 57.9 %collective-permute-start.47 = (bf16[32,3712]{1,0:T(8,128)(2,1)}, bf16[32,3712]{1,0:T(8,128)(2,1)}, u32[]{:S(2)}, u32[]{:S(2)}) collective-permute-start(bf16[32,3712]{1,0:T(8,128)(2,1)} %get-tuple-element.44), channel_id=1, source_target_pairs={{24,0},{26,2},{28,4},{30,6},{0,8},{2,10},{4,12},{6,14},{8,16},{10,... | collective-permute-start | bytes 712712 | tf_op jit(solution)/shard_map/ppermute | solution.py:54
  401.1 57.8 %collective-permute-start.48 = (bf16[32,3712]{1,0:T(8,128)(2,1)}, bf16[32,3712]{1,0:T(8,128)(2,1)}, u32[]{:S(2)}, u32[]{:S(2)}) collective-permute-start(bf16[32,3712]{1,0:T(8,128)(2,1)} %get-tuple-element.46), channel_id=1, source_target_pairs={{16,0},{18,2},{20,4},{22,6},{24,8},{26,10},{28,12},{30,14},{0,16},... | collective-permute-start | bytes 712712 | tf_op jit(solution)/shard_map/ppermute | solution.py:54
  401.9 57.0 %collective-permute-start.49 = (bf16[32,3712]{1,0:T(8,128)(2,1)}, bf16[32,3712]{1,0:T(8,128)(2,1)}, u32[]{:S(2)}, u32[]{:S(2)}) collective-permute-start(bf16[32,3712]{1,0:T(8,128)(2,1)} %get-tuple-element.45), channel_id=1, source_target_pairs={{8,0},{10,2},{12,4},{14,6},{16,8},{18,10},{20,12},{22,14},{24,16},... | collective-permute-start | bytes 712712 | tf_op jit(solution)/shard_map/ppermute | solution.py:54
  (152 other events, 2985.3 us)

commit v3 on v2

v3 whole, which is shorter than its diff:
```python
import jax
import jax.numpy as jnp
from jax import lax
from jax.experimental import pallas as pl
from jax.experimental.pallas import tpu as pltpu
from jax.sharding import PartitionSpec as P


BF = jnp.bfloat16
F32 = jnp.float32
LANES = 128
ANY = pl.BlockSpec(memory_space=pl.ANY)


def split_axis(total):
    cores = 2
    chips = total // cores
    b = 1
    while b * b * 4 <= chips:
        b *= 2
    return chips // b, b, cores


def block_of(size, most):
    return max(n for n in range(LANES, most + 1, LANES) if size % n == 0)


def nearest_steps(size):
    return sorted(range(1, size), key=lambda k: (min(k, size - k), k))


class Grid:
    def __init__(self):
        self.total = lax.axis_size("expert")
        self.sizes = split_axis(self.total)
        self.me = lax.axis_index("expert")
        _, nb, nc = self.sizes
        self.pos = (self.me // (nb * nc), (self.me // nc) % nb, self.me % nc)
        self.parts = lax.axis_size("tensor")
        self.part = lax.axis_index("tensor")

    def flat(self, a, b, c):
        _, nb, nc = self.sizes
        return (a * nb + b) * nc + c

    def shift(self, value, axis, step):
        pairs = []
        for a in range(self.sizes[0]):
            for b in range(self.sizes[1]):
                for c in range(self.sizes[2]):
                    src = [a, b, c]
                    src[axis] = (src[axis] + step) % self.sizes[axis]
                    pairs.append((self.flat(*src), self.flat(a, b, c)))
        return lax.ppermute(value, "expert", pairs)

    def tensor_shift(self, value, step):
        n = self.parts
        return lax.ppermute(value, "tensor", [((i + step) % n, i) for i in range(n)])

    def ids(self):
        na, nb, nc = self.sizes
        a, b, c = self.pos
        places = [(da, db, dc) for dc in range(nc) for db in range(nb) for da in range(na)]
        return jnp.stack(
            [self.flat((a + da) % na, (b + db) % nb, (c + dc) % nc) for da, db, dc in places]
        ).astype(jnp.int32)

    def gather_small(self, own):
        out = own[None]
        for axis in range(3):
            parts = [out]
            for k in range(1, self.sizes[axis]):
                parts.append(self.shift(out, axis, k))
            out = jnp.concatenate(parts)
        return out

    def nearest(self):
        return nearest_steps(self.sizes[0])

    def gather(self, own, together=False):
        na, nb, nc = self.sizes
        line = {0: own}
        for k in self.nearest():
            line[k] = self.shift(own, 0, k)
        plane = [line[k] for k in range(na)]
        for j in range(1, nb):
            for k in range(na):
                plane.append(self.shift(line[k], 1, j))
        out = list(plane)
        for d in range(1, nc):
            for piece in [jnp.stack(plane)] if together else plane:
                out.append(self.shift(piece, 2, d))
        return out

    def gather_rows(self, own, lent):
        na, nb, nc = self.sizes
        width = own.shape[1]
        keep = width - (self.parts - 1) * lent
        mine = lax.dynamic_slice_in_dim(own, self.part * lent, keep, 1)
        lend = self.part * ((width - lent) // (self.parts - 1) - lent)
        plane = [(0, None, own)]
        swaps = [(0, None, own)]
        line = {}
        for k in self.nearest():
            line[k] = self.shift(mine, 0, k)
        for j in range(1, nb):
            piece = self.shift(own, 1, j)
            plane.append((j * na, None, piece))
            swaps.append((j * na, None, piece))
        for j in range(nb):
            row = dict(line)
            if j > 0:
                for k in self.nearest():
                    row[k] = self.shift(line[k], 1, j)
            kinds = [row]
            for h in range(1, self.parts):
                lent_row = {}
                for k in self.nearest():
                    piece = row[k]
                    if lent < keep:
                        piece = lax.dynamic_slice_in_dim(piece, lend, lent, 1)
                    lent_row[k] = self.tensor_shift(piece, h)
                kinds.append(lent_row)
            for h, pieces in enumerate(kinds):
                plane += [(j * na + k, h, pieces[k]) for k in range(1, na)]
                group = jnp.concatenate([pieces[k] for k in range(1, na)])
                swaps.append((j * na + 1, h, group))
        out = list(plane)
        for d in range(1, nc):
            for block, h, piece in swaps:
                out.append((d * na * nb + block, h, self.shift(piece, 2, d)))
        return out


def row_copies(where, at_ref, piece_refs, whole, sem, parts, tok):
    width = whole.shape[1]
    copies = []
    for n, ((block, h), ref) in enumerate(zip(where, piece_refs)):
        rows = pl.ds(block * tok, ref.shape[0])
        if h is None:
            to = whole.at[rows, :]
        else:
            cols = ref.shape[1]
            step = (width - cols) // (parts - 1)
            start = pl.multiple_of(((at_ref[0] + h) % parts) * step, LANES)
            to = whole.at[rows, pl.ds(start, cols)]
        copies.append(pltpu.make_async_copy(ref, to, sem.at[n]))
    return copies


def products(weight_refs, weights, acc, wsem, copies, whole, window_copy):
    steps, block = weights.shape[1:3]

    def fetch(i, j):
        rows = pl.ds(pl.multiple_of(j * block, LANES), block)
        return pltpu.make_async_copy(weight_refs[i].at[rows, :], weights.at[i, j], wsem.at[i, j])

    ahead = min(2, steps)
    for copy in copies:
        copy.start()
    for j in range(ahead):
        for i in range(len(weight_refs)):
            fetch(i, j).start()
    for copy in copies:
        copy.wait()

    def step(j, carry):
        @pl.when(j + ahead < steps)
        def _():
            for i in range(len(weight_refs)):
                fetch(i, j + ahead).start()

        rows = whole[:, pl.ds(pl.multiple_of(j * block, LANES), block)]
        for i in range(len(weight_refs)):
            fetch(i, j).wait()
            part = jnp.dot(rows, weights[i, j], preferred_element_type=F32)

            @pl.when(j == 0)
            def _(i=i, part=part):
                acc[i] = part

            @pl.when(j > 0)
            def _(i=i, part=part):
                acc[i] += part

        return carry

    lax.fori_loop(0, steps, step, 0)
    window_copy.start()


def pick_matrix(place, rows):
    ids = lax.broadcasted_iota(jnp.int32, (rows, place.shape[1]), 0)
    return jnp.where(ids == place, 1.0, 0.0).astype(BF)


def window_of(width, depth):
    return min(width, -(-(depth + LANES - 1) // LANES) * LANES)


def gate_kernel(where, parts, tok, at_ref, wg_ref, wu_ref, gate_ref, place_ref, *refs):
    count = len(where)
    pieces = refs[:count]
    proj_ref, up_ref, down_ref, window_ref, whole, weights, acc, sem, wsem, osem = refs[count:]
    start = pl.multiple_of(at_ref[1], LANES)
    window = pltpu.make_async_copy(
        whole.at[:, pl.ds(start, window_ref.shape[1])], window_ref, osem.at[0]
    )
    copies = row_copies(where, at_ref, pieces, whole, sem, parts, tok)
    products([wg_ref, wu_ref], weights, acc, wsem, copies, whole, window)
    outs = [
        pltpu.make_async_copy(acc.at[0], proj_ref, osem.at[1]),
        pltpu.make_async_copy(acc.at[1], up_ref, osem.at[2]),
    ]
    for copy in outs:
        copy.start()
    proj = acc[0]
    hidden = proj * jax.nn.sigmoid(proj) * acc[1]
    weighted = (gate_ref[...] * hidden).astype(BF)
    pick = pick_matrix(place_ref[...], down_ref.shape[0])
    down_ref[...] = jnp.dot(pick, weighted, preferred_element_type=F32).astype(BF)
    for copy in [window] + outs:
        copy.wait()


def down_kernel(where, parts, tok, at_ref, wd_ref, gate_ref, place_ref, proj_ref, up_ref, *refs):
    count = len(where)
    pieces = refs[:count]
    pre_ref, upg_ref, pre_rows_ref, upg_rows_ref, score_ref, window_ref = refs[count : count + 6]
    whole, weights, acc, sem, wsem, osem = refs[count + 6 :]
    start = pl.multiple_of(at_ref[1], LANES)
    window = pltpu.make_async_copy(
        whole.at[:, pl.ds(start, window_ref.shape[1])], window_ref, osem.at[0]
    )
    copies = row_copies(where, at_ref, pieces, whole, sem, parts, tok)
    products([wd_ref], weights, acc, wsem, copies, whole, window)
    proj, up, dy_down = proj_ref[...], up_ref[...], acc[0]
    sigma = jax.nn.sigmoid(proj)
    activated = proj * sigma
    score = jnp.sum(activated * up * dy_down, axis=1, keepdims=True)
    lane = lax.broadcasted_iota(jnp.int32, score_ref.shape, 1)
    score_ref[...] = jnp.where(lane == at_ref[2], score, 0.0).astype(BF)
    grad = gate_ref[...] * dy_down
    upg = (grad * activated).astype(BF)
    pre = (grad * up * sigma * (1.0 + proj * (1.0 - sigma))).astype(BF)
    pre_ref[...] = pre
    upg_ref[...] = upg
    pick = pick_matrix(place_ref[...], pre_rows_ref.shape[0])
    pre_rows_ref[...] = jnp.dot(pick, pre, preferred_element_type=F32).astype(BF)
    upg_rows_ref[...] = jnp.dot(pick, upg, preferred_element_type=F32).astype(BF)
    window.wait()


def full(shape):
    return pl.BlockSpec(shape, lambda *_: (0,) * len(shape))


def forward_call(kernel, at, weights, small, pieces, outs, far, width, rows_all, depth, parts, tok):
    where = [(block, h) for block, h, _ in pieces]
    values = [piece for _, _, piece in pieces]
    hidden = weights[0].shape[1]
    block = block_of(width, 1792)
    steps = width // block
    window = window_of(width, depth)
    body = lambda *refs: kernel(where, parts, tok, *refs)
    return pl.pallas_call(
        body,
        grid_spec=pltpu.PrefetchScalarGridSpec(
            num_scalar_prefetch=1,
            grid=(1,),
            in_specs=[ANY for _ in weights]
            + [full(value.shape) for value in small]
            + [ANY for _ in values],
            out_specs=[ANY] * far + [full(out.shape) for out in outs[far:]] + [ANY],
            scratch_shapes=[
                pltpu.VMEM((rows_all, width), BF),
                pltpu.VMEM((len(weights), steps, block, hidden), BF),
                pltpu.VMEM((len(weights), rows_all, hidden), F32),
                pltpu.SemaphoreType.DMA((len(values),)),
                pltpu.SemaphoreType.DMA((len(weights), steps)),
                pltpu.SemaphoreType.DMA((1 + far,)),
            ],
        ),
        out_shape=list(outs) + [jax.ShapeDtypeStruct((rows_all, window), BF)],
    )(at, *weights, *small, *values)


def input_kernel(index_ref, pre_ref, up_ref, score_ref, wg_ref, wu_ref, out_ref, weights, obuf, wsem, osem):
    dims = (((1,), (1,)), ((), ()))
    cores, rows, _ = out_ref.shape
    steps, block = weights.shape[1:3]
    part = steps * block
    wide = score_ref.shape[1]

    def fetch(i, j):
        at = pl.ds(pl.multiple_of(index_ref[0] * part + j * block, LANES), block)
        return pltpu.make_async_copy((wg_ref, wu_ref)[i].at[at, :], weights.at[i, j], wsem.at[i, j])

    def put(c, j):
        cols = pl.ds(pl.multiple_of(j * block, LANES), block)
        return pltpu.make_async_copy(obuf.at[j, c], out_ref.at[c, :, cols], osem.at[c, j])

    def put_score(c):
        return pltpu.make_async_copy(
            score_ref.at[pl.ds(c * rows, rows), :],
            out_ref.at[c, :, pl.ds(part, wide)],
            osem.at[c, steps],
        )

    for j in range(steps):
        for i in range(2):
            fetch(i, j).start()
    for c in range(cores):
        put_score(c).start()

    def step(j, carry):
        fetch(0, j).wait()
        fetch(1, j).wait()
        acc = lax.dot_general(pre_ref[...], weights[0, j], dims, preferred_element_type=F32)
        acc = acc + lax.dot_general(up_ref[...], weights[1, j], dims, preferred_element_type=F32)
        for c in range(cores):
            obuf[j, c] = acc[c * rows : (c + 1) * rows].astype(BF)
            put(c, j).start()
        return carry

    lax.fori_loop(0, steps, step, 0)
    for c in range(cores):
        put_score(c).wait()
        for j in range(steps):
            put(c, j).wait()


def input_part(grid, h, pre, up, score, w_gate, w_up):
    tokens, hidden = pre.shape
    width = w_gate.shape[0]
    parts, cores = grid.parts, grid.sizes[2]
    part = width // parts
    block = block_of(part, 512)
    steps = part // block
    index = ((grid.part + h) % parts).astype(jnp.int32).reshape(1)
    rows = tokens // cores
    return pl.pallas_call(
        input_kernel,
        grid_spec=pltpu.PrefetchScalarGridSpec(
            num_scalar_prefetch=1,
            grid=(1,),
            in_specs=[full((tokens, hidden)), full((tokens, hidden)), full(score.shape), ANY, ANY],
            out_specs=ANY,
            scratch_shapes=[
                pltpu.VMEM((2, steps, block, hidden), BF),
                pltpu.VMEM((steps, cores, rows, block), BF),
                pltpu.SemaphoreType.DMA((2, steps)),
                pltpu.SemaphoreType.DMA((cores, steps + 1)),
            ],
        ),
        out_shape=jax.ShapeDtypeStruct((cores, rows, part + LANES), BF),
    )(index, pre, up, score, w_gate, w_up)


def pick_kernel(place_ref, both_ref, xo_ref, dyo_ref):
    per, depth, rows = xo_ref.shape
    dims = (((1,), (1,)), ((), ()))
    for n in range(per):
        pick = pick_matrix(place_ref[n], rows)
        both = lax.dot_general(both_ref[...], pick, dims, preferred_element_type=F32).astype(BF)
        xo_ref[n] = both[:depth]
        dyo_ref[n] = both[depth:]


def picked(place, x_t, dy_t, rows):
    slots, tokens = place.shape
    depth = x_t.shape[0]
    per = 4 if slots % 4 == 0 else 1
    out = jax.ShapeDtypeStruct((slots, depth, rows), BF)
    both = jnp.concatenate([x_t, dy_t])
    return pl.pallas_call(
        pick_kernel,
        grid=(slots // per,),
        in_specs=[pl.BlockSpec((per, 1, tokens), lambda s: (s, 0, 0)), full(both.shape)],
        out_specs=[pl.BlockSpec((per, depth, rows), lambda s: (s, 0, 0))] * 2,
        out_shape=[out, out],
    )(place.reshape(slots, 1, tokens), both)


def expert_kernel(slots, replicas, first, table_ref, rows_ref, *refs):
    pieces = []
    for ref in refs:
        if len(pieces) < slots:
            pieces += [ref] if len(ref.shape) == 2 else [ref.at[n] for n in range(ref.shape[0])]
    out_ref, left, right, obuf, sem_l, sem_r, osem = refs[-7:]
    experts = slots - replicas

    def left_copy(i):
        return pltpu.make_async_copy(rows_ref.at[i], left.at[i], sem_l.at[i])

    def right_copy(i, at):
        return pltpu.make_async_copy(pieces[i], right.at[at], sem_r.at[at])

    def put(e):
        return pltpu.make_async_copy(obuf.at[e], out_ref.at[e, first], osem.at[e])

    def issue(n, carry):
        i = table_ref[jnp.where(n < replicas, experts + n, n - replicas)]
        left_copy(i).start()
        for k in range(slots):

            @pl.when(i == k)
            def _(k=k):
                right_copy(k, k).start()

        return carry

    lax.fori_loop(0, slots, issue, 0)
    for r in range(replicas):
        i = table_ref[experts + r]
        left_copy(i).wait()
        right_copy(0, i).wait()

    def step(e, carry):
        at = table_ref[e]
        left_copy(at).wait()
        right_copy(0, at).wait()
        owned = table_ref[slots] == e
        for r in range(1, replicas):
            owned = jnp.logical_or(owned, table_ref[slots + r] == e)
        value = jnp.dot(left[at], right[at], preferred_element_type=F32)

        @pl.when(jnp.logical_not(owned))
        def _():
            obuf[e] = value.astype(BF)

        @pl.when(owned)
        def _():
            total = value
            for r in range(replicas):
                i = table_ref[experts + r]
                more = jnp.dot(left[i], right[i], preferred_element_type=F32)
                total = total + jnp.where(table_ref[slots + r] == e, more, 0.0)
            obuf[e] = total.astype(BF)

        put(e).start()
        return carry

    lax.fori_loop(0, experts, step, 0)

    def finish(e, carry):
        put(e).wait()
        return carry

    lax.fori_loop(0, experts, finish, 0)


def expert_sums(table, rows, pieces, first, total, previous, replicas):
    slots, depth, n = rows.shape
    experts = slots - replicas
    hidden = pieces[0].shape[-1]
    operands = [rows] + list(pieces)
    aliases = {}
    if previous is not None:
        operands.append(previous)
        aliases = {len(operands): 0}
    return pl.pallas_call(
        lambda *refs: expert_kernel(slots, replicas, first, *refs),
        grid_spec=pltpu.PrefetchScalarGridSpec(
            num_scalar_prefetch=1,
            grid=(1,),
            in_specs=[ANY for _ in operands],
            out_specs=ANY,
            scratch_shapes=[
                pltpu.VMEM((slots, depth, n), BF),
                pltpu.VMEM((slots, n, hidden), BF),
                pltpu.VMEM((experts, depth, hidden), BF),
                pltpu.SemaphoreType.DMA((slots,)),
                pltpu.SemaphoreType.DMA((slots,)),
                pltpu.SemaphoreType.DMA((experts,)),
            ],
        ),
        out_shape=jax.ShapeDtypeStruct((experts, total, depth, hidden), BF),
        input_output_aliases=aliases,
    )(table, *operands)


def lent_columns(width, parts, sevenths):
    if parts > 2:
        return width // parts
    return width * sevenths // 7 // LANES * LANES


def after(value, *others):
    return lax.optimization_barrier((value, *others))[0]


def per_device(tokens, cotangent, gate_weights, route_slots, replica_owner, w_gate, w_up, w_down):
    grid = Grid()
    slots = grid.total
    na, nb, nc = grid.sizes
    tok, width = tokens.shape
    top = route_slots.shape[1]
    rows = tok * top * 3 // 2
    replicas = replica_owner.shape[0]
    wg, wu, wd = w_gate[0], w_up[0], w_down[0]
    hidden = wg.shape[1]
    all_tok = tok * slots
    depth = width // slots
    part = width // grid.parts

    meta = jnp.concatenate(
        [route_slots.astype(BF), gate_weights, jnp.zeros((tok, LANES - 2 * top), BF)], axis=1
    )
    meta_all = grid.gather_small(meta).reshape(all_tok, LANES)
    x_pieces = grid.gather_rows(tokens, width // grid.parts)
    dy_pieces = grid.gather_rows(cotangent, lent_columns(width, grid.parts, 2))

    ids = grid.ids()
    routes = meta_all[:, :top].astype(jnp.int32)
    gates = meta_all[:, top : 2 * top].astype(F32)
    token_ids = (ids[:, None] * tok + jnp.arange(tok, dtype=jnp.int32)[None, :]).reshape(-1)
    named = jnp.any(routes[None, :, :] == ids[:, None, None], axis=2)
    before = (token_ids[:, None] < token_ids[None, :]).astype(BF)
    place = jnp.dot(named.astype(BF), before, preferred_element_type=F32).astype(jnp.int32)
    place = jnp.where(named, place, -1)
    gate = jnp.sum(jnp.where(routes == ids[0], gates, 0.0), axis=1)[:, None]

    first = grid.me * depth
    window = window_of(width, depth)
    start = jnp.minimum(first // LANES * LANES, width - window)
    at = jnp.stack([grid.part, start, grid.me]).astype(jnp.int32)
    square = jax.ShapeDtypeStruct((all_tok, hidden), F32)
    square_b = jax.ShapeDtypeStruct((all_tok, hidden), BF)
    proj, up_proj, down, x_window = forward_call(
        gate_kernel,
        at,
        [wg, wu],
        [gate, place[:1]],
        x_pieces,
        [square, square, jax.ShapeDtypeStruct((rows, hidden), BF)],
        2,
        width,
        all_tok,
        depth,
        grid.parts,
        tok,
    )
    down_all = grid.gather(down, together=True)
    pre, upg, pre_rows, upg_rows, score, dy_window = forward_call(
        down_kernel,
        at,
        [wd],
        [gate, place[:1], proj, up_proj],
        dy_pieces,
        [
            square_b,
            square_b,
            jax.ShapeDtypeStruct((rows, hidden), BF),
            jax.ShapeDtypeStruct((rows, hidden), BF),
            jax.ShapeDtypeStruct((all_tok, LANES), BF),
        ],
        0,
        width,
        all_tok,
        depth,
        grid.parts,
        tok,
    )
    pre_all = grid.gather(pre_rows)
    upg_all = grid.gather(upg_rows)

    terms = {}
    for h in [*range(1, grid.parts), 0]:
        share = input_part(grid, h, pre, upg, score, wg, wu)
        total = share[0].astype(F32)
        for k in range(1, nc):
            total = total + grid.shift(share[k], 2, -k).astype(F32)
        terms[h] = total.astype(BF)
        if h > 0:
            terms[h] = grid.tensor_shift(terms[h], -h)
    terms = [terms[h] for h in range(grid.parts)]
    if grid.parts > 2:
        terms = list(jnp.roll(jnp.stack(terms)[::-1], grid.part + 1, axis=0))
    total = terms[0].astype(F32)
    for term in terms[1:]:
        total = total + term.astype(F32)
    total = total.astype(BF).reshape(nb, na, tok, part + LANES)
    half = part // 2 // LANES * LANES
    left, right = total[..., :half], total[..., half:]
    left_line, right_line = left[0].astype(F32), right[:, 0].astype(F32)
    for k in nearest_steps(na):
        right_line = right_line + grid.shift(right[:, k], 0, -k).astype(F32)
    for k in range(1, nb):
        left_line = left_line + grid.shift(left[k], 1, -k).astype(F32)
    left_line, right_line = left_line.astype(BF), right_line.astype(BF)
    left_sum, right_sum = left_line[0].astype(F32), right_line[0].astype(F32)
    for k in nearest_steps(na):
        left_sum = left_sum + grid.shift(left_line[k], 0, -k).astype(F32)
    for k in range(1, nb):
        right_sum = right_sum + grid.shift(right_line[k], 1, -k).astype(F32)
    last = jnp.concatenate([left_sum, right_sum], axis=1)
    input_grads = last[:, :part].astype(BF)
    lane = jnp.arange(LANES, dtype=jnp.int32)
    own_routes = route_slots[:, :, None] == lane[None, None, :]
    gate_grads = jnp.sum(jnp.where(own_routes, last[:, None, part:], 0.0), axis=2).astype(BF)

    x_window, dy_window = after(x_window, share), after(dy_window, share)
    x_t = lax.dynamic_slice_in_dim(x_window, first - start, depth, 1).T
    dy_t = lax.dynamic_slice_in_dim(dy_window, first - start, depth, 1).T
    spot = jnp.sum(
        jnp.where(
            ids[None, :] == jnp.arange(slots, dtype=jnp.int32)[:, None],
            jnp.arange(slots, dtype=jnp.int32)[None, :],
            0,
        ),
        axis=1,
    )
    x_pick, dy_pick = picked(place, x_t, dy_t, rows)
    table = jnp.concatenate([spot, replica_owner]).astype(jnp.int32)
    out = expert_sums(table, dy_pick, down_all, 2, 3, None, replicas)
    out = expert_sums(table, x_pick, pre_all, 0, 3, out, replicas)
    out = expert_sums(table, x_pick, upg_all, 1, 3, out, replicas)
    return input_grads, gate_grads, jnp.transpose(out, (0, 2, 1, 3))


def solution(mesh):
    in_specs = (
        P("expert", None),
        P("expert", None),
        P("expert", None),
        P("expert", None),
        P(),
        P("expert", None, "tensor"),
        P("expert", None, "tensor"),
        P("expert", None, "tensor"),
    )
    out_specs = (P("expert", "tensor"), P("expert", None), P(None, "expert", None, "tensor"))

    return jax.shard_map(
        per_device, mesh=mesh, in_specs=in_specs, out_specs=out_specs, check_vma=False
    )
```

time: 466 us -> 419 us (0.90)
  waiting for transfers between devices: 247 us -> 201 us
  Pallas kernels: 104 us -> 94.7 us
  starting transfers between devices: 74.9 us -> 80.1 us
    ppermute x82 -> x79, waiting for transfers between devices: 221 us -> 181 us  [shift(): return lax.ppermute(value, 'expert', pairs)]
    ppermute x13, waiting for transfers between devices: 26.1 us -> 19.7 us  [tensor_shift(): lax.ppermute(value, 'tensor', [((i + step) % n, i) for i in range(n)])]
    pallas_call x4, Pallas kernels: 50.1 us -> 44.1 us  [the longest x3 33.1 us: expert_sums(): pl.pallas_call(lambda *refs: expert_kernel(slots, replicas, first, *refs)...]
    ppermute x82 -> x79, starting transfers between devices: 62.8 us -> 65 us  [shift(): return lax.ppermute(value, 'expert', pairs)]
  transfers between devices with their start and end apart: 95 -> 92, of which waited for: 44 -> 39; matrix products, arithmetic and copies ran while one was open for 5% -> 8% of each run, Pallas kernels for 17% -> 23%
where the time goes in v3:
time: 419 us; the launch traced here: 413 us
  waiting for transfers between devices  201 us (48%)
  Pallas kernels  94.7 us (23%)
  starting transfers between devices  80.1 us (19%)
  local copies, waits for them, and re-layouts  23.3 us (6%)
  other arithmetic  12.5 us (3%)
    ppermute x79, waiting for transfers between devices, shift(): return lax.ppermute(value, 'expert', pairs)  181 us
    ppermute x79, starting transfers between devices, shift(): return lax.ppermute(value, 'expert', pairs)  65 us
    pallas_call x2, Pallas kernels, forward_call(): pl.pallas_call(body, grid_spec=pltpu.PrefetchScalarGridSpec(num_scalar_pr...  33.2 us
    pallas_call x3, Pallas kernels, expert_sums(): pl.pallas_call(lambda *refs: expert_kernel(slots, replicas, first, *refs)...  33.1 us
    ppermute x13, waiting for transfers between devices, tensor_shift(): lax.ppermute(value, 'tensor', [((i + step) % n, i) for i in range(n)])  19.7 us
    pallas_call x2, Pallas kernels, input_part(): pl.pallas_call(input_kernel, grid_spec=pltpu.PrefetchScalarGridSpec(num_s...  17.4 us
    ppermute x13, starting transfers between devices, tensor_shift(): lax.ppermute(value, 'tensor', [((i + step) % n, i) for i in range(n)])  15.2 us
    pallas_call x1, Pallas kernels, picked(): pl.pallas_call(pick_kernel, grid=(slots // per,), in_specs=[pl.BlockSpec(...  11.1 us
  transfers between devices with their start and end apart: 92, of which 39 were waited for; matrix products, arithmetic and copies ran while one was open for 8% of the time, Pallas kernels for 23%

profile of v3, /device:TPU:16, one launch (start us, length us, event | category | flops | bytes accessed | tf_op | source)
XLA Modules:
  0.0 413.5 jit_solution(6857798124082820841)
XLA Ops:
  14.7 9.9 %collective-permute-done.3 = bf16[4,32,128]{2,1,0:T(8,128)(2,1)S(1)} collective-permute-done((bf16[4,32,128]{2,1,0:T(8,128)(2,1)S(1)}, bf16[4,32,128]{2,1,0:T(8,128)(2,1)S(1)}, u32[]{:S(2)}, u32[]{:S(2)}) %collective-permute-start.3) | collective-permute-done | bytes 32800 | tf_op jit(solution)/shard_map/ppermute | solution.py:54
  31.6 19.3 %collective-permute-done.25.refs_8_ = bf16[32,5120]{1,0:T(8,128)(2,1)S(1)} collective-permute-done((bf16[32,5120]{1,0:T(8,128)(2,1)S(1)}, bf16[32,5120]{1,0:T(8,128)(2,1)S(1)}, u32[]{:S(2)}, u32[]{:S(2)}) %collective-permute-start.25) | collective-permute-done | bytes 327712 | tf_op jit(solution)/shard_map/ppermute | solution.py:54
  81.7 9.7 %collective-permute-done.31.refs_14_ = bf16[32,5120]{1,0:T(8,128)(2,1)S(1)} collective-permute-done((bf16[32,5120]{1,0:T(8,128)(2,1)S(1)}, bf16[32,5120]{1,0:T(8,128)(2,1)S(1)}, u32[]{:S(2)}, u32[]{:S(2)}) %collective-permute-start.31) | collective-permute-done | bytes 327712 | tf_op jit(solution)/shard_map/ppermute | solution.py:54
  103.4 5.2 %collective-permute-done.30.refs_13_ = bf16[32,2048]{1,0:T(8,128)(2,1)S(1)} collective-permute-done((bf16[32,2048]{1,0:T(8,128)(2,1)S(1)}, bf16[32,2048]{1,0:T(8,128)(2,1)S(1)}, u32[]{:S(2)}, u32[]{:S(2)}) %collective-permute-start.30) | collective-permute-done | bytes 131104 | tf_op jit(solution)/shard_map/ppermute | solution.py:58
  125.8 19.4 %shard_map.103 = (f32[512,512]{1,0:T(8,128)}, f32[512,512]{1,0:T(8,128)}, bf16[384,512]{1,0:T(8,128)(2,1)}, bf16[512,640]{1,0:T(8,128)(2,1)}) custom-call(s32[3]{0:T(128)} %pad_add_fusion.refs_0_, bf16[7168,512]{1,0:T(8,128)(2,1)} %bitcast.113, bf16[7168,512]{1,0:T(8,128)(2,1)} %bitcast.116, f32[512,1]{1,0:T(8,128)} %copy.65.refs_3_.refs_2_, ...), custom_call_target="tpu_custom_call" | custom-call | tf_op jit(solution)/shard_map/pallas_call | solution.py:266
  153.6 13.8 %shard_map.104 = (bf16[512,512]{1,0:T(8,128)(2,1)}, bf16[512,512]{1,0:T(8,128)(2,1)}, bf16[384,512]{1,0:T(8,128)(2,1)}, bf16[384,512]{1,0:T(8,128)(2,1)}, bf16[5...) custom-call(s32[3]{0:T(128)} %pad_add_fusion.refs_0_, bf16[7168,512]{1,0:T(8,128)(2,1)} %bitcast.123, ...), custom_call_target="tpu_custom_call" | custom-call | tf_op jit(solution)/shard_map/pallas_call | solution.py:266
  167.5 8.6 %shard_map.106 = bf16[2,256,3712]{2,1,0:T(8,128)(2,1)} custom-call(s32[1]{0:T(128)} %bitcast.28.index_ref, bf16[512,512]{1,0:T(8,128)(2,1)} %get-tuple-element.19.pre_ref, bf16[512,512]{1,0:T(8,128)(2,1)} %get-tuple-element.20.up_ref, bf16[512,128]{1,0:T(8,128)(2,1)} %get-tuple-element.21.score_ref, bf16[7168,512]{1,0:T(8,128)(2,1)} %bitcast.114, ...), custom_call_target="tpu_custom_call" | custom-call | tf_op jit(solution)/shard_map/pallas_call | solution.py:342
  177.8 8.8 %shard_map.105 = bf16[2,256,3712]{2,1,0:T(8,128)(2,1)} custom-call(s32[1]{0:T(128)} %bitcast.index_ref, bf16[512,512]{1,0:T(8,128)(2,1)} %get-tuple-element.19.pre_ref, bf16[512,512]{1,0:T(8,128)(2,1)} %get-tuple-element.20.up_ref, bf16[512,128]{1,0:T(8,128)(2,1)} %get-tuple-element.21.score_ref, bf16[7168,512]{1,0:T(8,128)(2,1)} %bitcast.115, ...), custom_call_target="tpu_custom_call" | custom-call | tf_op jit(solution)/shard_map/pallas_call | solution.py:342
  189.1 13.1 %collective-permute-done.86.refs_5_ = bf16[384,512]{1,0:T(8,128)(2,1)S(1)} collective-permute-done((bf16[384,512]{1,0:T(8,128)(2,1)}, bf16[384,512]{1,0:T(8,128)(2,1)S(1)}, u32[]{:S(2)}, u32[]{:S(2)}) %collective-permute-start.86) | collective-permute-done | bytes 393248 | tf_op jit(solution)/shard_map/ppermute | solution.py:54
  207.4 7.8 %collective-permute-done.70.refs_4_ = bf16[384,512]{1,0:T(8,128)(2,1)S(1)} collective-permute-done((bf16[384,512]{1,0:T(8,128)(2,1)}, bf16[384,512]{1,0:T(8,128)(2,1)S(1)}, u32[]{:S(2)}, u32[]{:S(2)}) %collective-permute-start.70) | collective-permute-done | bytes 393248 | tf_op jit(solution)/shard_map/ppermute | solution.py:54
  232.7 16.2 %collective-permute-done.55.refs_4_ = bf16[384,512]{1,0:T(8,128)(2,1)} collective-permute-done((bf16[384,512]{1,0:T(8,128)(2,1)S(1)}, bf16[384,512]{1,0:T(8,128)(2,1)}, u32[]{:S(2)}, u32[]{:S(2)}) %collective-permute-start.55) | collective-permute-done | bytes 393248 | tf_op jit(solution)/shard_map/ppermute | solution.py:54
  260.9 8.4 %collective-permute-done.90.refs_9_ = bf16[384,512]{1,0:T(8,128)(2,1)S(1)} collective-permute-done((bf16[384,512]{1,0:T(8,128)(2,1)S(1)}, bf16[384,512]{1,0:T(8,128)(2,1)S(1)}, u32[]{:S(2)}, u32[]{:S(2)}) %collective-permute-start.90) | collective-permute-done | bytes 393248 | tf_op jit(solution)/shard_map/ppermute | solution.py:54
  269.4 8.4 %collective-permute-done.73.refs_7_ = bf16[384,512]{1,0:T(8,128)(2,1)S(1)} collective-permute-done((bf16[384,512]{1,0:T(8,128)(2,1)}, bf16[384,512]{1,0:T(8,128)(2,1)S(1)}, u32[]{:S(2)}, u32[]{:S(2)}) %collective-permute-start.73) | collective-permute-done | bytes 393248 | tf_op jit(solution)/shard_map/ppermute | solution.py:54
  280.8 5.4 %collective-permute-done.74.refs_8_ = bf16[384,512]{1,0:T(8,128)(2,1)S(1)} collective-permute-done((bf16[384,512]{1,0:T(8,128)(2,1)S(1)}, bf16[384,512]{1,0:T(8,128)(2,1)S(1)}, u32[]{:S(2)}, u32[]{:S(2)}) %collective-permute-start.74) | collective-permute-done | bytes 393248 | tf_op jit(solution)/shard_map/ppermute | solution.py:54
  286.2 6.4 %collective-permute-done.75.refs_9_ = bf16[384,512]{1,0:T(8,128)(2,1)S(1)} collective-permute-done((bf16[384,512]{1,0:T(8,128)(2,1)S(1)}, bf16[384,512]{1,0:T(8,128)(2,1)S(1)}, u32[]{:S(2)}, u32[]{:S(2)}) %collective-permute-start.75) | collective-permute-done | bytes 393248 | tf_op jit(solution)/shard_map/ppermute | solution.py:54
  301.2 5.4 %collective-permute-done.58.refs_7_ = bf16[384,512]{1,0:T(8,128)(2,1)S(1)} collective-permute-done((bf16[384,512]{1,0:T(8,128)(2,1)}, bf16[384,512]{1,0:T(8,128)(2,1)S(1)}, u32[]{:S(2)}, u32[]{:S(2)}) %collective-permute-start.58) | collective-permute-done | bytes 393248 | tf_op jit(solution)/shard_map/ppermute | solution.py:54
  307.7 7.3 %collective-permute-done.59.refs_8_ = bf16[384,512]{1,0:T(8,128)(2,1)} collective-permute-done((bf16[384,512]{1,0:T(8,128)(2,1)}, bf16[384,512]{1,0:T(8,128)(2,1)}, u32[]{:S(2)}, u32[]{:S(2)}) %collective-permute-start.59) | collective-permute-done | bytes 393248 | tf_op jit(solution)/shard_map/ppermute | solution.py:54
  315.1 7.6 %collective-permute-done.60.refs_9_ = bf16[384,512]{1,0:T(8,128)(2,1)} collective-permute-done((bf16[384,512]{1,0:T(8,128)(2,1)S(1)}, bf16[384,512]{1,0:T(8,128)(2,1)}, u32[]{:S(2)}, u32[]{:S(2)}) %collective-permute-start.60) | collective-permute-done | bytes 393248 | tf_op jit(solution)/shard_map/ppermute | solution.py:54
  335.7 5.3 %collective-permute-start.52 = (bf16[2,32,1920]{2,1,0:T(8,128)(2,1)}, bf16[2,32,1920]{2,1,0:T(8,128)(2,1)}, u32[]{:S(2)}, u32[]{:S(2)}) collective-permute-start(bf16[2,32,1920]{2,1,0:T(8,128)(2,1)} %get-tuple-element.44), channel_id=1, source_target_pairs={{16,0},{18,2},{20,4},{22,6},{24,8},{26,10},{28,12},{30,14},{0,16},... | collective-permute-start | bytes 737288 | tf_op jit(solution)/shard_map/ppermute | solution.py:54
  342.2 11.1 %shard_map.107 = (bf16[16,448,384]{2,1,0:T(8,128)(2,1)}, bf16[16,448,384]{2,1,0:T(8,128)(2,1)}) custom-call(s32[16,1,512]{2,1,0:T(1,128)} %reshape.199.place_ref, bf16[896,512]{1,0:T(8,128)(2,1)} %pad_maximum_fusion.2.both_ref), custom_call_target="tpu_custom_call" | custom-call | tf_op jit(solution)/shard_map/pallas_call | solution.py:376
  353.3 11.0 %shard_map.108.refs_18_ = bf16[14,3,448,512]{3,2,1,0:T(8,128)(2,1)} custom-call(s32[18]{0:T(128)} %pad_add_fusion.1.refs_0_, bf16[16,448,384]{2,1,0:T(8,128)(2,1)} %get-tuple-element.29.refs_1_, bf16[384,512]{1,0:T(8,128)(2,1)} %get-tuple-element.30.refs_2_, bf16[384,512]{1,0:T(8,128)(2,1)} %copy-done.7, bf16[384,512]{1,0:T(8,128)(2,1)} %copy-done.8, ...), custom_call_target="tpu_custom_call" | custom-call | tf_op jit(solution)/shard_map/pallas_call | solution.py:462
  364.3 11.0 %shard_map.109.refs_18_ = bf16[14,3,448,512]{3,2,1,0:T(8,128)(2,1)} custom-call(s32[18]{0:T(128)} %pad_add_fusion.1.refs_0_, bf16[16,448,384]{2,1,0:T(8,128)(2,1)} %get-tuple-element.26.refs_1_, bf16[384,512]{1,0:T(8,128)(2,1)} %get-tuple-element.28.refs_2_, bf16[384,512]{1,0:T(8,128)(2,1)} %collective-permute-done.69.refs_3_, ...), custom_call_target="tpu_custom_call", output_to_operand_aliasing={{}: (18, {})} | custom-call | tf_op jit(solution)/shard_map/pallas_call | solution.py:462
  375.3 11.0 %shard_map.110 = bf16[14,3,448,512]{3,2,1,0:T(8,128)(2,1)} custom-call(s32[18]{0:T(128)} %pad_add_fusion.1.refs_0_, bf16[16,448,384]{2,1,0:T(8,128)(2,1)} %get-tuple-element.26.refs_1_, bf16[384,512]{1,0:T(8,128)(2,1)} %get-tuple-element.27.refs_2_, bf16[384,512]{1,0:T(8,128)(2,1)} %collective-permute-done.54.refs_3_, ...), custom_call_target="tpu_custom_call", output_to_operand_aliasing={{}: (18, {})} | custom-call | tf_op jit(solution)/shard_map/pallas_call | solution.py:462
  393.9 8.4 %collective-permute-done.46 = bf16[4,32,1792]{2,1,0:T(8,128)(2,1)S(1)} collective-permute-done((bf16[4,32,1792]{2,1,0:T(8,128)(2,1)S(1)}, bf16[4,32,1792]{2,1,0:T(8,128)(2,1)S(1)}, u32[]{:S(2)}, u32[]{:S(2)}) %collective-permute-start.46) | collective-permute-done | bytes 458784 | tf_op jit(solution)/shard_map/ppermute | solution.py:54
  (381 shorter events, 173.2 us)
Async XLA Ops:
  12.5 67.1 %collective-permute-start.5 = (bf16[32,7168]{1,0:T(8,128)(2,1)}, bf16[32,7168]{1,0:T(8,128)(2,1)}, u32[]{:S(2)}, u32[]{:S(2)}) collective-permute-start(bf16[32,7168]{1,0:T(8,128)(2,1)} %refs_5_.1), channel_id=1, source_target_pairs={{4,0},{6,2},{0,4},{2,6},{12,8},{14,10},{8,12},{10,14},{20,16},{22,... | collective-permute-start | bytes 1376264 | tf_op jit(solution)/shard_map/ppermute | solution.py:54
  26.0 55.2 %collective-permute-start.18 = (bf16[32,7168]{1,0:T(8,128)(2,1)S(1)}, bf16[32,7168]{1,0:T(8,128)(2,1)}, u32[]{:S(2)}, u32[]{:S(2)}) collective-permute-start(bf16[32,7168]{1,0:T(8,128)(2,1)S(1)} %copy-done.15), channel_id=1, source_target_pairs={{2,0},{0,2},{6,4},{4,6},{10,8},{8,10},{14,12},{12,14},{18,16},{16,... | collective-permute-start | bytes 1376264 | tf_op jit(solution)/shard_map/ppermute | solution.py:54
  71.0 37.6 %collective-permute-start.24 = (bf16[32,7168]{1,0:T(8,128)(2,1)S(1)}, bf16[32,7168]{1,0:T(8,128)(2,1)}, u32[]{:S(2)}, u32[]{:S(2)}) collective-permute-start(bf16[32,7168]{1,0:T(8,128)(2,1)S(1)} %copy-done.14), channel_id=1, source_target_pairs={{4,0},{6,2},{0,4},{2,6},{12,8},{14,10},{8,12},{10,14},{20,16},{22,... | collective-permute-start | bytes 1376264 | tf_op jit(solution)/shard_map/ppermute | solution.py:54
  121.3 31.2 %collective-permute-start.39 = (bf16[96,5120]{1,0:T(8,128)(2,1)}, bf16[96,5120]{1,0:T(8,128)(2,1)S(1)}, u32[]{:S(2)}, u32[]{:S(2)}) collective-permute-start(bf16[96,5120]{1,0:T(8,128)(2,1)} %pad_maximum_fusion), channel_id=1, source_target_pairs={{2,0},{0,2},{6,4},{4,6},{10,8},{8,10},{14,12},{12,14},{18,16},{16,... | collective-permute-start | bytes 2949128 | tf_op jit(solution)/shard_map/ppermute | solution.py:54
  121.8 31.8 %collective-permute-start.41 = (bf16[96,5120]{1,0:T(8,128)(2,1)}, bf16[96,5120]{1,0:T(8,128)(2,1)}, u32[]{:S(2)}, u32[]{:S(2)}) collective-permute-start(bf16[96,5120]{1,0:T(8,128)(2,1)} %pad_maximum_fusion.1), channel_id=1, source_target_pairs={{2,0},{0,2},{6,4},{4,6},{10,8},{8,10},{14,12},{12,14},{18,16},{16,... | collective-permute-start | bytes 2949128 | tf_op jit(solution)/shard_map/ppermute | solution.py:54
  147.0 39.6 %collective-permute-start.84 = (bf16[384,512]{1,0:T(8,128)(2,1)}, bf16[384,512]{1,0:T(8,128)(2,1)S(1)}, u32[]{:S(2)}, u32[]{:S(2)}) collective-permute-start(bf16[384,512]{1,0:T(8,128)(2,1)} %get-tuple-element.30.refs_2_), channel_id=1, source_target_pairs={{8,0},{10,2},{12,4},{14,6},{16,8},{18,10},{20,12},{22,14},{24,16},... | collective-permute-start | bytes 1179656 | tf_op jit(solution)/shard_map/ppermute | solution.py:54
  147.0 42.1 %collective-permute-start.85 = (bf16[384,512]{1,0:T(8,128)(2,1)}, bf16[384,512]{1,0:T(8,128)(2,1)S(1)}, u32[]{:S(2)}, u32[]{:S(2)}) collective-permute-start(bf16[384,512]{1,0:T(8,128)(2,1)} %get-tuple-element.30.refs_2_), channel_id=1, source_target_pairs={{16,0},{18,2},{20,4},{22,6},{24,8},{26,10},{28,12},{30,14},{0,16},... | collective-permute-start | bytes 1179656 | tf_op jit(solution)/shard_map/ppermute | solution.py:54
  150.5 51.8 %collective-permute-start.86 = (bf16[384,512]{1,0:T(8,128)(2,1)}, bf16[384,512]{1,0:T(8,128)(2,1)S(1)}, u32[]{:S(2)}, u32[]{:S(2)}) collective-permute-start(bf16[384,512]{1,0:T(8,128)(2,1)} %get-tuple-element.30.refs_2_), channel_id=1, source_target_pairs={{24,0},{26,2},{28,4},{30,6},{0,8},{2,10},{4,12},{6,14},{8,16},{10,... | collective-permute-start | bytes 1179656 | tf_op jit(solution)/shard_map/ppermute | solution.py:54
  152.4 53.7 %collective-permute-start.87 = (bf16[384,512]{1,0:T(8,128)(2,1)}, bf16[384,512]{1,0:T(8,128)(2,1)S(1)}, u32[]{:S(2)}, u32[]{:S(2)}) collective-permute-start(bf16[384,512]{1,0:T(8,128)(2,1)} %get-tuple-element.30.refs_2_), channel_id=1, source_target_pairs={{4,0},{6,2},{0,4},{2,6},{12,8},{14,10},{8,12},{10,14},{20,16},{22,... | collective-permute-start | bytes 1179656 | tf_op jit(solution)/shard_map/ppermute | solution.py:54
  167.4 40.0 %collective-permute-start.69 = (bf16[384,512]{1,0:T(8,128)(2,1)}, bf16[384,512]{1,0:T(8,128)(2,1)}, u32[]{:S(2)}, u32[]{:S(2)}) collective-permute-start(bf16[384,512]{1,0:T(8,128)(2,1)} %get-tuple-element.28.refs_2_), channel_id=1, source_target_pairs={{8,0},{10,2},{12,4},{14,6},{16,8},{18,10},{20,12},{22,14},{24,16},... | collective-permute-start | bytes 1179656 | tf_op jit(solution)/shard_map/ppermute | solution.py:54
  186.7 28.6 %collective-permute-start.70 = (bf16[384,512]{1,0:T(8,128)(2,1)}, bf16[384,512]{1,0:T(8,128)(2,1)S(1)}, u32[]{:S(2)}, u32[]{:S(2)}) collective-permute-start(bf16[384,512]{1,0:T(8,128)(2,1)} %get-tuple-element.28.refs_2_), channel_id=1, source_target_pairs={{16,0},{18,2},{20,4},{22,6},{24,8},{26,10},{28,12},{30,14},{0,16},... | collective-permute-start | bytes 1179656 | tf_op jit(solution)/shard_map/ppermute | solution.py:54
  189.1 29.9 %collective-permute-start.71 = (bf16[384,512]{1,0:T(8,128)(2,1)}, bf16[384,512]{1,0:T(8,128)(2,1)S(1)}, u32[]{:S(2)}, u32[]{:S(2)}) collective-permute-start(bf16[384,512]{1,0:T(8,128)(2,1)} %get-tuple-element.28.refs_2_), channel_id=1, source_target_pairs={{24,0},{26,2},{28,4},{30,6},{0,8},{2,10},{4,12},{6,14},{8,16},{10,... | collective-permute-start | bytes 1179656 | tf_op jit(solution)/shard_map/ppermute | solution.py:54
  202.2 53.7 %collective-permute-start.44 = (bf16[256,3712]{1,0:T(8,128)(2,1)S(1)}, bf16[256,3712]{1,0:T(8,128)(2,1)S(1)}, u32[]{:S(2)}, u32[]{:S(2)}) collective-permute-start(bf16[256,3712]{1,0:T(8,128)(2,1)S(1)} %slice_bitcast_fusion), channel_id=1, source_target_pairs={{2,0},{0,2},{6,4},{4,6},{10,8},{8,10},{14,12},{12,14},{18,16},{16,... | collective-permute-start | bytes 5701640 | tf_op jit(solution)/shard_map/ppermute | solution.py:54
  221.8 31.0 %collective-permute-start.56 = (bf16[384,512]{1,0:T(8,128)(2,1)S(1)}, bf16[384,512]{1,0:T(8,128)(2,1)S(1)}, u32[]{:S(2)}, u32[]{:S(2)}) collective-permute-start(bf16[384,512]{1,0:T(8,128)(2,1)S(1)} %copy-done.40), channel_id=1, source_target_pairs={{24,0},{26,2},{28,4},{30,6},{0,8},{2,10},{4,12},{6,14},{8,16},{10,... | collective-permute-start | bytes 1179656 | tf_op jit(solution)/shard_map/ppermute | solution.py:54
  254.8 31.4 %collective-permute-start.74 = (bf16[384,512]{1,0:T(8,128)(2,1)S(1)}, bf16[384,512]{1,0:T(8,128)(2,1)S(1)}, u32[]{:S(2)}, u32[]{:S(2)}) collective-permute-start(bf16[384,512]{1,0:T(8,128)(2,1)S(1)} %collective-permute-done.70.refs_4_), channel_id=1, source_target_pairs={{4,0},{6,2},{0,4},{2,6},{12,8},{14,10},{8,12},{10,14},{20,16},{22,... | collective-permute-start | bytes 1179656 | tf_op jit(solution)/shard_map/ppermute | solution.py:54
  256.0 36.6 %collective-permute-start.75 = (bf16[384,512]{1,0:T(8,128)(2,1)S(1)}, bf16[384,512]{1,0:T(8,128)(2,1)S(1)}, u32[]{:S(2)}, u32[]{:S(2)}) collective-permute-start(bf16[384,512]{1,0:T(8,128)(2,1)S(1)} %collective-permute-done.71.refs_5_), channel_id=1, source_target_pairs={{4,0},{6,2},{0,4},{2,6},{12,8},{14,10},{8,12},{10,14},{20,16},{22,... | collective-permute-start | bytes 1179656 | tf_op jit(solution)/shard_map/ppermute | solution.py:54
  260.9 66.7 %collective-permute-start.43 = (bf16[256,3712]{1,0:T(8,128)(2,1)}, bf16[256,3712]{1,0:T(8,128)(2,1)}, u32[]{:S(2)}, u32[]{:S(2)}) collective-permute-start(bf16[256,3712]{1,0:T(8,128)(2,1)} %slice_bitcast_fusion.2), channel_id=1, source_target_pairs={{2,0},{0,2},{6,4},{4,6},{10,8},{8,10},{14,12},{12,14},{18,16},{16,... | collective-permute-start | bytes 5701640 | tf_op jit(solution)/shard_map/ppermute | solution.py:54
  277.8 50.3 %collective-permute-start.45 = (bf16[256,3712]{1,0:T(8,128)(2,1)S(1)}, bf16[256,3712]{1,0:T(8,128)(2,1)}, u32[]{:S(2)}, u32[]{:S(2)}) collective-permute-start(bf16[256,3712]{1,0:T(8,128)(2,1)S(1)} %fusion), channel_id=1, source_target_pairs={{1,0},{0,1},{3,2},{2,3},{5,4},{4,5},{7,6},{6,7},{9,8},{8,9},{11,10... | collective-permute-start | bytes 5701640 | tf_op jit(solution)/shard_map/ppermute | solution.py:58
  293.5 42.1 %collective-permute-start.91 = (bf16[8,384,512]{2,1,0:T(8,128)(2,1)}, bf16[8,384,512]{2,1,0:T(8,128)(2,1)}, u32[]{:S(2)}, u32[]{:S(2)}) collective-permute-start(bf16[8,384,512]{2,1,0:T(8,128)(2,1)} %bitcast_dynamic-update-slice_fusion), channel_id=1, source_target_pairs={{2,0},{0,2},{6,4},{4,6},{10,8},{8,10},{14,12},{12,14},{18,16},{16,... | collective-permute-start | bytes 9437192 | tf_op jit(solution)/shard_map/ppermute | solution.py:54
  332.2 43.1 %collective-permute-start.67 = (bf16[384,512]{1,0:T(8,128)(2,1)}, bf16[384,512]{1,0:T(8,128)(2,1)}, u32[]{:S(2)}, u32[]{:S(2)}) collective-permute-start(bf16[384,512]{1,0:T(8,128)(2,1)} %collective-permute-done.59.refs_8_), channel_id=1, source_target_pairs={{2,0},{0,2},{6,4},{4,6},{10,8},{8,10},{14,12},{12,14},{18,16},{16,... | collective-permute-start | bytes 1179656 | tf_op jit(solution)/shard_map/ppermute | solution.py:54
  332.6 42.7 %collective-permute-start.68 = (bf16[384,512]{1,0:T(8,128)(2,1)}, bf16[384,512]{1,0:T(8,128)(2,1)}, u32[]{:S(2)}, u32[]{:S(2)}) collective-permute-start(bf16[384,512]{1,0:T(8,128)(2,1)} %collective-permute-done.60.refs_9_), channel_id=1, source_target_pairs={{2,0},{0,2},{6,4},{4,6},{10,8},{8,10},{14,12},{12,14},{18,16},{16,... | collective-permute-start | bytes 1179656 | tf_op jit(solution)/shard_map/ppermute | solution.py:54
  333.6 52.8 %collective-permute-start.50 = (bf16[2,32,1920]{2,1,0:T(8,128)(2,1)}, bf16[2,32,1920]{2,1,0:T(8,128)(2,1)S(1)}, u32[]{:S(2)}, u32[]{:S(2)}) collective-permute-start(bf16[2,32,1920]{2,1,0:T(8,128)(2,1)} %get-tuple-element.42), channel_id=1, source_target_pairs={{24,0},{26,2},{28,4},{30,6},{0,8},{2,10},{4,12},{6,14},{8,16},{10,... | collective-permute-start | bytes 737288 | tf_op jit(solution)/shard_map/ppermute | solution.py:54
  333.9 52.5 %collective-permute-start.51 = (bf16[2,32,1920]{2,1,0:T(8,128)(2,1)}, bf16[2,32,1920]{2,1,0:T(8,128)(2,1)}, u32[]{:S(2)}, u32[]{:S(2)}) collective-permute-start(bf16[2,32,1920]{2,1,0:T(8,128)(2,1)} %get-tuple-element.43), channel_id=1, source_target_pairs={{8,0},{10,2},{12,4},{14,6},{16,8},{18,10},{20,12},{22,14},{24,16},... | collective-permute-start | bytes 737288 | tf_op jit(solution)/shard_map/ppermute | solution.py:54
  335.7 50.7 %collective-permute-start.52 = (bf16[2,32,1920]{2,1,0:T(8,128)(2,1)}, bf16[2,32,1920]{2,1,0:T(8,128)(2,1)}, u32[]{:S(2)}, u32[]{:S(2)}) collective-permute-start(bf16[2,32,1920]{2,1,0:T(8,128)(2,1)} %get-tuple-element.44), channel_id=1, source_target_pairs={{16,0},{18,2},{20,4},{22,6},{24,8},{26,10},{28,12},{30,14},{0,16},... | collective-permute-start | bytes 737288 | tf_op jit(solution)/shard_map/ppermute | solution.py:54
  (137 other events, 2864.0 us)

commit v4 on v3

--- a/solution.py
+++ b/solution.py
@@ -92,7 +92,7 @@
                 out.append(self.shift(piece, 2, d))
         return out
 
-    def gather_rows(self, own, lent):
+    def gather_rows(self, own, lent, turn=()):
         na, nb, nc = self.sizes
         width = own.shape[1]
         keep = width - (self.parts - 1) * lent
@@ -119,8 +119,13 @@
                     piece = row[k]
                     if lent < keep:
                         piece = lax.dynamic_slice_in_dim(piece, lend, lent, 1)
-                    lent_row[k] = self.tensor_shift(piece, h)
+                    if j > 0 and k in turn:
+                        lent_row[k] = self.shift(lent_rows[h][k], 1, j)
+                    else:
+                        lent_row[k] = self.tensor_shift(piece, h)
                 kinds.append(lent_row)
+            if j == 0:
+                lent_rows = kinds
             for h, pieces in enumerate(kinds):
                 plane += [(j * na + k, h, pieces[k]) for k in range(1, na)]
                 group = jnp.concatenate([pieces[k] for k in range(1, na)])
@@ -285,10 +290,10 @@
     )(at, *weights, *small, *values)
 
 
-def input_kernel(index_ref, pre_ref, up_ref, score_ref, wg_ref, wu_ref, out_ref, weights, obuf, wsem, osem):
+def input_kernel(index_ref, pre_ref, up_ref, score_ref, wg_ref, wu_ref, *refs):
     dims = (((1,), (1,)), ((), ()))
-    cores, rows, _ = out_ref.shape
-    steps, block = weights.shape[1:3]
+    *out_refs, weights, obuf, wsem, osem = refs
+    steps, cores, rows, block = obuf.shape
     part = steps * block
     wide = score_ref.shape[1]
 
@@ -298,12 +303,12 @@
 
     def put(c, j):
         cols = pl.ds(pl.multiple_of(j * block, LANES), block)
-        return pltpu.make_async_copy(obuf.at[j, c], out_ref.at[c, :, cols], osem.at[c, j])
+        return pltpu.make_async_copy(obuf.at[j, c], out_refs[c].at[:, cols], osem.at[c, j])
 
     def put_score(c):
         return pltpu.make_async_copy(
             score_ref.at[pl.ds(c * rows, rows), :],
-            out_ref.at[c, :, pl.ds(part, wide)],
+            out_refs[c].at[:, pl.ds(part, wide)],
             osem.at[c, steps],
         )
 
@@ -345,7 +350,7 @@
             num_scalar_prefetch=1,
             grid=(1,),
             in_specs=[full((tokens, hidden)), full((tokens, hidden)), full(score.shape), ANY, ANY],
-            out_specs=ANY,
+            out_specs=[ANY] * cores,
             scratch_shapes=[
                 pltpu.VMEM((2, steps, block, hidden), BF),
                 pltpu.VMEM((steps, cores, rows, block), BF),
@@ -353,33 +358,30 @@
                 pltpu.SemaphoreType.DMA((cores, steps + 1)),
             ],
         ),
-        out_shape=jax.ShapeDtypeStruct((cores, rows, part + LANES), BF),
+        out_shape=[jax.ShapeDtypeStruct((rows, part + LANES), BF)] * cores,
     )(index, pre, up, score, w_gate, w_up)
 
 
-def pick_kernel(place_ref, both_ref, xo_ref, dyo_ref):
-    per, depth, rows = xo_ref.shape
+def pick_kernel(place_ref, features_ref, out_ref):
     dims = (((1,), (1,)), ((), ()))
-    for n in range(per):
-        pick = pick_matrix(place_ref[n], rows)
-        both = lax.dot_general(both_ref[...], pick, dims, preferred_element_type=F32).astype(BF)
-        xo_ref[n] = both[:depth]
-        dyo_ref[n] = both[depth:]
-
-
-def picked(place, x_t, dy_t, rows):
+    for n in range(out_ref.shape[0]):
+        pick = pick_matrix(place_ref[n], out_ref.shape[2])
+        out_ref[n] = lax.dot_general(
+            features_ref[...], pick, dims, preferred_element_type=F32
+        ).astype(BF)
+
+
+def picked(place, features, rows):
     slots, tokens = place.shape
-    depth = x_t.shape[0]
+    depth = features.shape[0]
     per = 4 if slots % 4 == 0 else 1
-    out = jax.ShapeDtypeStruct((slots, depth, rows), BF)
-    both = jnp.concatenate([x_t, dy_t])
     return pl.pallas_call(
         pick_kernel,
         grid=(slots // per,),
-        in_specs=[pl.BlockSpec((per, 1, tokens), lambda s: (s, 0, 0)), full(both.shape)],
-        out_specs=[pl.BlockSpec((per, depth, rows), lambda s: (s, 0, 0))] * 2,
-        out_shape=[out, out],
-    )(place.reshape(slots, 1, tokens), both)
+        in_specs=[pl.BlockSpec((per, 1, tokens), lambda s: (s, 0, 0)), full(features.shape)],
+        out_specs=pl.BlockSpec((per, depth, rows), lambda s: (s, 0, 0)),
+        out_shape=jax.ShapeDtypeStruct((slots, depth, rows), BF),
+    )(place.reshape(slots, 1, tokens), features)
 
 
 def expert_kernel(slots, replicas, first, table_ref, rows_ref, *refs):
@@ -480,12 +482,6 @@
     )(table, *operands)
 
 
-def lent_columns(width, parts, sevenths):
-    if parts > 2:
-        return width // parts
-    return width * sevenths // 7 // LANES * LANES
-
-
 def after(value, *others):
     return lax.optimization_barrier((value, *others))[0]
 
@@ -509,7 +505,7 @@
     )
     meta_all = grid.gather_small(meta).reshape(all_tok, LANES)
     x_pieces = grid.gather_rows(tokens, width // grid.parts)
-    dy_pieces = grid.gather_rows(cotangent, lent_columns(width, grid.parts, 2))
+    dy_pieces = grid.gather_rows(cotangent, width // grid.parts, grid.nearest()[-1:])
 
     ids = grid.ids()
     routes = meta_all[:, :top].astype(jnp.int32)
@@ -541,7 +537,7 @@
         grid.parts,
         tok,
     )
-    down_all = grid.gather(down, together=True)
+    down_all = grid.gather(down)
     pre, upg, pre_rows, upg_rows, score, dy_window = forward_call(
         down_kernel,
         at,
@@ -567,7 +563,7 @@
 
     terms = {}
     for h in [*range(1, grid.parts), 0]:
-        share = input_part(grid, h, pre, upg, score, wg, wu)
+        share = shares = input_part(grid, h, pre, upg, score, wg, wu)
         total = share[0].astype(F32)
         for k in range(1, nc):
             total = total + grid.shift(share[k], 2, -k).astype(F32)
@@ -600,7 +596,7 @@
     own_routes = route_slots[:, :, None] == lane[None, None, :]
     gate_grads = jnp.sum(jnp.where(own_routes, last[:, None, part:], 0.0), axis=2).astype(BF)
 
-    x_window, dy_window = after(x_window, share), after(dy_window, share)
+    dy_window = after(dy_window, *shares)
     x_t = lax.dynamic_slice_in_dim(x_window, first - start, depth, 1).T
     dy_t = lax.dynamic_slice_in_dim(dy_window, first - start, depth, 1).T
     spot = jnp.sum(
@@ -611,7 +607,8 @@
         ),
         axis=1,
     )
-    x_pick, dy_pick = picked(place, x_t, dy_t, rows)
+    x_pick = picked(place, x_t, rows)
+    dy_pick = picked(place, dy_t, rows)
     table = jnp.concatenate([spot, replica_owner]).astype(jnp.int32)
     out = expert_sums(table, dy_pick, down_all, 2, 3, None, replicas)
     out = expert_sums(table, x_pick, pre_all, 0, 3, out, replicas)

time: 419 us -> 425 us (1.014)
  local copies, waits for them, and re-layouts: 23.3 us -> 13.5 us
  starting transfers between devices: 80.1 us -> 85.2 us
  waiting for transfers between devices: 201 us -> 206 us
    ppermute x13 -> x12, waiting for transfers between devices: 19.7 us -> 29 us  [tensor_shift(): lax.ppermute(value, 'tensor', [((i + step) % n, i) for i in range(n)])]
    squeeze x2 -> x0, local copies, waits for them, and re-layouts: 4.7 us -> none  [per_device(): total = total + grid.shift(share[k], 2, -k).astype(F32)]
    unnamed x154 -> x167, local copies, waits for them, and re-layouts: 8.59 us -> 4.7 us
    ppermute x79 -> x87, starting transfers between devices: 65 us -> 68.8 us  [shift(): return lax.ppermute(value, 'expert', pairs)]
    ppermute x79 -> x87, waiting for transfers between devices: 181 us -> 177 us  [shift(): return lax.ppermute(value, 'expert', pairs)]
    pallas_call x1 -> x2, Pallas kernels: 11.1 us -> 13.5 us  [picked(): pl.pallas_call(pick_kernel, grid=(slots // per,), in_specs=[pl.BlockSpec(...]
    ppermute x13 -> x12, starting transfers between devices: 15.2 us -> 16.4 us  [tensor_shift(): lax.ppermute(value, 'tensor', [((i + step) % n, i) for i in range(n)])]
  transfers between devices with their start and end apart: 92 -> 99, of which waited for: 39 -> 39; matrix products, arithmetic and copies ran while one was open for 8% -> 5% of each run, Pallas kernels for 23% -> 23%
where the time goes in v4:
time: 425 us; the launch traced here: 420 us
  waiting for transfers between devices  206 us (48%)
  Pallas kernels  97.5 us (23%)
  starting transfers between devices  85.2 us (20%)
  other arithmetic  15.4 us (4%)
  local copies, waits for them, and re-layouts  13.5 us (3%)
    ppermute x87, waiting for transfers between devices, shift(): return lax.ppermute(value, 'expert', pairs)  177 us
    ppermute x87, starting transfers between devices, shift(): return lax.ppermute(value, 'expert', pairs)  68.8 us
    pallas_call x2, Pallas kernels, forward_call(): pl.pallas_call(body, grid_spec=pltpu.PrefetchScalarGridSpec(num_scalar_pr...  33.3 us
    pallas_call x3, Pallas kernels, expert_sums(): pl.pallas_call(lambda *refs: expert_kernel(slots, replicas, first, *refs)...  33.1 us
    ppermute x12, waiting for transfers between devices, tensor_shift(): lax.ppermute(value, 'tensor', [((i + step) % n, i) for i in range(n)])  29 us
    pallas_call x2, Pallas kernels, input_part(): pl.pallas_call(input_kernel, grid_spec=pltpu.PrefetchScalarGridSpec(num_s...  17.6 us
    ppermute x12, starting transfers between devices, tensor_shift(): lax.ppermute(value, 'tensor', [((i + step) % n, i) for i in range(n)])  16.4 us
    pallas_call x2, Pallas kernels, picked(): pl.pallas_call(pick_kernel, grid=(slots // per,), in_specs=[pl.BlockSpec(...  13.5 us
  transfers between devices with their start and end apart: 99, of which 39 were waited for; matrix products, arithmetic and copies ran while one was open for 5% of the time, Pallas kernels for 23%

profile of v4, /device:TPU:16, one launch (start us, length us, event | category | flops | bytes accessed | tf_op | source)
XLA Modules:
  0.0 419.9 jit_solution(11941081346391254730)
XLA Ops:
  14.7 9.7 %collective-permute-done.3 = bf16[4,32,128]{2,1,0:T(8,128)(2,1)S(1)} collective-permute-done((bf16[4,32,128]{2,1,0:T(8,128)(2,1)S(1)}, bf16[4,32,128]{2,1,0:T(8,128)(2,1)S(1)}, u32[]{:S(2)}, u32[]{:S(2)}) %collective-permute-start.3) | collective-permute-done | bytes 32800 | tf_op jit(solution)/shard_map/ppermute | solution.py:54
  31.7 12.2 %collective-permute-done.25.refs_8_ = bf16[32,3584]{1,0:T(8,128)(2,1)S(1)} collective-permute-done((bf16[32,3584]{1,0:T(8,128)(2,1)S(1)}, bf16[32,3584]{1,0:T(8,128)(2,1)S(1)}, u32[]{:S(2)}, u32[]{:S(2)}) %collective-permute-start.25) | collective-permute-done | bytes 229408 | tf_op jit(solution)/shard_map/ppermute | solution.py:54
  116.8 19.5 %shard_map.103 = (f32[512,512]{1,0:T(8,128)}, f32[512,512]{1,0:T(8,128)}, bf16[384,512]{1,0:T(8,128)(2,1)}, bf16[512,640]{1,0:T(8,128)(2,1)}) custom-call(s32[3]{0:T(128)} %pad_add_fusion.refs_0_, bf16[7168,512]{1,0:T(8,128)(2,1)} %bitcast.83, bf16[7168,512]{1,0:T(8,128)(2,1)} %bitcast.86, f32[512,1]{1,0:T(8,128)} %copy.65.refs_3_.refs_2_, ...), custom_call_target="tpu_custom_call" | custom-call | tf_op jit(solution)/shard_map/pallas_call | solution.py:271
  139.3 13.8 %shard_map.104 = (bf16[512,512]{1,0:T(8,128)(2,1)}, bf16[512,512]{1,0:T(8,128)(2,1)}, bf16[384,512]{1,0:T(8,128)(2,1)}, bf16[384,512]{1,0:T(8,128)(2,1)}, bf16[5...) custom-call(s32[3]{0:T(128)} %pad_add_fusion.refs_0_, bf16[7168,512]{1,0:T(8,128)(2,1)} %bitcast.93, ...), custom_call_target="tpu_custom_call" | custom-call | tf_op jit(solution)/shard_map/pallas_call | solution.py:271
  153.2 8.8 %shard_map.106 = (bf16[256,3712]{1,0:T(8,128)(2,1)}, bf16[256,3712]{1,0:T(8,128)(2,1)}) custom-call(s32[1]{0:T(128)} %bitcast.26.index_ref, bf16[512,512]{1,0:T(8,128)(2,1)} %get-tuple-element.20.pre_ref, bf16[512,512]{1,0:T(8,128)(2,1)} %get-tuple-element.21.up_ref, bf16[512,128]{1,0:T(8,128)(2,1)} %get-tuple-element.22.score_ref, ...), custom_call_target="tpu_custom_call" | custom-call | tf_op jit(solution)/shard_map/pallas_call | solution.py:347
  165.4 9.2 %collective-permute-done.86.refs_5_ = bf16[384,512]{1,0:T(8,128)(2,1)} collective-permute-done((bf16[384,512]{1,0:T(8,128)(2,1)S(1)}, bf16[384,512]{1,0:T(8,128)(2,1)}, u32[]{:S(2)}, u32[]{:S(2)}) %collective-permute-start.86) | collective-permute-done | bytes 393248 | tf_op jit(solution)/shard_map/ppermute | solution.py:54
  177.8 5.2 %collective-permute-done.69.refs_3_ = bf16[384,512]{1,0:T(8,128)(2,1)} collective-permute-done((bf16[384,512]{1,0:T(8,128)(2,1)S(1)}, bf16[384,512]{1,0:T(8,128)(2,1)}, u32[]{:S(2)}, u32[]{:S(2)}) %collective-permute-start.69) | collective-permute-done | bytes 393248 | tf_op jit(solution)/shard_map/ppermute | solution.py:54
  183.0 23.5 %collective-permute-done.70.refs_4_ = bf16[384,512]{1,0:T(8,128)(2,1)S(1)} collective-permute-done((bf16[384,512]{1,0:T(8,128)(2,1)S(1)}, bf16[384,512]{1,0:T(8,128)(2,1)S(1)}, u32[]{:S(2)}, u32[]{:S(2)}) %collective-permute-start.70) | collective-permute-done | bytes 393248 | tf_op jit(solution)/shard_map/ppermute | solution.py:54
  212.8 5.8 %collective-permute-done.54.refs_3_ = bf16[384,512]{1,0:T(8,128)(2,1)} collective-permute-done((bf16[384,512]{1,0:T(8,128)(2,1)S(1)}, bf16[384,512]{1,0:T(8,128)(2,1)}, u32[]{:S(2)}, u32[]{:S(2)}) %collective-permute-start.54) | collective-permute-done | bytes 393248 | tf_op jit(solution)/shard_map/ppermute | solution.py:54
  218.6 22.0 %collective-permute-done.55.refs_4_ = bf16[384,512]{1,0:T(8,128)(2,1)} collective-permute-done((bf16[384,512]{1,0:T(8,128)(2,1)S(1)}, bf16[384,512]{1,0:T(8,128)(2,1)}, u32[]{:S(2)}, u32[]{:S(2)}) %collective-permute-start.55) | collective-permute-done | bytes 393248 | tf_op jit(solution)/shard_map/ppermute | solution.py:54
  247.4 8.8 %shard_map.105 = (bf16[256,3712]{1,0:T(8,128)(2,1)}, bf16[256,3712]{1,0:T(8,128)(2,1)}) custom-call(s32[1]{0:T(128)} %bitcast.index_ref, bf16[512,512]{1,0:T(8,128)(2,1)} %get-tuple-element.20.pre_ref, bf16[512,512]{1,0:T(8,128)(2,1)} %get-tuple-element.21.up_ref, bf16[512,128]{1,0:T(8,128)(2,1)} %get-tuple-element.22.score_ref, bf16[7168,512]{1,0:T(8,128)(2,1)} %bitcast.85, ...), custom_call_target="tpu_custom_call" | custom-call | tf_op jit(solution)/shard_map/pallas_call | solution.py:347
  261.1 6.9 %collective-permute-done.90.refs_9_ = bf16[384,512]{1,0:T(8,128)(2,1)} collective-permute-done((bf16[384,512]{1,0:T(8,128)(2,1)}, bf16[384,512]{1,0:T(8,128)(2,1)}, u32[]{:S(2)}, u32[]{:S(2)}) %collective-permute-start.90) | collective-permute-done | bytes 393248 | tf_op jit(solution)/shard_map/ppermute | solution.py:54
  280.2 8.4 %collective-permute-done.74.refs_8_ = bf16[384,512]{1,0:T(8,128)(2,1)S(1)} collective-permute-done((bf16[384,512]{1,0:T(8,128)(2,1)S(1)}, bf16[384,512]{1,0:T(8,128)(2,1)S(1)}, u32[]{:S(2)}, u32[]{:S(2)}) %collective-permute-start.74) | collective-permute-done | bytes 393248 | tf_op jit(solution)/shard_map/ppermute | solution.py:54
  288.7 8.0 %collective-permute-done.75.refs_9_ = bf16[384,512]{1,0:T(8,128)(2,1)S(1)} collective-permute-done((bf16[384,512]{1,0:T(8,128)(2,1)S(1)}, bf16[384,512]{1,0:T(8,128)(2,1)S(1)}, u32[]{:S(2)}, u32[]{:S(2)}) %collective-permute-start.75) | collective-permute-done | bytes 393248 | tf_op jit(solution)/shard_map/ppermute | solution.py:54
  300.5 9.0 %collective-permute-done.58.refs_7_ = bf16[384,512]{1,0:T(8,128)(2,1)S(1)} collective-permute-done((bf16[384,512]{1,0:T(8,128)(2,1)}, bf16[384,512]{1,0:T(8,128)(2,1)S(1)}, u32[]{:S(2)}, u32[]{:S(2)}) %collective-permute-start.58) | collective-permute-done | bytes 393248 | tf_op jit(solution)/shard_map/ppermute | solution.py:54
  309.4 8.5 %collective-permute-done.59.refs_8_ = bf16[384,512]{1,0:T(8,128)(2,1)} collective-permute-done((bf16[384,512]{1,0:T(8,128)(2,1)}, bf16[384,512]{1,0:T(8,128)(2,1)}, u32[]{:S(2)}, u32[]{:S(2)}) %collective-permute-start.59) | collective-permute-done | bytes 393248 | tf_op jit(solution)/shard_map/ppermute | solution.py:54
  318.0 7.5 %collective-permute-done.60.refs_9_ = bf16[384,512]{1,0:T(8,128)(2,1)} collective-permute-done((bf16[384,512]{1,0:T(8,128)(2,1)}, bf16[384,512]{1,0:T(8,128)(2,1)}, u32[]{:S(2)}, u32[]{:S(2)}) %collective-permute-start.60) | collective-permute-done | bytes 393248 | tf_op jit(solution)/shard_map/ppermute | solution.py:54
  339.1 5.3 %collective-permute-start.52 = (bf16[2,32,1920]{2,1,0:T(8,128)(2,1)}, bf16[2,32,1920]{2,1,0:T(8,128)(2,1)}, u32[]{:S(2)}, u32[]{:S(2)}) collective-permute-start(bf16[2,32,1920]{2,1,0:T(8,128)(2,1)} %get-tuple-element.46), channel_id=1, source_target_pairs={{16,0},{18,2},{20,4},{22,6},{24,8},{26,10},{28,12},{30,14},{0,16},... | collective-permute-start | bytes 737288 | tf_op jit(solution)/shard_map/ppermute | solution.py:54
  345.4 6.7 %shard_map.108.refs_1_ = bf16[16,448,384]{2,1,0:T(8,128)(2,1)} custom-call(s32[16,1,512]{2,1,0:T(1,128)} %reshape.196.place_ref, bf16[448,512]{1,0:T(8,128)(2,1)} %dynamic-slice_bitcast_fusion.features_ref), custom_call_target="tpu_custom_call" | custom-call | tf_op jit(solution)/shard_map/pallas_call | solution.py:378
  353.0 6.8 %shard_map.107.refs_1_ = bf16[16,448,384]{2,1,0:T(8,128)(2,1)} custom-call(s32[16,1,512]{2,1,0:T(1,128)} %reshape.196.place_ref, bf16[448,512]{1,0:T(8,128)(2,1)} %dynamic-slice_bitcast_fusion.1.features_ref), custom_call_target="tpu_custom_call" | custom-call | tf_op jit(solution)/shard_map/pallas_call | solution.py:378
  359.8 11.0 %shard_map.109.refs_18_ = bf16[14,3,448,512]{3,2,1,0:T(8,128)(2,1)} custom-call(s32[18]{0:T(128)} %pad_add_fusion.1.refs_0_, bf16[16,448,384]{2,1,0:T(8,128)(2,1)} %shard_map.108.refs_1_, bf16[384,512]{1,0:T(8,128)(2,1)} %get-tuple-element.32.refs_2_, bf16[384,512]{1,0:T(8,128)(2,1)} %copy-done.40, bf16[384,512]{1,0:T(8,128)(2,1)} %copy-done.41, ...), custom_call_target="tpu_custom_call" | custom-call | tf_op jit(solution)/shard_map/pallas_call | solution.py:464
  370.9 11.0 %shard_map.110.refs_18_ = bf16[14,3,448,512]{3,2,1,0:T(8,128)(2,1)} custom-call(s32[18]{0:T(128)} %pad_add_fusion.1.refs_0_, bf16[16,448,384]{2,1,0:T(8,128)(2,1)} %shard_map.107.refs_1_, bf16[384,512]{1,0:T(8,128)(2,1)} %get-tuple-element.29.refs_2_, bf16[384,512]{1,0:T(8,128)(2,1)} %collective-permute-done.69.refs_3_, ...), custom_call_target="tpu_custom_call", output_to_operand_aliasing={{}: (18, {})} | custom-call | tf_op jit(solution)/shard_map/pallas_call | solution.py:464
  381.9 11.0 %shard_map.111 = bf16[14,3,448,512]{3,2,1,0:T(8,128)(2,1)} custom-call(s32[18]{0:T(128)} %pad_add_fusion.1.refs_0_, bf16[16,448,384]{2,1,0:T(8,128)(2,1)} %shard_map.107.refs_1_, bf16[384,512]{1,0:T(8,128)(2,1)} %get-tuple-element.28.refs_2_, bf16[384,512]{1,0:T(8,128)(2,1)} %collective-permute-done.54.refs_3_, ...), custom_call_target="tpu_custom_call", output_to_operand_aliasing={{}: (18, {})} | custom-call | tf_op jit(solution)/shard_map/pallas_call | solution.py:464
  400.5 8.1 %collective-permute-done.46 = bf16[4,32,1792]{2,1,0:T(8,128)(2,1)S(1)} collective-permute-done((bf16[4,32,1792]{2,1,0:T(8,128)(2,1)S(1)}, bf16[4,32,1792]{2,1,0:T(8,128)(2,1)S(1)}, u32[]{:S(2)}, u32[]{:S(2)}) %collective-permute-start.46) | collective-permute-done | bytes 458784 | tf_op jit(solution)/shard_map/ppermute | solution.py:54
  (400 shorter events, 171.3 us)
Async XLA Ops:
  12.5 57.9 %collective-permute-start.5 = (bf16[32,7168]{1,0:T(8,128)(2,1)S(1)}, bf16[32,7168]{1,0:T(8,128)(2,1)S(1)}, u32[]{:S(2)}, u32[]{:S(2)}) collective-permute-start(bf16[32,7168]{1,0:T(8,128)(2,1)S(1)} %copy-done.2), channel_id=1, source_target_pairs={{4,0},{6,2},{0,4},{2,6},{12,8},{14,10},{8,12},{10,14},{20,16},{22,... | collective-permute-start | bytes 1376264 | tf_op jit(solution)/shard_map/ppermute | solution.py:54
  25.7 46.2 %collective-permute-start.18 = (bf16[32,7168]{1,0:T(8,128)(2,1)S(1)}, bf16[32,7168]{1,0:T(8,128)(2,1)S(1)}, u32[]{:S(2)}, u32[]{:S(2)}) collective-permute-start(bf16[32,7168]{1,0:T(8,128)(2,1)S(1)} %copy-done.2), channel_id=1, source_target_pairs={{2,0},{0,2},{6,4},{4,6},{10,8},{8,10},{14,12},{12,14},{18,16},{16,... | collective-permute-start | bytes 1376264 | tf_op jit(solution)/shard_map/ppermute | solution.py:54
  113.5 25.8 %collective-permute-start.41 = (bf16[96,3584]{1,0:T(8,128)(2,1)}, bf16[96,3584]{1,0:T(8,128)(2,1)}, u32[]{:S(2)}, u32[]{:S(2)}) collective-permute-start(bf16[96,3584]{1,0:T(8,128)(2,1)} %pad_maximum_fusion.6), channel_id=1, source_target_pairs={{2,0},{0,2},{6,4},{4,6},{10,8},{8,10},{14,12},{12,14},{18,16},{16,... | collective-permute-start | bytes 2064392 | tf_op jit(solution)/shard_map/ppermute | solution.py:54
  113.6 25.7 %collective-permute-start.40 = (bf16[96,3584]{1,0:T(8,128)(2,1)}, bf16[96,3584]{1,0:T(8,128)(2,1)}, u32[]{:S(2)}, u32[]{:S(2)}) collective-permute-start(bf16[96,3584]{1,0:T(8,128)(2,1)} %pad_maximum_fusion.5), channel_id=1, source_target_pairs={{2,0},{0,2},{6,4},{4,6},{10,8},{8,10},{14,12},{12,14},{18,16},{16,... | collective-permute-start | bytes 2064392 | tf_op jit(solution)/shard_map/ppermute | solution.py:54
  114.1 25.2 %collective-permute-start.42 = (bf16[96,3584]{1,0:T(8,128)(2,1)}, bf16[96,3584]{1,0:T(8,128)(2,1)}, u32[]{:S(2)}, u32[]{:S(2)}) collective-permute-start(bf16[96,3584]{1,0:T(8,128)(2,1)} %pad_maximum_fusion.7), channel_id=1, source_target_pairs={{2,0},{0,2},{6,4},{4,6},{10,8},{8,10},{14,12},{12,14},{18,16},{16,... | collective-permute-start | bytes 2064392 | tf_op jit(solution)/shard_map/ppermute | solution.py:54
  136.3 28.2 %collective-permute-start.84 = (bf16[384,512]{1,0:T(8,128)(2,1)}, bf16[384,512]{1,0:T(8,128)(2,1)S(1)}, u32[]{:S(2)}, u32[]{:S(2)}) collective-permute-start(bf16[384,512]{1,0:T(8,128)(2,1)} %get-tuple-element.32.refs_2_), channel_id=1, source_target_pairs={{8,0},{10,2},{12,4},{14,6},{16,8},{18,10},{20,12},{22,14},{24,16},... | collective-permute-start | bytes 1179656 | tf_op jit(solution)/shard_map/ppermute | solution.py:54
  136.4 28.1 %collective-permute-start.85 = (bf16[384,512]{1,0:T(8,128)(2,1)}, bf16[384,512]{1,0:T(8,128)(2,1)S(1)}, u32[]{:S(2)}, u32[]{:S(2)}) collective-permute-start(bf16[384,512]{1,0:T(8,128)(2,1)} %get-tuple-element.32.refs_2_), channel_id=1, source_target_pairs={{16,0},{18,2},{20,4},{22,6},{24,8},{26,10},{28,12},{30,14},{0,16},... | collective-permute-start | bytes 1179656 | tf_op jit(solution)/shard_map/ppermute | solution.py:54
  161.9 106.1 %collective-permute-start.44 = (bf16[256,3712]{1,0:T(8,128)(2,1)}, bf16[256,3712]{1,0:T(8,128)(2,1)}, u32[]{:S(2)}, u32[]{:S(2)}) collective-permute-start(bf16[256,3712]{1,0:T(8,128)(2,1)} %get-tuple-element.26), channel_id=1, source_target_pairs={{2,0},{0,2},{6,4},{4,6},{10,8},{8,10},{14,12},{12,14},{18,16},{16,... | collective-permute-start | bytes 5701640 | tf_op jit(solution)/shard_map/ppermute | solution.py:54
  174.6 31.8 %collective-permute-start.70 = (bf16[384,512]{1,0:T(8,128)(2,1)S(1)}, bf16[384,512]{1,0:T(8,128)(2,1)S(1)}, u32[]{:S(2)}, u32[]{:S(2)}) collective-permute-start(bf16[384,512]{1,0:T(8,128)(2,1)S(1)} %copy-done.43), channel_id=1, source_target_pairs={{16,0},{18,2},{20,4},{22,6},{24,8},{26,10},{28,12},{30,14},{0,16},... | collective-permute-start | bytes 1179656 | tf_op jit(solution)/shard_map/ppermute | solution.py:54
  176.9 31.0 %collective-permute-start.71 = (bf16[384,512]{1,0:T(8,128)(2,1)S(1)}, bf16[384,512]{1,0:T(8,128)(2,1)S(1)}, u32[]{:S(2)}, u32[]{:S(2)}) collective-permute-start(bf16[384,512]{1,0:T(8,128)(2,1)S(1)} %copy-done.43), channel_id=1, source_target_pairs={{24,0},{26,2},{28,4},{30,6},{0,8},{2,10},{4,12},{6,14},{8,16},{10,... | collective-permute-start | bytes 1179656 | tf_op jit(solution)/shard_map/ppermute | solution.py:54
  176.9 33.0 %collective-permute-start.72 = (bf16[384,512]{1,0:T(8,128)(2,1)S(1)}, bf16[384,512]{1,0:T(8,128)(2,1)S(1)}, u32[]{:S(2)}, u32[]{:S(2)}) collective-permute-start(bf16[384,512]{1,0:T(8,128)(2,1)S(1)} %copy-done.43), channel_id=1, source_target_pairs={{4,0},{6,2},{0,4},{2,6},{12,8},{14,10},{8,12},{10,14},{20,16},{22,... | collective-permute-start | bytes 1179656 | tf_op jit(solution)/shard_map/ppermute | solution.py:54
  183.0 29.0 %collective-permute-start.76 = (bf16[384,512]{1,0:T(8,128)(2,1)S(1)}, bf16[384,512]{1,0:T(8,128)(2,1)S(1)}, u32[]{:S(2)}, u32[]{:S(2)}) collective-permute-start(bf16[384,512]{1,0:T(8,128)(2,1)S(1)} %copy-done.43), channel_id=1, source_target_pairs={{2,0},{0,2},{6,4},{4,6},{10,8},{8,10},{14,12},{12,14},{18,16},{16,... | collective-permute-start | bytes 1179656 | tf_op jit(solution)/shard_map/ppermute | solution.py:54
  207.9 32.7 %collective-permute-start.55 = (bf16[384,512]{1,0:T(8,128)(2,1)S(1)}, bf16[384,512]{1,0:T(8,128)(2,1)}, u32[]{:S(2)}, u32[]{:S(2)}) collective-permute-start(bf16[384,512]{1,0:T(8,128)(2,1)S(1)} %copy-done.42), channel_id=1, source_target_pairs={{16,0},{18,2},{20,4},{22,6},{24,8},{26,10},{28,12},{30,14},{0,16},... | collective-permute-start | bytes 1179656 | tf_op jit(solution)/shard_map/ppermute | solution.py:54
  210.0 34.6 %collective-permute-start.56 = (bf16[384,512]{1,0:T(8,128)(2,1)S(1)}, bf16[384,512]{1,0:T(8,128)(2,1)}, u32[]{:S(2)}, u32[]{:S(2)}) collective-permute-start(bf16[384,512]{1,0:T(8,128)(2,1)S(1)} %copy-done.42), channel_id=1, source_target_pairs={{24,0},{26,2},{28,4},{30,6},{0,8},{2,10},{4,12},{6,14},{8,16},{10,... | collective-permute-start | bytes 1179656 | tf_op jit(solution)/shard_map/ppermute | solution.py:54
  211.9 33.6 %collective-permute-start.57 = (bf16[384,512]{1,0:T(8,128)(2,1)S(1)}, bf16[384,512]{1,0:T(8,128)(2,1)S(1)}, u32[]{:S(2)}, u32[]{:S(2)}) collective-permute-start(bf16[384,512]{1,0:T(8,128)(2,1)S(1)} %copy-done.42), channel_id=1, source_target_pairs={{4,0},{6,2},{0,4},{2,6},{12,8},{14,10},{8,12},{10,14},{20,16},{22,... | collective-permute-start | bytes 1179656 | tf_op jit(solution)/shard_map/ppermute | solution.py:54
  218.6 37.6 %collective-permute-start.61 = (bf16[384,512]{1,0:T(8,128)(2,1)S(1)}, bf16[384,512]{1,0:T(8,128)(2,1)}, u32[]{:S(2)}, u32[]{:S(2)}) collective-permute-start(bf16[384,512]{1,0:T(8,128)(2,1)S(1)} %copy-done.42), channel_id=1, source_target_pairs={{2,0},{0,2},{6,4},{4,6},{10,8},{8,10},{14,12},{12,14},{18,16},{16,... | collective-permute-start | bytes 1179656 | tf_op jit(solution)/shard_map/ppermute | solution.py:54
  272.4 57.4 %collective-permute-start.43 = (bf16[256,3712]{1,0:T(8,128)(2,1)}, bf16[256,3712]{1,0:T(8,128)(2,1)S(1)}, u32[]{:S(2)}, u32[]{:S(2)}) collective-permute-start(bf16[256,3712]{1,0:T(8,128)(2,1)} %get-tuple-element.24), channel_id=1, source_target_pairs={{2,0},{0,2},{6,4},{4,6},{10,8},{8,10},{14,12},{12,14},{18,16},{16,... | collective-permute-start | bytes 5701640 | tf_op jit(solution)/shard_map/ppermute | solution.py:54
  272.6 57.2 %collective-permute-start.45 = (bf16[256,3712]{1,0:T(8,128)(2,1)}, bf16[256,3712]{1,0:T(8,128)(2,1)}, u32[]{:S(2)}, u32[]{:S(2)}) collective-permute-start(bf16[256,3712]{1,0:T(8,128)(2,1)} %add_convert_fusion.1), channel_id=1, source_target_pairs={{1,0},{0,1},{3,2},{2,3},{5,4},{4,5},{7,6},{6,7},{9,8},{8,9},{11,10... | collective-permute-start | bytes 5701640 | tf_op jit(solution)/shard_map/ppermute | solution.py:58
  299.3 26.2 %collective-permute-start.60 = (bf16[384,512]{1,0:T(8,128)(2,1)}, bf16[384,512]{1,0:T(8,128)(2,1)}, u32[]{:S(2)}, u32[]{:S(2)}) collective-permute-start(bf16[384,512]{1,0:T(8,128)(2,1)} %collective-permute-done.56.refs_5_), channel_id=1, source_target_pairs={{4,0},{6,2},{0,4},{2,6},{12,8},{14,10},{8,12},{10,14},{20,16},{22,... | collective-permute-start | bytes 1179656 | tf_op jit(solution)/shard_map/ppermute | solution.py:54
  335.6 46.3 %collective-permute-start.67 = (bf16[384,512]{1,0:T(8,128)(2,1)}, bf16[384,512]{1,0:T(8,128)(2,1)}, u32[]{:S(2)}, u32[]{:S(2)}) collective-permute-start(bf16[384,512]{1,0:T(8,128)(2,1)} %collective-permute-done.59.refs_8_), channel_id=1, source_target_pairs={{2,0},{0,2},{6,4},{4,6},{10,8},{8,10},{14,12},{12,14},{18,16},{16,... | collective-permute-start | bytes 1179656 | tf_op jit(solution)/shard_map/ppermute | solution.py:54
  335.7 46.2 %collective-permute-start.68 = (bf16[384,512]{1,0:T(8,128)(2,1)}, bf16[384,512]{1,0:T(8,128)(2,1)}, u32[]{:S(2)}, u32[]{:S(2)}) collective-permute-start(bf16[384,512]{1,0:T(8,128)(2,1)} %collective-permute-done.60.refs_9_), channel_id=1, source_target_pairs={{2,0},{0,2},{6,4},{4,6},{10,8},{8,10},{14,12},{12,14},{18,16},{16,... | collective-permute-start | bytes 1179656 | tf_op jit(solution)/shard_map/ppermute | solution.py:54
  337.1 55.9 %collective-permute-start.50 = (bf16[2,32,1920]{2,1,0:T(8,128)(2,1)}, bf16[2,32,1920]{2,1,0:T(8,128)(2,1)S(1)}, u32[]{:S(2)}, u32[]{:S(2)}) collective-permute-start(bf16[2,32,1920]{2,1,0:T(8,128)(2,1)} %get-tuple-element.44), channel_id=1, source_target_pairs={{24,0},{26,2},{28,4},{30,6},{0,8},{2,10},{4,12},{6,14},{8,16},{10,... | collective-permute-start | bytes 737288 | tf_op jit(solution)/shard_map/ppermute | solution.py:54
  337.1 55.9 %collective-permute-start.51 = (bf16[2,32,1920]{2,1,0:T(8,128)(2,1)}, bf16[2,32,1920]{2,1,0:T(8,128)(2,1)}, u32[]{:S(2)}, u32[]{:S(2)}) collective-permute-start(bf16[2,32,1920]{2,1,0:T(8,128)(2,1)} %get-tuple-element.45), channel_id=1, source_target_pairs={{8,0},{10,2},{12,4},{14,6},{16,8},{18,10},{20,12},{22,14},{24,16},... | collective-permute-start | bytes 737288 | tf_op jit(solution)/shard_map/ppermute | solution.py:54
  339.1 53.9 %collective-permute-start.52 = (bf16[2,32,1920]{2,1,0:T(8,128)(2,1)}, bf16[2,32,1920]{2,1,0:T(8,128)(2,1)}, u32[]{:S(2)}, u32[]{:S(2)}) collective-permute-start(bf16[2,32,1920]{2,1,0:T(8,128)(2,1)} %get-tuple-element.46), channel_id=1, source_target_pairs={{16,0},{18,2},{20,4},{22,6},{24,8},{26,10},{28,12},{30,14},{0,16},... | collective-permute-start | bytes 737288 | tf_op jit(solution)/shard_map/ppermute | solution.py:54
  (154 other events, 2656.5 us)

commit v5 on v4

--- a/solution.py
+++ b/solution.py
@@ -590,11 +590,13 @@
         left_sum = left_sum + grid.shift(left_line[k], 0, -k).astype(F32)
     for k in range(1, nb):
         right_sum = right_sum + grid.shift(right_line[k], 1, -k).astype(F32)
-    last = jnp.concatenate([left_sum, right_sum], axis=1)
-    input_grads = last[:, :part].astype(BF)
+    scores = right_sum[:, part - half :]
+    input_grads = jnp.concatenate(
+        [left_sum.astype(BF), right_sum[:, : part - half].astype(BF)], axis=1
+    )
     lane = jnp.arange(LANES, dtype=jnp.int32)
     own_routes = route_slots[:, :, None] == lane[None, None, :]
-    gate_grads = jnp.sum(jnp.where(own_routes, last[:, None, part:], 0.0), axis=2).astype(BF)
+    gate_grads = jnp.sum(jnp.where(own_routes, scores[:, None, :], 0.0), axis=2).astype(BF)
 
     dy_window = after(dy_window, *shares)
     x_t = lax.dynamic_slice_in_dim(x_window, first - start, depth, 1).T

time: 425 us -> 425 us (level)
  no operation moved by 1% of the time
where the time goes in v5:
time: 425 us; the launch traced here: 420 us
  waiting for transfers between devices  206 us (48%)
  Pallas kernels  97.6 us (23%)
  starting transfers between devices  85.3 us (20%)
  other arithmetic  15.3 us (4%)
  local copies, waits for them, and re-layouts  13.6 us (3%)
    ppermute x87, waiting for transfers between devices, shift(): return lax.ppermute(value, 'expert', pairs)  177 us
    ppermute x87, starting transfers between devices, shift(): return lax.ppermute(value, 'expert', pairs)  68.9 us
    pallas_call x2, Pallas kernels, forward_call(): pl.pallas_call(body, grid_spec=pltpu.PrefetchScalarGridSpec(num_scalar_pr...  33.3 us
    pallas_call x3, Pallas kernels, expert_sums(): pl.pallas_call(lambda *refs: expert_kernel(slots, replicas, first, *refs)...  33.1 us
    ppermute x12, waiting for transfers between devices, tensor_shift(): lax.ppermute(value, 'tensor', [((i + step) % n, i) for i in range(n)])  29 us
    pallas_call x2, Pallas kernels, input_part(): pl.pallas_call(input_kernel, grid_spec=pltpu.PrefetchScalarGridSpec(num_s...  17.6 us
    ppermute x12, starting transfers between devices, tensor_shift(): lax.ppermute(value, 'tensor', [((i + step) % n, i) for i in range(n)])  16.4 us
    pallas_call x2, Pallas kernels, picked(): pl.pallas_call(pick_kernel, grid=(slots // per,), in_specs=[pl.BlockSpec(...  13.5 us
  transfers between devices with their start and end apart: 99, of which 39 were waited for; matrix products, arithmetic and copies ran while one was open for 5% of the time, Pallas kernels for 23%

profile of v5, /device:TPU:16, one launch (start us, length us, event | category | flops | bytes accessed | tf_op | source)
XLA Modules:
  0.0 420.0 jit_solution(16939624900359572558)
XLA Ops:
  14.7 9.7 %collective-permute-done.3 = bf16[4,32,128]{2,1,0:T(8,128)(2,1)S(1)} collective-permute-done((bf16[4,32,128]{2,1,0:T(8,128)(2,1)S(1)}, bf16[4,32,128]{2,1,0:T(8,128)(2,1)S(1)}, u32[]{:S(2)}, u32[]{:S(2)}) %collective-permute-start.3) | collective-permute-done | bytes 32800 | tf_op jit(solution)/shard_map/ppermute | solution.py:54
  31.7 12.2 %collective-permute-done.25.refs_8_ = bf16[32,3584]{1,0:T(8,128)(2,1)S(1)} collective-permute-done((bf16[32,3584]{1,0:T(8,128)(2,1)S(1)}, bf16[32,3584]{1,0:T(8,128)(2,1)S(1)}, u32[]{:S(2)}, u32[]{:S(2)}) %collective-permute-start.25) | collective-permute-done | bytes 229408 | tf_op jit(solution)/shard_map/ppermute | solution.py:54
  116.8 19.5 %shard_map.103 = (f32[512,512]{1,0:T(8,128)}, f32[512,512]{1,0:T(8,128)}, bf16[384,512]{1,0:T(8,128)(2,1)}, bf16[512,640]{1,0:T(8,128)(2,1)}) custom-call(s32[3]{0:T(128)} %pad_add_fusion.refs_0_, bf16[7168,512]{1,0:T(8,128)(2,1)} %bitcast.81, bf16[7168,512]{1,0:T(8,128)(2,1)} %bitcast.84, f32[512,1]{1,0:T(8,128)} %copy.65.refs_3_.refs_2_, ...), custom_call_target="tpu_custom_call" | custom-call | tf_op jit(solution)/shard_map/pallas_call | solution.py:271
  139.3 13.8 %shard_map.104 = (bf16[512,512]{1,0:T(8,128)(2,1)}, bf16[512,512]{1,0:T(8,128)(2,1)}, bf16[384,512]{1,0:T(8,128)(2,1)}, bf16[384,512]{1,0:T(8,128)(2,1)}, bf16[5...) custom-call(s32[3]{0:T(128)} %pad_add_fusion.refs_0_, bf16[7168,512]{1,0:T(8,128)(2,1)} %bitcast.91, ...), custom_call_target="tpu_custom_call" | custom-call | tf_op jit(solution)/shard_map/pallas_call | solution.py:271
  153.2 8.8 %shard_map.106 = (bf16[256,3712]{1,0:T(8,128)(2,1)}, bf16[256,3712]{1,0:T(8,128)(2,1)}) custom-call(s32[1]{0:T(128)} %bitcast.26.index_ref, bf16[512,512]{1,0:T(8,128)(2,1)} %get-tuple-element.20.pre_ref, bf16[512,512]{1,0:T(8,128)(2,1)} %get-tuple-element.21.up_ref, bf16[512,128]{1,0:T(8,128)(2,1)} %get-tuple-element.22.score_ref, ...), custom_call_target="tpu_custom_call" | custom-call | tf_op jit(solution)/shard_map/pallas_call | solution.py:347
  165.4 9.2 %collective-permute-done.86.refs_5_ = bf16[384,512]{1,0:T(8,128)(2,1)} collective-permute-done((bf16[384,512]{1,0:T(8,128)(2,1)S(1)}, bf16[384,512]{1,0:T(8,128)(2,1)}, u32[]{:S(2)}, u32[]{:S(2)}) %collective-permute-start.86) | collective-permute-done | bytes 393248 | tf_op jit(solution)/shard_map/ppermute | solution.py:54
  177.8 5.2 %collective-permute-done.69.refs_3_ = bf16[384,512]{1,0:T(8,128)(2,1)} collective-permute-done((bf16[384,512]{1,0:T(8,128)(2,1)S(1)}, bf16[384,512]{1,0:T(8,128)(2,1)}, u32[]{:S(2)}, u32[]{:S(2)}) %collective-permute-start.69) | collective-permute-done | bytes 393248 | tf_op jit(solution)/shard_map/ppermute | solution.py:54
  183.0 23.5 %collective-permute-done.70.refs_4_ = bf16[384,512]{1,0:T(8,128)(2,1)S(1)} collective-permute-done((bf16[384,512]{1,0:T(8,128)(2,1)S(1)}, bf16[384,512]{1,0:T(8,128)(2,1)S(1)}, u32[]{:S(2)}, u32[]{:S(2)}) %collective-permute-start.70) | collective-permute-done | bytes 393248 | tf_op jit(solution)/shard_map/ppermute | solution.py:54
  212.8 5.8 %collective-permute-done.54.refs_3_ = bf16[384,512]{1,0:T(8,128)(2,1)} collective-permute-done((bf16[384,512]{1,0:T(8,128)(2,1)S(1)}, bf16[384,512]{1,0:T(8,128)(2,1)}, u32[]{:S(2)}, u32[]{:S(2)}) %collective-permute-start.54) | collective-permute-done | bytes 393248 | tf_op jit(solution)/shard_map/ppermute | solution.py:54
  218.6 22.0 %collective-permute-done.55.refs_4_ = bf16[384,512]{1,0:T(8,128)(2,1)} collective-permute-done((bf16[384,512]{1,0:T(8,128)(2,1)S(1)}, bf16[384,512]{1,0:T(8,128)(2,1)}, u32[]{:S(2)}, u32[]{:S(2)}) %collective-permute-start.55) | collective-permute-done | bytes 393248 | tf_op jit(solution)/shard_map/ppermute | solution.py:54
  247.5 8.8 %shard_map.105 = (bf16[256,3712]{1,0:T(8,128)(2,1)}, bf16[256,3712]{1,0:T(8,128)(2,1)}) custom-call(s32[1]{0:T(128)} %bitcast.index_ref, bf16[512,512]{1,0:T(8,128)(2,1)} %get-tuple-element.20.pre_ref, bf16[512,512]{1,0:T(8,128)(2,1)} %get-tuple-element.21.up_ref, bf16[512,128]{1,0:T(8,128)(2,1)} %get-tuple-element.22.score_ref, bf16[7168,512]{1,0:T(8,128)(2,1)} %bitcast.83, ...), custom_call_target="tpu_custom_call" | custom-call | tf_op jit(solution)/shard_map/pallas_call | solution.py:347
  261.2 6.9 %collective-permute-done.90.refs_9_ = bf16[384,512]{1,0:T(8,128)(2,1)} collective-permute-done((bf16[384,512]{1,0:T(8,128)(2,1)}, bf16[384,512]{1,0:T(8,128)(2,1)}, u32[]{:S(2)}, u32[]{:S(2)}) %collective-permute-start.90) | collective-permute-done | bytes 393248 | tf_op jit(solution)/shard_map/ppermute | solution.py:54
  280.3 8.4 %collective-permute-done.74.refs_8_ = bf16[384,512]{1,0:T(8,128)(2,1)S(1)} collective-permute-done((bf16[384,512]{1,0:T(8,128)(2,1)S(1)}, bf16[384,512]{1,0:T(8,128)(2,1)S(1)}, u32[]{:S(2)}, u32[]{:S(2)}) %collective-permute-start.74) | collective-permute-done | bytes 393248 | tf_op jit(solution)/shard_map/ppermute | solution.py:54
  288.7 8.0 %collective-permute-done.75.refs_9_ = bf16[384,512]{1,0:T(8,128)(2,1)S(1)} collective-permute-done((bf16[384,512]{1,0:T(8,128)(2,1)S(1)}, bf16[384,512]{1,0:T(8,128)(2,1)S(1)}, u32[]{:S(2)}, u32[]{:S(2)}) %collective-permute-start.75) | collective-permute-done | bytes 393248 | tf_op jit(solution)/shard_map/ppermute | solution.py:54
  300.5 9.0 %collective-permute-done.58.refs_7_ = bf16[384,512]{1,0:T(8,128)(2,1)S(1)} collective-permute-done((bf16[384,512]{1,0:T(8,128)(2,1)}, bf16[384,512]{1,0:T(8,128)(2,1)S(1)}, u32[]{:S(2)}, u32[]{:S(2)}) %collective-permute-start.58) | collective-permute-done | bytes 393248 | tf_op jit(solution)/shard_map/ppermute | solution.py:54
  309.5 8.5 %collective-permute-done.59.refs_8_ = bf16[384,512]{1,0:T(8,128)(2,1)} collective-permute-done((bf16[384,512]{1,0:T(8,128)(2,1)}, bf16[384,512]{1,0:T(8,128)(2,1)}, u32[]{:S(2)}, u32[]{:S(2)}) %collective-permute-start.59) | collective-permute-done | bytes 393248 | tf_op jit(solution)/shard_map/ppermute | solution.py:54
  318.0 7.5 %collective-permute-done.60.refs_9_ = bf16[384,512]{1,0:T(8,128)(2,1)} collective-permute-done((bf16[384,512]{1,0:T(8,128)(2,1)}, bf16[384,512]{1,0:T(8,128)(2,1)}, u32[]{:S(2)}, u32[]{:S(2)}) %collective-permute-start.60) | collective-permute-done | bytes 393248 | tf_op jit(solution)/shard_map/ppermute | solution.py:54
  339.2 5.3 %collective-permute-start.52 = (bf16[2,32,1920]{2,1,0:T(8,128)(2,1)}, bf16[2,32,1920]{2,1,0:T(8,128)(2,1)}, u32[]{:S(2)}, u32[]{:S(2)}) collective-permute-start(bf16[2,32,1920]{2,1,0:T(8,128)(2,1)} %get-tuple-element.46), channel_id=1, source_target_pairs={{16,0},{18,2},{20,4},{22,6},{24,8},{26,10},{28,12},{30,14},{0,16},... | collective-permute-start | bytes 737288 | tf_op jit(solution)/shard_map/ppermute | solution.py:54
  345.5 6.7 %shard_map.108.refs_1_ = bf16[16,448,384]{2,1,0:T(8,128)(2,1)} custom-call(s32[16,1,512]{2,1,0:T(1,128)} %reshape.196.place_ref, bf16[448,512]{1,0:T(8,128)(2,1)} %dynamic-slice_bitcast_fusion.features_ref), custom_call_target="tpu_custom_call" | custom-call | tf_op jit(solution)/shard_map/pallas_call | solution.py:378
  353.1 6.8 %shard_map.107.refs_1_ = bf16[16,448,384]{2,1,0:T(8,128)(2,1)} custom-call(s32[16,1,512]{2,1,0:T(1,128)} %reshape.196.place_ref, bf16[448,512]{1,0:T(8,128)(2,1)} %dynamic-slice_bitcast_fusion.1.features_ref), custom_call_target="tpu_custom_call" | custom-call | tf_op jit(solution)/shard_map/pallas_call | solution.py:378
  359.9 11.0 %shard_map.109.refs_18_ = bf16[14,3,448,512]{3,2,1,0:T(8,128)(2,1)} custom-call(s32[18]{0:T(128)} %pad_add_fusion.1.refs_0_, bf16[16,448,384]{2,1,0:T(8,128)(2,1)} %shard_map.108.refs_1_, bf16[384,512]{1,0:T(8,128)(2,1)} %get-tuple-element.32.refs_2_, bf16[384,512]{1,0:T(8,128)(2,1)} %copy-done.40, bf16[384,512]{1,0:T(8,128)(2,1)} %copy-done.41, ...), custom_call_target="tpu_custom_call" | custom-call | tf_op jit(solution)/shard_map/pallas_call | solution.py:464
  370.9 11.0 %shard_map.110.refs_18_ = bf16[14,3,448,512]{3,2,1,0:T(8,128)(2,1)} custom-call(s32[18]{0:T(128)} %pad_add_fusion.1.refs_0_, bf16[16,448,384]{2,1,0:T(8,128)(2,1)} %shard_map.107.refs_1_, bf16[384,512]{1,0:T(8,128)(2,1)} %get-tuple-element.29.refs_2_, bf16[384,512]{1,0:T(8,128)(2,1)} %collective-permute-done.69.refs_3_, ...), custom_call_target="tpu_custom_call", output_to_operand_aliasing={{}: (18, {})} | custom-call | tf_op jit(solution)/shard_map/pallas_call | solution.py:464
  382.0 11.0 %shard_map.111 = bf16[14,3,448,512]{3,2,1,0:T(8,128)(2,1)} custom-call(s32[18]{0:T(128)} %pad_add_fusion.1.refs_0_, bf16[16,448,384]{2,1,0:T(8,128)(2,1)} %shard_map.107.refs_1_, bf16[384,512]{1,0:T(8,128)(2,1)} %get-tuple-element.28.refs_2_, bf16[384,512]{1,0:T(8,128)(2,1)} %collective-permute-done.54.refs_3_, ...), custom_call_target="tpu_custom_call", output_to_operand_aliasing={{}: (18, {})} | custom-call | tf_op jit(solution)/shard_map/pallas_call | solution.py:464
  400.6 8.1 %collective-permute-done.46 = bf16[4,32,1792]{2,1,0:T(8,128)(2,1)S(1)} collective-permute-done((bf16[4,32,1792]{2,1,0:T(8,128)(2,1)S(1)}, bf16[4,32,1792]{2,1,0:T(8,128)(2,1)S(1)}, u32[]{:S(2)}, u32[]{:S(2)}) %collective-permute-start.46) | collective-permute-done | bytes 458784 | tf_op jit(solution)/shard_map/ppermute | solution.py:54
  (401 shorter events, 171.4 us)
Async XLA Ops:
  12.5 57.9 %collective-permute-start.5 = (bf16[32,7168]{1,0:T(8,128)(2,1)S(1)}, bf16[32,7168]{1,0:T(8,128)(2,1)S(1)}, u32[]{:S(2)}, u32[]{:S(2)}) collective-permute-start(bf16[32,7168]{1,0:T(8,128)(2,1)S(1)} %copy-done.2), channel_id=1, source_target_pairs={{4,0},{6,2},{0,4},{2,6},{12,8},{14,10},{8,12},{10,14},{20,16},{22,... | collective-permute-start | bytes 1376264 | tf_op jit(solution)/shard_map/ppermute | solution.py:54
  25.7 46.2 %collective-permute-start.18 = (bf16[32,7168]{1,0:T(8,128)(2,1)S(1)}, bf16[32,7168]{1,0:T(8,128)(2,1)S(1)}, u32[]{:S(2)}, u32[]{:S(2)}) collective-permute-start(bf16[32,7168]{1,0:T(8,128)(2,1)S(1)} %copy-done.2), channel_id=1, source_target_pairs={{2,0},{0,2},{6,4},{4,6},{10,8},{8,10},{14,12},{12,14},{18,16},{16,... | collective-permute-start | bytes 1376264 | tf_op jit(solution)/shard_map/ppermute | solution.py:54
  113.5 25.8 %collective-permute-start.41 = (bf16[96,3584]{1,0:T(8,128)(2,1)}, bf16[96,3584]{1,0:T(8,128)(2,1)}, u32[]{:S(2)}, u32[]{:S(2)}) collective-permute-start(bf16[96,3584]{1,0:T(8,128)(2,1)} %pad_maximum_fusion.6), channel_id=1, source_target_pairs={{2,0},{0,2},{6,4},{4,6},{10,8},{8,10},{14,12},{12,14},{18,16},{16,... | collective-permute-start | bytes 2064392 | tf_op jit(solution)/shard_map/ppermute | solution.py:54
  113.6 25.7 %collective-permute-start.40 = (bf16[96,3584]{1,0:T(8,128)(2,1)}, bf16[96,3584]{1,0:T(8,128)(2,1)}, u32[]{:S(2)}, u32[]{:S(2)}) collective-permute-start(bf16[96,3584]{1,0:T(8,128)(2,1)} %pad_maximum_fusion.5), channel_id=1, source_target_pairs={{2,0},{0,2},{6,4},{4,6},{10,8},{8,10},{14,12},{12,14},{18,16},{16,... | collective-permute-start | bytes 2064392 | tf_op jit(solution)/shard_map/ppermute | solution.py:54
  114.1 25.2 %collective-permute-start.42 = (bf16[96,3584]{1,0:T(8,128)(2,1)}, bf16[96,3584]{1,0:T(8,128)(2,1)}, u32[]{:S(2)}, u32[]{:S(2)}) collective-permute-start(bf16[96,3584]{1,0:T(8,128)(2,1)} %pad_maximum_fusion.7), channel_id=1, source_target_pairs={{2,0},{0,2},{6,4},{4,6},{10,8},{8,10},{14,12},{12,14},{18,16},{16,... | collective-permute-start | bytes 2064392 | tf_op jit(solution)/shard_map/ppermute | solution.py:54
  136.3 28.2 %collective-permute-start.84 = (bf16[384,512]{1,0:T(8,128)(2,1)}, bf16[384,512]{1,0:T(8,128)(2,1)S(1)}, u32[]{:S(2)}, u32[]{:S(2)}) collective-permute-start(bf16[384,512]{1,0:T(8,128)(2,1)} %get-tuple-element.32.refs_2_), channel_id=1, source_target_pairs={{8,0},{10,2},{12,4},{14,6},{16,8},{18,10},{20,12},{22,14},{24,16},... | collective-permute-start | bytes 1179656 | tf_op jit(solution)/shard_map/ppermute | solution.py:54
  136.4 28.2 %collective-permute-start.85 = (bf16[384,512]{1,0:T(8,128)(2,1)}, bf16[384,512]{1,0:T(8,128)(2,1)S(1)}, u32[]{:S(2)}, u32[]{:S(2)}) collective-permute-start(bf16[384,512]{1,0:T(8,128)(2,1)} %get-tuple-element.32.refs_2_), channel_id=1, source_target_pairs={{16,0},{18,2},{20,4},{22,6},{24,8},{26,10},{28,12},{30,14},{0,16},... | collective-permute-start | bytes 1179656 | tf_op jit(solution)/shard_map/ppermute | solution.py:54
  162.0 106.1 %collective-permute-start.44 = (bf16[256,3712]{1,0:T(8,128)(2,1)}, bf16[256,3712]{1,0:T(8,128)(2,1)}, u32[]{:S(2)}, u32[]{:S(2)}) collective-permute-start(bf16[256,3712]{1,0:T(8,128)(2,1)} %get-tuple-element.26), channel_id=1, source_target_pairs={{2,0},{0,2},{6,4},{4,6},{10,8},{8,10},{14,12},{12,14},{18,16},{16,... | collective-permute-start | bytes 5701640 | tf_op jit(solution)/shard_map/ppermute | solution.py:54
  174.6 31.9 %collective-permute-start.70 = (bf16[384,512]{1,0:T(8,128)(2,1)S(1)}, bf16[384,512]{1,0:T(8,128)(2,1)S(1)}, u32[]{:S(2)}, u32[]{:S(2)}) collective-permute-start(bf16[384,512]{1,0:T(8,128)(2,1)S(1)} %copy-done.43), channel_id=1, source_target_pairs={{16,0},{18,2},{20,4},{22,6},{24,8},{26,10},{28,12},{30,14},{0,16},... | collective-permute-start | bytes 1179656 | tf_op jit(solution)/shard_map/ppermute | solution.py:54
  177.0 31.0 %collective-permute-start.71 = (bf16[384,512]{1,0:T(8,128)(2,1)S(1)}, bf16[384,512]{1,0:T(8,128)(2,1)S(1)}, u32[]{:S(2)}, u32[]{:S(2)}) collective-permute-start(bf16[384,512]{1,0:T(8,128)(2,1)S(1)} %copy-done.43), channel_id=1, source_target_pairs={{24,0},{26,2},{28,4},{30,6},{0,8},{2,10},{4,12},{6,14},{8,16},{10,... | collective-permute-start | bytes 1179656 | tf_op jit(solution)/shard_map/ppermute | solution.py:54
  177.0 33.0 %collective-permute-start.72 = (bf16[384,512]{1,0:T(8,128)(2,1)S(1)}, bf16[384,512]{1,0:T(8,128)(2,1)S(1)}, u32[]{:S(2)}, u32[]{:S(2)}) collective-permute-start(bf16[384,512]{1,0:T(8,128)(2,1)S(1)} %copy-done.43), channel_id=1, source_target_pairs={{4,0},{6,2},{0,4},{2,6},{12,8},{14,10},{8,12},{10,14},{20,16},{22,... | collective-permute-start | bytes 1179656 | tf_op jit(solution)/shard_map/ppermute | solution.py:54
  183.0 28.9 %collective-permute-start.76 = (bf16[384,512]{1,0:T(8,128)(2,1)S(1)}, bf16[384,512]{1,0:T(8,128)(2,1)S(1)}, u32[]{:S(2)}, u32[]{:S(2)}) collective-permute-start(bf16[384,512]{1,0:T(8,128)(2,1)S(1)} %copy-done.43), channel_id=1, source_target_pairs={{2,0},{0,2},{6,4},{4,6},{10,8},{8,10},{14,12},{12,14},{18,16},{16,... | collective-permute-start | bytes 1179656 | tf_op jit(solution)/shard_map/ppermute | solution.py:54
  208.0 32.7 %collective-permute-start.55 = (bf16[384,512]{1,0:T(8,128)(2,1)S(1)}, bf16[384,512]{1,0:T(8,128)(2,1)}, u32[]{:S(2)}, u32[]{:S(2)}) collective-permute-start(bf16[384,512]{1,0:T(8,128)(2,1)S(1)} %copy-done.42), channel_id=1, source_target_pairs={{16,0},{18,2},{20,4},{22,6},{24,8},{26,10},{28,12},{30,14},{0,16},... | collective-permute-start | bytes 1179656 | tf_op jit(solution)/shard_map/ppermute | solution.py:54
  210.0 34.6 %collective-permute-start.56 = (bf16[384,512]{1,0:T(8,128)(2,1)S(1)}, bf16[384,512]{1,0:T(8,128)(2,1)}, u32[]{:S(2)}, u32[]{:S(2)}) collective-permute-start(bf16[384,512]{1,0:T(8,128)(2,1)S(1)} %copy-done.42), channel_id=1, source_target_pairs={{24,0},{26,2},{28,4},{30,6},{0,8},{2,10},{4,12},{6,14},{8,16},{10,... | collective-permute-start | bytes 1179656 | tf_op jit(solution)/shard_map/ppermute | solution.py:54
  212.0 33.6 %collective-permute-start.57 = (bf16[384,512]{1,0:T(8,128)(2,1)S(1)}, bf16[384,512]{1,0:T(8,128)(2,1)S(1)}, u32[]{:S(2)}, u32[]{:S(2)}) collective-permute-start(bf16[384,512]{1,0:T(8,128)(2,1)S(1)} %copy-done.42), channel_id=1, source_target_pairs={{4,0},{6,2},{0,4},{2,6},{12,8},{14,10},{8,12},{10,14},{20,16},{22,... | collective-permute-start | bytes 1179656 | tf_op jit(solution)/shard_map/ppermute | solution.py:54
  218.6 37.7 %collective-permute-start.61 = (bf16[384,512]{1,0:T(8,128)(2,1)S(1)}, bf16[384,512]{1,0:T(8,128)(2,1)}, u32[]{:S(2)}, u32[]{:S(2)}) collective-permute-start(bf16[384,512]{1,0:T(8,128)(2,1)S(1)} %copy-done.42), channel_id=1, source_target_pairs={{2,0},{0,2},{6,4},{4,6},{10,8},{8,10},{14,12},{12,14},{18,16},{16,... | collective-permute-start | bytes 1179656 | tf_op jit(solution)/shard_map/ppermute | solution.py:54
  272.4 57.4 %collective-permute-start.43 = (bf16[256,3712]{1,0:T(8,128)(2,1)}, bf16[256,3712]{1,0:T(8,128)(2,1)S(1)}, u32[]{:S(2)}, u32[]{:S(2)}) collective-permute-start(bf16[256,3712]{1,0:T(8,128)(2,1)} %get-tuple-element.24), channel_id=1, source_target_pairs={{2,0},{0,2},{6,4},{4,6},{10,8},{8,10},{14,12},{12,14},{18,16},{16,... | collective-permute-start | bytes 5701640 | tf_op jit(solution)/shard_map/ppermute | solution.py:54
  272.7 57.2 %collective-permute-start.45 = (bf16[256,3712]{1,0:T(8,128)(2,1)}, bf16[256,3712]{1,0:T(8,128)(2,1)}, u32[]{:S(2)}, u32[]{:S(2)}) collective-permute-start(bf16[256,3712]{1,0:T(8,128)(2,1)} %add_convert_fusion.1), channel_id=1, source_target_pairs={{1,0},{0,1},{3,2},{2,3},{5,4},{4,5},{7,6},{6,7},{9,8},{8,9},{11,10... | collective-permute-start | bytes 5701640 | tf_op jit(solution)/shard_map/ppermute | solution.py:58
  299.4 26.2 %collective-permute-start.60 = (bf16[384,512]{1,0:T(8,128)(2,1)}, bf16[384,512]{1,0:T(8,128)(2,1)}, u32[]{:S(2)}, u32[]{:S(2)}) collective-permute-start(bf16[384,512]{1,0:T(8,128)(2,1)} %collective-permute-done.56.refs_5_), channel_id=1, source_target_pairs={{4,0},{6,2},{0,4},{2,6},{12,8},{14,10},{8,12},{10,14},{20,16},{22,... | collective-permute-start | bytes 1179656 | tf_op jit(solution)/shard_map/ppermute | solution.py:54
  335.7 46.3 %collective-permute-start.67 = (bf16[384,512]{1,0:T(8,128)(2,1)}, bf16[384,512]{1,0:T(8,128)(2,1)}, u32[]{:S(2)}, u32[]{:S(2)}) collective-permute-start(bf16[384,512]{1,0:T(8,128)(2,1)} %collective-permute-done.59.refs_8_), channel_id=1, source_target_pairs={{2,0},{0,2},{6,4},{4,6},{10,8},{8,10},{14,12},{12,14},{18,16},{16,... | collective-permute-start | bytes 1179656 | tf_op jit(solution)/shard_map/ppermute | solution.py:54
  335.8 46.2 %collective-permute-start.68 = (bf16[384,512]{1,0:T(8,128)(2,1)}, bf16[384,512]{1,0:T(8,128)(2,1)}, u32[]{:S(2)}, u32[]{:S(2)}) collective-permute-start(bf16[384,512]{1,0:T(8,128)(2,1)} %collective-permute-done.60.refs_9_), channel_id=1, source_target_pairs={{2,0},{0,2},{6,4},{4,6},{10,8},{8,10},{14,12},{12,14},{18,16},{16,... | collective-permute-start | bytes 1179656 | tf_op jit(solution)/shard_map/ppermute | solution.py:54
  337.2 55.9 %collective-permute-start.50 = (bf16[2,32,1920]{2,1,0:T(8,128)(2,1)}, bf16[2,32,1920]{2,1,0:T(8,128)(2,1)S(1)}, u32[]{:S(2)}, u32[]{:S(2)}) collective-permute-start(bf16[2,32,1920]{2,1,0:T(8,128)(2,1)} %get-tuple-element.44), channel_id=1, source_target_pairs={{24,0},{26,2},{28,4},{30,6},{0,8},{2,10},{4,12},{6,14},{8,16},{10,... | collective-permute-start | bytes 737288 | tf_op jit(solution)/shard_map/ppermute | solution.py:54
  337.2 55.9 %collective-permute-start.51 = (bf16[2,32,1920]{2,1,0:T(8,128)(2,1)}, bf16[2,32,1920]{2,1,0:T(8,128)(2,1)}, u32[]{:S(2)}, u32[]{:S(2)}) collective-permute-start(bf16[2,32,1920]{2,1,0:T(8,128)(2,1)} %get-tuple-element.45), channel_id=1, source_target_pairs={{8,0},{10,2},{12,4},{14,6},{16,8},{18,10},{20,12},{22,14},{24,16},... | collective-permute-start | bytes 737288 | tf_op jit(solution)/shard_map/ppermute | solution.py:54
  339.2 53.9 %collective-permute-start.52 = (bf16[2,32,1920]{2,1,0:T(8,128)(2,1)}, bf16[2,32,1920]{2,1,0:T(8,128)(2,1)}, u32[]{:S(2)}, u32[]{:S(2)}) collective-permute-start(bf16[2,32,1920]{2,1,0:T(8,128)(2,1)} %get-tuple-element.46), channel_id=1, source_target_pairs={{16,0},{18,2},{20,4},{22,6},{24,8},{26,10},{28,12},{30,14},{0,16},... | collective-permute-start | bytes 737288 | tf_op jit(solution)/shard_map/ppermute | solution.py:54
  (154 other events, 2656.9 us)
